TPU v7x, 32 devices: a whole 2x2x4 slice. The times are simulated.
32 devices in a mesh: replica: 4 (over y, x), group: 8 (over z, core).
Axes of the slice: x: 2, y: 2, z: 4, core: 2. Of those that a mesh axis runs over, the one named last changes fastest.
Arguments:
- tokens: float32 [16384, 384], P(('replica', 'group')), may hold values from -6 to 6
- image_count: int32 [4], replicated, may hold values from 10 to 20, as said below
- w_qkv: float32 [384, 1152], P(None, 'group'), may hold values from -0.3125 to 0.3125
- w_out: float32 [384, 384], P(None, 'group'), may hold values from -1.75 to 1.75
- w_up: float32 [384, 1536], P(None, 'group'), may hold values from -0.3125 to 0.3125
- w_down: float32 [1536, 384], P('group'), may hold values from -0.15625 to 0.15625
- vectors: float32 [12, 384], P(None, 'group'), may hold values from -2 to 2
- cotangent: float32 [16384, 384], P(('replica', 'group')), may hold values from -6 to 6
- mom_qkv: float32 [384, 1152], P(None, 'group'), may hold values from -384 to 384
- mom_out: float32 [384, 384], P(None, 'group'), may hold values from -384 to 384
- mom_up: float32 [384, 1536], P(None, 'group'), may hold values from -384 to 384
- mom_down: float32 [1536, 384], P('group'), may hold values from -384 to 384
- mom_vectors: float32 [12, 384], P(None, 'group'), may hold values from -384 to 384
Outputs:
- block_out: float32 [16384, 384], P(('replica', 'group'))
- grad_tokens: float32 [16384, 384], P(('replica', 'group'))
- grad_qkv: float32 [384, 1152], P(None, 'group')
- grad_out: float32 [384, 384], P(None, 'group')
- grad_up: float32 [384, 1536], P(None, 'group')
- grad_down: float32 [1536, 384], P('group')
- grad_vectors: float32 [12, 384], P(None, 'group')
- new_mom_qkv: float32 [384, 1152], P(None, 'group')
- new_mom_out: float32 [384, 384], P(None, 'group')
- new_mom_up: float32 [384, 1536], P(None, 'group')
- new_mom_down: float32 [1536, 384], P('group')
- new_mom_vectors: float32 [12, 384], P(None, 'group')
- update_qkv: float32 [384, 1152], P(None, 'group')
- update_out: float32 [384, 384], P(None, 'group')
- update_up: float32 [384, 1536], P(None, 'group')
- update_down: float32 [1536, 384], P('group')
- update_vectors: float32 [12, 384], P(None, 'group')
Inputs may be any that keep to these rules, and one draw needn't show every extreme that they name: Replica r holds images 0 to image_count[r] - 1 in its first 197 * image_count[r] slots; one replica holds 20 images and one holds 10.
All inputs are finite; a program needn't handle non-finite values.
Results may differ from a plain program's by a relative error of at most 0.0003.
Values sent between devices are 32-bit elements; how exact they have to be, the bound alone decides.
No kernel may reach another device: no remote copies, remote signals or barrier semaphores. Data moves between devices by JAX's collectives and lax.ppermute only.
A program may use at most 128 MiB of HBM per device.

v0:
```python
import functools

import jax
import jax.numpy as jnp
from jax import lax
from jax.experimental import pallas as pl
from jax.experimental.pallas import tpu as pltpu
from jax.sharding import PartitionSpec as P

D = 384
HEADS = 6
HEAD_DIM = 64
FF = 1536
L = 197
NS_STEPS = 5
SLOTS = 4
SLOT = 208
HALO = 200
TILE = 512

f32, bf16 = jnp.float32, jnp.bfloat16
high = lax.Precision.HIGH
precise = lax.Precision.HIGHEST
ns_coeffs = (3.4445, -4.775, 2.0315)
norm_eps = 1e-06
ns_eps = 1e-07
muon_momentum = 0.95
vector_momentum = 0.9
muon_rate = 0.5
vector_rate = 0.001
mask_fill = -1e30

UPPER = ((0, 0), (0, 1), (0, 2), (1, 1), (1, 2), (2, 2))
NN = (((1,), (0,)), ((), ()))
NT = (((1,), (1,)), ((), ()))
TN = (((0,), (0,)), ((), ()))
VMEM = pl.BlockSpec(memory_space=pltpu.VMEM)
SMEM = pl.BlockSpec(memory_space=pltpu.SMEM)


def call(body, outs, scratch=(), flops=0, data=0):
    def run(scalars, *arrays):
        return pl.pallas_call(
            body,
            out_shape=[jax.ShapeDtypeStruct(s, t) for s, t in outs],
            in_specs=[SMEM] + [VMEM] * len(arrays),
            out_specs=[VMEM] * len(outs),
            scratch_shapes=[pltpu.VMEM(s, t) for s, t in scratch],
            compiler_params=pltpu.CompilerParams(vmem_limit_bytes=28 << 20),
            cost_estimate=pl.CostEstimate(flops=flops, bytes_accessed=data, transcendentals=0),
        )(scalars, *arrays)

    return run


def mm(a, b, dims):
    return lax.dot_general(a, b, dims, preferred_element_type=f32)


def fdot(a, b, dims, precision=high):
    return lax.dot_general(a, b, dims, precision=precision, preferred_element_type=f32)


def halves(x):
    hi = x.astype(bf16)
    return hi, (x - hi.astype(f32)).astype(bf16)


def triple(x):
    hi, lo = halves(x)
    return jnp.concatenate([hi, hi, lo], axis=1)


def by_rows(hi, lo, both):
    wide = mm(hi, both[:, : 2 * D], NN)
    return wide[:, :D] + wide[:, D:] + mm(lo, both[:, :D], NN)


def by_tokens(hi, lo, other):
    wide = mm(hi, other[:, D:], TN)
    return wide[:, :D] + wide[:, D:] + mm(lo, other[:, :D], TN)


def standardized(x):
    centered = x - jnp.mean(x, axis=-1, keepdims=True)
    rstd = lax.rsqrt(jnp.mean(centered * centered, axis=-1, keepdims=True) + norm_eps)
    return centered * rstd, rstd


def norm_back(d_norm, xhat, rstd, scale):
    g = d_norm * (1.0 + scale)
    return rstd * (
        g - jnp.mean(g, axis=-1, keepdims=True) - xhat * jnp.mean(g * xhat, axis=-1, keepdims=True)
    )


def row_sum(x):
    return jnp.sum(x, axis=0, keepdims=True)


def window_start(scalars, slot):
    start = HALO - scalars[0] + L * slot
    aligned = pl.multiple_of((start // 8) * 8, 8)
    return aligned, start - aligned


def fill_window(window, lower, own, upper):
    rows = own.shape[0]
    window[:HALO, :] = lower[...]
    window[HALO : HALO + rows, :] = own[...]
    window[HALO + rows : 2 * HALO + rows, :] = upper[...]
    window[2 * HALO + rows :, :] = jnp.zeros((window.shape[0] - 2 * HALO - rows, D), f32)


def load_slot(window, scalars, slot):
    aligned, shift = window_start(scalars, slot)
    block = window[pl.ds(aligned, SLOT + 8), :]
    return pltpu.roll(block, lax.rem(SLOT + 8 - shift, SLOT + 8), 0)[:SLOT]


def store_slot(window, scalars, slot, value):
    aligned, shift = window_start(scalars, slot)
    block = jnp.concatenate([value, jnp.zeros((8, value.shape[1]), f32)], axis=0)
    block = pltpu.roll(block, shift, 0)
    rows = lax.broadcasted_iota(jnp.int32, (SLOT + 8, 1), 0)
    window[pl.ds(aligned, SLOT + 8), :] = jnp.where(
        rows >= shift, block, window[pl.ds(aligned, SLOT + 8), :]
    )


def window_rows(rows):
    return 2 * HALO + rows + 96


def pairs(x):
    hi, lo = halves(x)
    return [
        jnp.concatenate([hi[:, at : at + HEAD_DIM], lo[:, at : at + HEAD_DIM]], axis=1)
        for at in range(0, D, HEAD_DIM)
    ]


def twice(x):
    return jnp.concatenate([x, x], axis=1)


def spread(x):
    hi, lo = x[:, :HEAD_DIM], x[:, HEAD_DIM:]
    return jnp.concatenate([hi, hi, lo, lo], axis=1)


def times(hi, lo, other):
    wide = mm(hi, other, NN)
    return wide[:, :HEAD_DIM] + wide[:, HEAD_DIM:] + mm(lo, other[:, :HEAD_DIM], NN)


def times_down(other, hi, lo):
    tall = mm(other, hi, NN)
    return tall[:HEAD_DIM] + tall[HEAD_DIM:] + mm(other[:HEAD_DIM], lo, NN)


def attend_kernel(
    scalars, lower, own, upper, w, vec, q2, kt2, v2, probs_hi, probs_lo, a3, middle, window, proj, att_win
):
    rows = own.shape[0]
    fill_window(window, lower, own, upper)
    step = (2 * HALO + rows) // 3

    def project_step(t, carry):
        at = pl.multiple_of(t * step, 16)
        xhat, _ = standardized(window[pl.ds(at, step), :])
        left = triple(xhat * (1.0 + vec[0:1, :]) + vec[1:2, :])
        for part, bias in ((0, vec[2:3, :]), (1, None), (2, vec[3:4, :])):
            value = mm(left, w[part * D : (part + 1) * D, :], NT)
            proj[pl.ds(at, step), part * D : (part + 1) * D] = value if bias is None else value + bias
        return carry

    lax.fori_loop(0, 3, project_step, 0)
    proj[2 * HALO + rows :, :] = jnp.zeros((96, 3 * D), f32)

    def slot_step(slot, carry):
        qkv = load_slot(proj, scalars, slot)
        keys = jnp.minimum(L, scalars[1] - L * slot)
        keep = lax.broadcasted_iota(jnp.int32, (SLOT, SLOT), 0) < keys
        q, k, v = (pairs(qkv[:, part * D : (part + 1) * D]) for part in range(3))
        heads = []
        for h in range(HEADS):
            q2[slot, h] = q[h]
            v2[slot, h] = v[h]
            kt2[slot, h] = jnp.transpose(k[h])
            scores = mm(twice(k[h]), spread(q[h]), NT) * HEAD_DIM**-0.5
            scores = jnp.where(keep, scores, mask_fill)
            weights = jnp.exp(scores - jnp.max(scores, axis=0, keepdims=True))
            weights = weights * (1.0 / jnp.sum(weights, axis=0, keepdims=True))
            hi, lo = halves(weights)
            probs_hi[slot, h] = hi
            probs_lo[slot, h] = lo
            heads.append(times_down(jnp.transpose(v[h]), hi, lo))
        store_slot(att_win, scalars, slot, jnp.transpose(jnp.concatenate(heads, axis=0)))
        return carry

    lax.fori_loop(0, SLOTS, slot_step, 0)
    att = triple(att_win[HALO : HALO + rows, :])
    a3[...] = att
    middle[...] = own[...] + mm(att, w[3 * D :, :], NT) + vec[4:5, :]


def attend(scalars, lower, own, upper, w, vec):
    rows = own.shape[0]
    return call(
        attend_kernel,
        [
            ((SLOTS, HEADS, SLOT, 128), bf16),
            ((SLOTS, HEADS, 128, SLOT), bf16),
            ((SLOTS, HEADS, SLOT, 128), bf16),
            ((SLOTS, HEADS, SLOT, SLOT), bf16),
            ((SLOTS, HEADS, SLOT, SLOT), bf16),
            ((rows, 3 * D), bf16),
            ((rows, D), f32),
        ],
        [
            ((window_rows(rows), D), f32),
            ((window_rows(rows), 3 * D), f32),
            ((window_rows(rows), D), f32),
        ],
        flops=10**8,
        data=1 << 18,
    )(scalars, lower, own, upper, w, vec)


def mlp_kernel(scalars, mid, cot, w, vec, bias, out, slope, n3, m3, *rest):
    parts, (total, h_hi, h_lo) = rest[:-3], rest[-3:]
    if len(parts) == 1:
        total = parts[0]
    rows = mid.shape[0]
    xhat, _ = standardized(mid[...])
    n3[...] = triple(xhat * (1.0 + vec[5:6, :]) + vec[6:7, :])
    live = lax.broadcasted_iota(jnp.int32, (rows, 1), 0) < scalars[2]
    m3[...] = triple(jnp.where(live, cot[...], 0.0))

    def tile_step(t, carry):
        at = pl.multiple_of(t * TILE, TILE)
        pre = mm(n3[...], w[pl.ds(at, TILE), :], NT) + bias[0:1, pl.ds(at, TILE)]
        cdf = 0.5 + 0.5 * lax.erf(pre * (0.5**0.5))
        slope[:, pl.ds(at, TILE)] = cdf + pre * (jnp.exp(-0.5 * pre * pre) * 0.3989422804014327)
        hi, lo = halves(pre * cdf)
        h_hi[:, pl.ds(at, TILE)] = hi
        h_lo[:, pl.ds(at, TILE)] = lo
        total[pl.ds(at, TILE), :] = by_tokens(hi, lo, m3)
        return carry

    lax.fori_loop(0, FF // TILE, tile_step, 0)
    out[...] = mid[...] + by_rows(h_hi[...], h_lo[...], w[FF:, :]) + vec[7:8, :]
    scatter_parts(scalars, total, parts, quarter_rows)


def mlp(scalars, parts, mid, cot, w, vec, bias):
    rows = mid.shape[0]
    outs, scratch = part_outs(parts, FF)
    return call(
        mlp_kernel,
        [((rows, D), f32), ((rows, FF), f32)] + [((rows, 3 * D), bf16)] * 2 + outs,
        [scratch] + [((rows, FF), bf16)] * 2,
        flops=10**8,
        data=1 << 18,
    )(scalars, mid, cot, w, vec, bias)


def mlp_back_kernel(scalars, mid, cot, w, vec, slope, m3, dmid, d_hi, d_lo, dvec, dbias):
    rows = mid.shape[0]

    def tile_step(t, carry):
        at = pl.multiple_of(t * TILE, TILE)
        d_pre = mm(m3[...], w[pl.ds(FF + at, TILE), :], NT) * slope[:, pl.ds(at, TILE)]
        dbias[0:1, pl.ds(at, TILE)] = row_sum(d_pre)
        hi, lo = halves(d_pre)
        d_hi[:, pl.ds(at, TILE)] = hi
        d_lo[:, pl.ds(at, TILE)] = lo
        return carry

    lax.fori_loop(0, FF // TILE, tile_step, 0)
    d_norm = by_rows(d_hi[...], d_lo[...], w[:FF, :])
    xhat, rstd = standardized(mid[...])
    live = lax.broadcasted_iota(jnp.int32, (rows, 1), 0) < scalars[2]
    masked = jnp.where(live, cot[...], 0.0)
    d_middle = masked + norm_back(d_norm, xhat, rstd, vec[5:6, :])
    dmid[...] = d_middle
    zero = jnp.zeros((4, D), f32)
    dvec[...] = jnp.concatenate(
        [zero, row_sum(d_middle), row_sum(d_norm * xhat), row_sum(d_norm), row_sum(masked)]
        + [dbias[0:1, i * D : (i + 1) * D] for i in range(4)]
        + [zero],
        axis=0,
    )


def mlp_back(scalars, mid, cot, w, vec, slope, m3):
    rows = mid.shape[0]
    return call(
        mlp_back_kernel,
        [((rows, D), f32)] + [((rows, FF), bf16)] * 2 + [((16, D), f32)],
        [((8, FF), f32)],
        flops=10**8,
        data=1 << 18,
    )(scalars, mid, cot, w, vec, slope, m3)


def place(scalars, chips, i, j, k):
    owner = 2 * lax.rem(scalars[4] + k, chips) + lax.bitwise_xor(scalars[5], i)
    return owner, lax.bitwise_xor(scalars[3], j)


def first_rows(owner, quarter, piece):
    return pl.multiple_of(
        jnp.where(quarter < 3, owner * 3 * piece + quarter * piece, 3 * D + owner * piece), piece
    )


def second_rows(owner, quarter, piece):
    half = piece // 2
    at = owner * 4 * half + quarter * half
    return pl.multiple_of(at, half), pl.multiple_of(FF + at, half)


def quarter_rows(owner, quarter, piece):
    return pl.multiple_of(owner * 4 * piece + quarter * piece, piece)


def part_outs(parts, rows):
    if parts is None:
        return [((rows, D), f32)], ((8, D), f32)
    return [(parts, f32)] * 4 + [((4, *parts), f32)], ((rows, D), f32)


def scatter_parts(scalars, total, outs, rows_of):
    if len(outs) == 1:
        return
    chips, piece, _ = outs[0].shape
    for n in range(8):
        for k in range(chips):
            owner, quarter = place(scalars, chips, n // 4, n % 4, k)
            rows = total[pl.ds(rows_of(owner, quarter, piece), piece), :]
            if n < 4:
                outs[n][k] = rows
            else:
                outs[4][n - 4, k] = rows


def up_grads_kernel(scalars, d_hi, d_lo, n3, *rest):
    outs, total = rest[:-1], rest[-1]
    if len(outs) == 1:
        total = outs[0]

    def tile_step(t, carry):
        at = pl.multiple_of(t * TILE, TILE)
        total[pl.ds(at, TILE), :] = by_tokens(d_hi[:, pl.ds(at, TILE)], d_lo[:, pl.ds(at, TILE)], n3)
        return carry

    lax.fori_loop(0, FF // TILE, tile_step, 0)
    scatter_parts(scalars, total, outs, quarter_rows)


def up_grads(scalars, parts, *arrays):
    outs, scratch = part_outs(parts, FF)
    return call(up_grads_kernel, outs, [scratch], flops=10**8, data=1 << 18)(scalars, *arrays)


def attend_back_kernel(first_slot, scalars, lower, own, upper, w, q2, kt2, v2, probs_hi, probs_lo, out, window):
    rows = own.shape[0]
    fill_window(window, lower, own, upper)

    def slot_step(step, carry):
        slot = first_slot + step
        row = lax.broadcasted_iota(jnp.int32, (SLOT, 1), 0)
        at_own = row + L * slot - scalars[0]
        mine = (at_own >= 0) & (at_own < rows) & (row < L)
        d_mid = jnp.where(row < L, load_slot(window, scalars, slot), 0.0)
        d_out = pairs(by_rows(*halves(d_mid), w[3 * D :, :]))
        d_q, d_k, d_v = [], [], []
        for h in range(HEADS):
            hi, lo = probs_hi[slot, h], probs_lo[slot, h]
            weights = hi.astype(f32) + lo.astype(f32)
            d_weights = mm(twice(v2[slot, h]), spread(d_out[h]), NT)
            mean = jnp.sum(weights * d_weights, axis=0, keepdims=True)
            s_hi, s_lo = halves(weights * (d_weights - mean) * HEAD_DIM**-0.5)
            d_v.append(times(hi, lo, d_out[h]))
            d_k.append(times(s_hi, s_lo, q2[slot, h]))
            d_q.append(times_down(kt2[slot, h], s_hi, s_lo))
        d_q = jnp.transpose(jnp.concatenate(d_q, axis=0))
        d_proj = jnp.concatenate([d_q] + d_k + d_v, axis=1)
        out[step] = jnp.where(mine, d_proj, 0.0)
        return carry

    lax.fori_loop(0, out.shape[0], slot_step, 0)


def attend_back(scalars, first_slot, slots, around, w, *saved):
    rows = around[1].shape[0]
    return call(
        functools.partial(attend_back_kernel, first_slot),
        [((slots, SLOT, 3 * D), f32)],
        [((window_rows(rows), D), f32)],
        flops=10**8,
        data=1 << 18,
    )(scalars, *around, w, *saved)[0]


def attend_grads_kernel(scalars, some, more, tokens, d_mid, vec, a3, *rest):
    outs, (d_hi, d_lo, sums), (total, window) = rest[:-5], rest[-5:-2], rest[-2:]
    if len(outs) == 1:
        total = outs[0]
    rows = tokens.shape[0]
    for i, part in enumerate((some, more)):

        def slot_step(step, carry, i=i, part=part):
            store_slot(window, scalars, i * part.shape[0] + step, part[step])
            return carry

        lax.fori_loop(0, part.shape[0], slot_step, 0)
    xhat, _ = standardized(tokens[...])
    n3 = triple(xhat * (1.0 + vec[0:1, :]) + vec[1:2, :])

    def part_step(part, carry):
        at = pl.ds(pl.multiple_of(part * D, D), D)
        d_proj = window[HALO : HALO + rows, at]
        hi, lo = halves(d_proj)
        d_hi[:, at] = hi
        d_lo[:, at] = lo
        total[at, :] = by_tokens(hi, lo, n3)
        sums[part] = jnp.broadcast_to(row_sum(d_proj), (8, D))
        return carry

    lax.fori_loop(0, 3, part_step, 0)
    total[3 * D :, :] = by_tokens(*halves(d_mid[...]), a3)
    scatter_parts(scalars, total, outs, first_rows)


def attend_grads(scalars, parts, some, more, tokens, d_mid, vec, a3):
    rows = tokens.shape[0]
    outs, scratch = part_outs(parts, 4 * D)
    return call(
        attend_grads_kernel,
        outs + [((rows, 3 * D), bf16)] * 2 + [((3, 8, D), f32)],
        [scratch, ((window_rows(rows), 3 * D), f32)],
        flops=10**8,
        data=1 << 18,
    )(scalars, some, more, tokens, d_mid, vec, a3)


def token_grads_kernel(scalars, d_hi, d_lo, w, tokens, d_mid, vec, sums, dvec_in, dtok, dvec):
    xhat, rstd = standardized(tokens[...])
    d_norm = by_rows(d_hi[...], d_lo[...], w[: 3 * D, :])
    dtok[...] = d_mid[...] + norm_back(d_norm, xhat, rstd, vec[0:1, :])
    new = [row_sum(d_norm * xhat), row_sum(d_norm), sums[0, 0:1], sums[2, 0:1], jnp.zeros((12, D), f32)]
    dvec[...] = dvec_in[...] + jnp.concatenate(new, axis=0)


def token_grads(scalars, *arrays):
    rows = arrays[0].shape[0]
    return call(
        token_grads_kernel, [((rows, D), f32), ((16, D), f32)], flops=10**8, data=1 << 18
    )(scalars, *arrays)


def store_split(w, at, x):
    hi, lo = halves(x)
    w[pl.ds(at, x.shape[0]), :] = jnp.concatenate([hi, lo, hi], axis=1)


def unpack_kernel(rows_of, chips, piece, step, scalars, *refs):
    mine, other, rest = refs[:4], refs[4:8], refs[8:]
    if step:
        vectors, (w, vec, bias, flat) = rest[:2], rest[2:]
    else:
        (w,) = rest
    for i, parts in enumerate((mine, other)):
        for j in range(4):
            for k in range(chips):
                owner, quarter = place(scalars, chips, i, j, chips - k)
                at = rows_of(owner, quarter, piece)
                at = at if isinstance(at, tuple) else (at,)
                share = piece // len(at)
                for n, to in enumerate(at):
                    base = k * piece + n * share
                    store_split(w, to, parts[j][base : base + share, :])
    if step:
        for i, parts in enumerate(vectors):
            for k in range(chips):
                owner, _ = place(scalars, chips, i, 0, chips - k)
                for s in range(3):
                    flat[pl.ds(pl.multiple_of((owner * 3 + s) * step, step), step), :] = parts[
                        k * step : (k + 1) * step, s * 128 : (s + 1) * 128
                    ]
        rows = jnp.transpose(flat[...])[:16, :]
        vec[...] = rows
        bias[...] = jnp.concatenate([rows[8 + s : 9 + s, :] for s in range(4)], axis=1)


def unpack(scalars, chips, mine, other, rows_of, *vectors):
    total = 8 * mine[0].shape[0]
    outs = [((total, 3 * D), bf16)]
    if vectors:
        outs += [((16, D), f32), ((1, FF), f32)]
    return call(
        functools.partial(
            unpack_kernel,
            rows_of,
            chips,
            mine[0].shape[0] // chips,
            vectors[0].shape[0] // chips if vectors else 0,
        ),
        outs,
        [((D, 128), f32)] if vectors else [],
        flops=10**8,
        data=1 << 18,
    )(scalars, *mine, *other, *vectors)


def own_gradients_kernel(scalars, *refs):
    parts, (mom, grads, new_mom, own, *gram) = refs[:4], refs[4:]
    piece = own.shape[0] // 4
    for j in range(4):
        quarter = lax.bitwise_xor(scalars[3], j)
        grads[pl.ds(pl.multiple_of(quarter * piece, piece), piece), :] = parts[j][:piece, :]
        for n in (1, 2):
            grads[pl.ds(pl.multiple_of((4 * n + quarter) * piece, piece), piece), :] = parts[j][
                n * piece : (n + 1) * piece, :
            ]
    new_mom[...] = muon_momentum * mom[...] + grads[...]
    replica = scalars[3]
    start = jnp.where(replica == 0, 4, jnp.where(replica == 1, 0, jnp.where(replica == 2, 8, 3)))
    count = jnp.where(replica == 1, 3, jnp.where(replica == 3, 1, 4)) * piece
    row = lax.broadcasted_iota(jnp.int32, (4 * piece, 1), 0)
    block = jnp.where(
        row < count, new_mom[pl.ds(pl.multiple_of(start * piece, piece), 4 * piece), :], 0.0
    )
    own[...] = block
    keep, send, total = gram
    gram = fdot(block, block, TN, precise)
    for n, (row, column) in enumerate(UPPER):
        total[n * 128 : (n + 1) * 128, :] = gram[
            row * 128 : (row + 1) * 128, column * 128 : (column + 1) * 128
        ]
    chips, share, _ = keep.shape
    for i, out in enumerate((keep, send)):
        for k in range(chips):
            at = lax.bitwise_xor(scalars[5], i) * chips + lax.rem(scalars[4] + k, chips)
            out[k] = total[pl.ds(pl.multiple_of(at * share, share), share), :]


def own_gradients(scalars, parts, mom, chips):
    rows = mom.shape[0]
    share = 128 * len(UPPER) // (2 * chips)
    return call(
        own_gradients_kernel,
        [((rows, D), f32)] * 2 + [((rows // 3, D), f32)] + [((chips, share, 128), f32)] * 2,
        [((128 * len(UPPER), 128), f32)],
        flops=10**8,
        data=1 << 18,
    )(scalars, *parts, mom)


def pieces(x):
    hi, mid = halves(x)
    return hi, mid, (x - hi.astype(f32) - mid.astype(f32)).astype(bf16)


def full_product(a, b):
    (ah, am, al), (bh, bm, bl) = a, b
    return mm(
        jnp.concatenate([ah, ah, am, ah, al, am], axis=1),
        jnp.concatenate([bh, bm, bh, bl, bh, bm], axis=0),
        NN,
    )


def three_product(a, b):
    (ah, am, _), (bh, bm, _) = a, b
    return mm(
        jnp.concatenate([ah, am, ah], axis=1), jnp.concatenate([bh, bh, bm], axis=0), NN
    )


def identity():
    row = lax.broadcasted_iota(jnp.int32, (D, D), 0)
    return jnp.where(row == lax.broadcasted_iota(jnp.int32, (D, D), 1), 1.0, 0.0)


def polynomial(gram, product):
    g = pieces(gram)
    return g, ns_coeffs[1] * gram + ns_coeffs[2] * product(g, g) + ns_coeffs[0] * identity()


def polar_step(gram, block):
    g, poly = polynomial(gram, full_product)
    p = pieces(poly)
    return full_product(p, pieces(full_product(p, g))), three_product(pieces(block), p)


def polar_end(gram, block):
    return three_product(pieces(block), pieces(polynomial(gram, three_product)[1]))


def polar_start(gram, block):
    scale = 1.0 / (jnp.sqrt(jnp.sum(gram * identity())) + ns_eps)
    return gram * (scale * scale), block * scale


def polar(gram, block):
    state = polar_start(gram, block)
    for _ in range(NS_STEPS - 1):
        state = polar_step(*state)
    return polar_end(*state)


def update_kernel(scalars, mine, other, own, out, total, gram, block):
    chips, share, _ = mine.shape
    for i, parts in enumerate((mine, other)):
        for k in range(chips):
            at = lax.bitwise_xor(scalars[5], i) * chips + lax.rem(scalars[4] + chips - k, chips)
            total[pl.ds(pl.multiple_of(at * share, share), share), :] = parts[k]
    blocks = {}
    for n, (row, column) in enumerate(UPPER):
        blocks[row, column] = total[n * 128 : (n + 1) * 128, :]
        if row != column:
            blocks[column, row] = jnp.transpose(blocks[row, column])
    gram[...], block[...] = polar_start(
        jnp.concatenate(
            [jnp.concatenate([blocks[row, column] for column in range(3)], axis=1) for row in range(3)],
            axis=0,
        ),
        own[...],
    )

    def step(_, carry):
        gram[...], block[...] = polar_step(gram[...], block[...])
        return carry

    lax.fori_loop(0, NS_STEPS - 1, step, 0)
    replica = scalars[3]
    rate = jnp.where(replica == 1, 3.0**0.5, jnp.where(replica == 0, (FF / D) ** 0.5, 1.0))
    out[...] = polar_end(gram[...], block[...]) * (-muon_rate * rate)


def update(scalars, mine, other, own):
    return call(
        update_kernel,
        [(own.shape, f32)],
        [((128 * len(UPPER), 128), f32), ((D, D), f32), (own.shape, f32)],
        flops=10**8, data=1 << 18
    )(scalars, mine, other, own)[0]


def local(
    tokens,
    image_count,
    w_qkv,
    w_out,
    w_up,
    w_down,
    vectors,
    cotangent,
    mom_qkv,
    mom_out,
    mom_up,
    mom_down,
    mom_vectors,
):
    group_size = lax.axis_size("group")
    replicas = lax.axis_size("replica")
    group_index = lax.axis_index("group")
    replica_index = lax.axis_index("replica")
    chips = group_size // 2
    tok_rows = tokens.shape[0]
    slab_rows = group_size * tok_rows
    image_total = lax.dynamic_index_in_dim(image_count, replica_index, 0, keepdims=False)
    first_slot = group_index * tok_rows
    first_image = first_slot // L
    scalars = jnp.stack(
        [
            first_slot - first_image * L,
            slab_rows - first_image * L,
            image_total * L - first_slot,
            replica_index,
            group_index // 2,
            group_index % 2,
        ]
    ).astype(jnp.int32)

    def swap(x):
        return lax.ppermute(x, "group", [(i, i ^ 1) for i in range(group_size)])

    def rotate(x, by):
        return lax.ppermute(
            x, "group", [(i, (i + 2 * by) % group_size) for i in range(group_size)]
        )

    def cross(x, by):
        return lax.ppermute(x, "replica", [(i, i ^ by) for i in range(replicas)])

    def halo(x):
        ends = group_size - 1
        lower = lax.ppermute(x[tok_rows - HALO :], "group", [(i, i + 1) for i in range(ends)])
        upper = lax.ppermute(x[:HALO], "group", [(i + 1, i) for i in range(ends)])
        return lower, x, upper

    def along_chips(x):
        return jnp.stack([x] + [rotate(x, k) for k in range(1, chips)])

    width = D // group_size
    piece = 4 * width // replicas
    cuts = (3 * width, width, 4 * width, 4 * width)
    first_stack = jnp.concatenate([w_qkv.T, w_out.T], axis=0)
    second_stack = jnp.concatenate([w_up.T, w_down], axis=0)
    mom_stack = jnp.concatenate([mom_qkv.T, mom_out.T, mom_up.T, mom_down], axis=0)
    around = halo(tokens)

    def split(stack):
        one, two, three, four = (stack[sum(cuts[:i]) : sum(cuts[: i + 1])] for i in range(4))
        return one.T, two.T, three.T, four

    def finish(block_out, grad_tokens, grads, new_mom, dvec, updates):
        grad_vectors = lax.dynamic_slice_in_dim(dvec[:12], group_index * width, width, 1)
        new_vectors = vector_momentum * mom_vectors + grad_vectors
        return (
            block_out,
            grad_tokens,
            *split(grads),
            grad_vectors,
            *split(new_mom),
            new_vectors,
            *updates,
            -vector_rate * new_vectors,
        )

    if replicas != 4 or piece % 16:
        def rows_of(stack, inner):
            parts = lax.all_gather(stack, "group")
            rows = jnp.concatenate(
                [parts[:, :inner].reshape(-1, D), parts[:, inner:].reshape(-1, D)], axis=0
            )
            hi, lo = halves(rows)
            return jnp.concatenate([hi, lo, hi], axis=1)

        def shares_of(total, cut, inner):
            one, two = total[:cut], total[cut:]
            parts = jnp.concatenate(
                [one.reshape(group_size, inner, D), two.reshape(group_size, -1, D)], axis=1
            )
            return lax.psum_scatter(parts, "group", scatter_dimension=0)

        w_one, w_two = rows_of(first_stack, 3 * width), rows_of(second_stack, 4 * width)
        vec = jnp.pad(lax.all_gather(vectors, "group", axis=1, tiled=True), ((0, 4), (0, 0)))
        *saved, a3, middle = attend(scalars, *around, w_one, vec)
        block_out, slope, n3, m3, down = mlp(
            scalars, None, middle, cotangent, w_two, vec, vec[8:12].reshape(1, FF)
        )
        d_middle, d_hi, d_lo, dvec = mlp_back(scalars, middle, cotangent, w_two, vec, slope, m3)
        second = jnp.concatenate([up_grads(scalars, None, d_hi, d_lo, n3)[0], down], axis=0)
        d_around = halo(d_middle)
        some, more = (attend_back(scalars, i, 2, d_around, w_one, *saved) for i in (0, 2))
        first, d_hi, d_lo, sums = attend_grads(
            scalars, None, some, more, tokens, d_middle, vec, a3
        )
        grad_tokens, dvec = token_grads(
            scalars, d_hi, d_lo, w_one, tokens, d_middle, vec, sums, dvec
        )
        grads, dvec = lax.psum(
            (
                jnp.concatenate(
                    [shares_of(first, 3 * D, 3 * width), shares_of(second, FF, 4 * width)], axis=0
                ),
                lax.psum(dvec, "group"),
            ),
            "replica",
        )
        new_mom = muon_momentum * mom_stack + grads
        blocks = [new_mom[sum(cuts[:i]) : sum(cuts[: i + 1])] for i in range(4)]
        grams = lax.psum(jnp.stack([fdot(x, x, TN, precise) for x in blocks]), "group")
        updates = [
            polar(grams[i], x) * (-muon_rate * rate)
            for i, (x, rate) in enumerate(zip(blocks, (3.0**0.5, 1.0, (FF / D) ** 0.5, 1.0)))
        ]
        updates = [x if i == 3 else x.T for i, x in enumerate(updates)]
        return finish(block_out, grad_tokens, grads, new_mom, dvec, updates)

    vec_block = jnp.pad(vectors.T, ((0, 0), (0, 116)))
    third = width // 3
    vec_block = jnp.concatenate([vec_block[s * third : (s + 1) * third] for s in range(3)], axis=1)
    my_first = lax.dynamic_slice_in_dim(first_stack, replica_index * piece, piece, 0)
    my_second = jnp.concatenate(
        [
            lax.dynamic_slice_in_dim(second_stack, (4 * n + replica_index) * piece, piece, 0)
            for n in range(2)
        ],
        axis=0,
    )

    others = range(1, replicas)
    start = jnp.concatenate([my_first, vec_block], axis=0)
    start = [start] + [rotate(start, k) for k in range(1, chips)]
    first = jnp.concatenate([x[:piece] for x in start], axis=0)
    vec_parts = jnp.concatenate([x[piece:] for x in start], axis=0)
    first, vec_parts, my_second, lower, upper, scalars = lax.optimization_barrier(
        (first, vec_parts, my_second, around[0], around[2], scalars)
    )
    around = lower, tokens, upper
    first_other, vec_other = [swap(first)], swap(vec_parts)
    first = [first] + [cross(first, j) for j in others]
    second = [my_second] + [rotate(my_second, k) for k in range(1, chips)]
    first[1:], second = lax.optimization_barrier((first[1:], second))
    second = jnp.concatenate(second, axis=0)
    second = [second] + [cross(second, j) for j in others]
    second_other = [swap(second[0])]
    first_other += [swap(first[j]) for j in others]
    w_one, vec, bias = unpack(
        scalars, chips, first, first_other, first_rows, vec_parts, vec_other
    )
    *saved, a3, middle = attend(scalars, *around, w_one, vec)
    for j in others:
        second[j], middle = lax.optimization_barrier((second[j], middle))
        second_other.append(swap(second[j]))
    w_two = unpack(scalars, chips, second, second_other, second_rows)[0]
    shape = (chips, piece, D)

    def join(keep, other):
        return [x + other[j] for j, x in enumerate(keep)]

    def exchange(parts):
        return [parts[0]] + [cross(parts[j], j) for j in others]

    block_out, slope, n3, m3, *keep, send = mlp(
        scalars, shape, middle, cotangent, w_two, vec, bias
    )
    other = swap(send)
    d_middle, d_hi, d_lo, dvec = mlp_back(scalars, middle, cotangent, w_two, vec, slope, m3)
    down, d_middle, d_hi = lax.optimization_barrier((join(keep, other), d_middle, d_hi))
    down = exchange(down)
    d_around = halo(d_middle)
    *keep, send = up_grads(scalars, shape, d_hi, d_lo, n3)
    keep, send, d_around = lax.optimization_barrier((keep, send, d_around))
    other = swap(send)
    some = attend_back(scalars, 0, 2, d_around, w_one, *saved)
    up, some, d_around = lax.optimization_barrier((join(keep, other), some, d_around))
    up = exchange(up)
    more = attend_back(scalars, 2, 2, d_around, w_one, *saved)
    *keep, send, d_hi, d_lo, sums = attend_grads(
        scalars, shape, some, more, tokens, d_middle, vec, a3
    )
    grad_tokens, dvec = token_grads(scalars, d_hi, d_lo, w_one, tokens, d_middle, vec, sums, dvec)
    keep, send, dvec, up, down = lax.optimization_barrier((keep, send, dvec, up, down))
    first = exchange(join(keep, swap(send)))
    dvec = dvec + swap(dvec)

    def over_chips(parts, *extra):
        parts = [
            jnp.concatenate([sum((x[k] for x in parts[1:]), parts[0][k]), *extra], axis=0)
            for k in range(chips)
        ]
        return sum((rotate(parts[k], k) for k in range(1, chips)), parts[0])

    down_sum, up_sum = over_chips(down), over_chips(up)
    first_sum = over_chips(first, dvec)
    sums = jnp.concatenate([first_sum[:piece], up_sum, down_sum, first_sum[piece:]], axis=0)
    parts = [sums] + [cross(sums, j) for j in others]
    dvec = sum((x[3 * piece :] for x in parts[1:]), parts[0][3 * piece :])
    grads, new_mom, own, keep, send = own_gradients(scalars, parts, mom_stack, chips)
    t = keep + swap(send)
    t = t[0] + sum(rotate(t[k], k) for k in range(1, chips))
    gram = along_chips(t)
    update_own = update(scalars, gram, swap(gram), own)
    updates = [update_own] + [cross(update_own, j) for j in others]

    def from_replica(owner, rows):
        at = lax.bitwise_xor(replica_index, owner)
        return lax.select_n(at, *(x[:rows] for x in updates))

    return finish(
        block_out,
        grad_tokens,
        grads,
        new_mom,
        dvec,
        (
            from_replica(1, 3 * width).T,
            from_replica(3, width).T,
            from_replica(0, 4 * width).T,
            from_replica(2, 4 * width),
        ),
    )


def solution(mesh):
    tokens, whole, columns, rows = P(("replica", "group"), None), P(), P(None, "group"), P("group", None)
    params = (columns, columns, columns, rows, columns)
    return jax.shard_map(
        local,
        mesh=mesh,
        in_specs=(tokens, whole, *params, tokens, *params),
        out_specs=(tokens, tokens, *params, *params, *params),
        check_vma=False,
    )
```

profile of v0, /device:TPU:0, one launch (start us, length us, event | category | flops | bytes accessed | tf_op | source)
XLA Modules:
  0.0 230.4 jit_solution(7152347102358929527)
XLA Ops:
  2.5 5.1 %collective-permute-start.2 = (f32[64,384]{1,0:T(8,128)S(1)}, f32[64,384]{1,0:T(8,128)S(1)}, u32[]{:S(2)}, u32[]{:S(2)}) collective-permute-start(f32[64,384]{1,0:T(8,128)S(1)} %maximum_maximum_fusion), channel_id=1, source_target_pairs={{0,6},{1,7},{2,0},{3,1},{4,2},{5,3},{6,4},{7,5},{8,14},{9,15},{10,... | collective-permute-start | bytes 294920 | tf_op jit(solution)/shard_map/ppermute | solution.py:694
  9.7 1.3 collective-permute-start.3
  13.8 2.5 %collective-permute-done.1 = f32[64,384]{1,0:T(8,128)S(1)} collective-permute-done((f32[64,384]{1,0:T(8,128)S(1)}, f32[64,384]{1,0:T(8,128)S(1)}, u32[]{:S(2)}, u32[]{:S(2)}) %collective-permute-start.1) | collective-permute-done | bytes 98336 | tf_op jit(solution)/shard_map/ppermute | solution.py:694
  17.2 4.9 %collective-permute-start.8 = (f32[96,384]{1,0:T(8,128)S(1)}, f32[96,384]{1,0:T(8,128)S(1)}, u32[]{:S(2)}, u32[]{:S(2)}) collective-permute-start(f32[96,384]{1,0:T(8,128)S(1)} %pad_maximum_fusion.8), channel_id=1, source_target_pairs={{0,2},{1,3},{2,4},{3,5},{4,6},{5,7},{6,0},{7,1},{8,10},{9,11},{10,... | collective-permute-start | bytes 442376 | tf_op jit(solution)/shard_map/ppermute | solution.py:694
  22.1 1.5 collective-permute-start.5
  23.6 1.5 collective-permute-start.6
  26.5 2.3 collective-permute-start.10
  28.7 7.1 %collective-permute-done.9 = f32[96,384]{1,0:T(8,128)S(1)} collective-permute-done((f32[96,384]{1,0:T(8,128)S(1)}, f32[96,384]{1,0:T(8,128)S(1)}, u32[]{:S(2)}, u32[]{:S(2)}) %collective-permute-start.9) | collective-permute-done | bytes 147488 | tf_op jit(solution)/shard_map/ppermute | solution.py:694
  36.4 2.4 %collective-permute-done.6.refs_2_ = f32[192,384]{1,0:T(8,128)S(1)} collective-permute-done((f32[192,384]{1,0:T(8,128)S(1)}, f32[192,384]{1,0:T(8,128)S(1)}, u32[]{:S(2)}, u32[]{:S(2)}) %collective-permute-start.6) | collective-permute-done | bytes 294944 | tf_op jit(solution)/shard_map/ppermute | solution.py:699
  41.1 1.4 collective-permute-start.11
  46.5 13.6 %shard_map.261 = (bf16[4,6,208,128]{3,2,1,0:T(8,128)(2,1)S(1)}, bf16[4,6,128,208]{3,2,1,0:T(8,128)(2,1)S(1)}, bf16[4,6,208,128]{3,2,1,0:T(8,128)(2,1)S(1)}, bf16...) custom-call(s32[6]{0:T(128)S(1)} %stack.42.scalars, ...), custom_call_target="tpu_custom_call" | custom-call | flops 100000000 | bytes 262144 | tf_op jit(solution)/shard_map/pallas_call | solution.py:43
  62.1 4.6 %collective-permute-done.12.refs_2_ = f32[384,384]{1,0:T(8,128)S(1)} collective-permute-done((f32[384,384]{1,0:T(8,128)S(1)}, f32[384,384]{1,0:T(8,128)S(1)}, u32[]{:S(2)}, u32[]{:S(2)}) %collective-permute-start.12) | collective-permute-done | bytes 589856 | tf_op jit(solution)/shard_map/ppermute | solution.py:699
  66.7 1.6 collective-permute-done.11.refs_3_
  68.9 1.5 collective-permute-done.20.refs_5_
  73.3 10.4 %shard_map.263 = (f32[512,384]{1,0:T(8,128)}, f32[512,1536]{1,0:T(8,128)S(1)}, bf16[512,1152]{1,0:T(8,128)(2,1)S(1)}, bf16[512,1152]{1,0:T(8,128)(2,1)S(1)}, f32...) custom-call(s32[6]{0:T(128)S(1)} %stack.42.scalars, ...), custom_call_target="tpu_custom_call" | custom-call | flops 100000000 | bytes 262144 | tf_op jit(solution)/shard_map/pallas_call | solution.py:43
  83.8 5.9 %shard_map.264 = (f32[512,384]{1,0:T(8,128)S(1)}, bf16[512,1536]{1,0:T(8,128)(2,1)S(1)}, bf16[512,1536]{1,0:T(8,128)(2,1)S(1)}, f32[16,384]{1,0:T(8,128)S(1)}) custom-call(s32[6]{0:T(128)S(1)} %stack.42.scalars, f32[512,384]{1,0:T(8,128)S(1)} %get-tuple-element.133.mid, f32[512,384]{1,0:T(8,128)S(1)} %copy-done.3, bf16[3072,1152]{1,0:T(8,128)(2,1)S(1)} %shard_map.262.w, ...), custom_call_target="tpu_custom_call" | custom-call | flops 100000000 | bytes 262144 | tf_op jit(solution)/shard_map/pallas_call | solution.py:43
  90.0 2.3 collective-permute-start.24
  93.6 3.5 %shard_map.265 = (f32[4,48,384]{2,1,0:T(8,128)S(1)}, f32[4,48,384]{2,1,0:T(8,128)S(1)}, f32[4,48,384]{2,1,0:T(8,128)S(1)}, f32[4,48,384]{2,1,0:T(8,128)S(1)}, f32[4,4,48,384]{3,2,1,0:T(8,128)S(1)}) custom-call(s32[6]{0:T(128)S(1)} %stack.42.scalars, bf16[512,1536]{1,0:T(8,128)(2,1)S(1)} %get-tuple-element.148.d_hi, ...), custom_call_target="tpu_custom_call" | custom-call | flops 100000000 | bytes 262144 | tf_op jit(solution)/shard_map/pallas_call | solution.py:43
  97.2 4.2 %collective-permute-start.26 = (f32[4,4,48,384]{3,2,1,0:T(8,128)S(1)}, f32[4,4,48,384]{3,2,1,0:T(8,128)S(1)}, u32[]{:S(2)}, u32[]{:S(2)}) collective-permute-start(f32[4,4,48,384]{3,2,1,0:T(8,128)S(1)} %get-tuple-element.158), channel_id=1, source_target_pairs={{0,1},{1,0},{2,3},{3,2},{4,5},{5,4},{6,7},{7,6},{8,9},{9,8},{10,11... | collective-permute-start | bytes 3538952 | tf_op jit(solution)/shard_map/ppermute | solution.py:691
  102.2 1.5 collective-permute-start.31
  104.9 5.6 %shard_map.266.some = f32[2,208,1152]{2,1,0:T(8,128)S(1)} custom-call(s32[6]{0:T(128)S(1)} %stack.42.scalars, f32[200,384]{1,0:T(8,128)S(1)} %collective-permute-done.24.lower, f32[512,384]{1,0:T(8,128)S(1)} %get-tuple-element.172.own.d_mid, f32[200,384]{1,0:T(8,128)S(1)} %collective-permute-done.25.upper, bf16[1536,1152]{1,0:T(8,128)(2,1)S(1)} %get-tuple-element.128.w, ...), custom_call_target="tpu_custom_call" | custom-call | flops 100000000 | bytes 262144 | tf_op jit(solution)/shard_map/pallas_call | solution.py:43
  111.5 1.5 collective-permute-start.28
  114.2 5.6 %shard_map.267.more = f32[2,208,1152]{2,1,0:T(8,128)S(1)} custom-call(s32[6]{0:T(128)S(1)} %stack.42.scalars, f32[200,384]{1,0:T(8,128)S(1)} %collective-permute-done.24.lower, f32[512,384]{1,0:T(8,128)S(1)} %get-tuple-element.172.own.d_mid, f32[200,384]{1,0:T(8,128)S(1)} %collective-permute-done.25.upper, bf16[1536,1152]{1,0:T(8,128)(2,1)S(1)} %get-tuple-element.128.w, ...), custom_call_target="tpu_custom_call" | custom-call | flops 100000000 | bytes 262144 | tf_op jit(solution)/shard_map/pallas_call | solution.py:43
  119.9 5.9 %shard_map.268 = (f32[4,48,384]{2,1,0:T(8,128)S(1)}, f32[4,48,384]{2,1,0:T(8,128)S(1)}, f32[4,48,384]{2,1,0:T(8,128)S(1)}, f32[4,48,384]{2,1,0:T(8,128)S(1)}, f3...) custom-call(s32[6]{0:T(128)S(1)} %stack.42.scalars, ...), custom_call_target="tpu_custom_call" | custom-call | flops 100000000 | bytes 262144 | tf_op jit(solution)/shard_map/pallas_call | solution.py:43
  125.8 3.6 %shard_map.269 = (f32[512,384]{1,0:T(8,128)}, f32[16,384]{1,0:T(8,128)S(1)}) custom-call(s32[6]{0:T(128)S(1)} %stack.42.scalars, bf16[512,1152]{1,0:T(8,128)(2,1)S(1)} %get-tuple-element.175.d_hi, bf16[512,1152]{1,0:T(8,128)(2,1)S(1)} %get-tuple-element.176.d_lo, bf16[1536,1152]{1,0:T(8,128)(2,1)S(1)} %get-tuple-element.128.w, f32[512,384]{1,0:T(8,128)S(1)} %copy-done, ...), custom_call_target="tpu_custom_call" | custom-call | flops 100000000 | bytes 262144 | tf_op jit(solution)/shard_map/pallas_call | solution.py:43
  132.1 1.8 collective-permute-start.44
  134.1 1.8 collective-permute-start.36
  137.7 1.9 collective-permute-done.45
  141.5 3.6 %collective-permute-done.36 = f32[4,48,384]{2,1,0:T(8,128)S(1)} collective-permute-done((f32[4,48,384]{2,1,0:T(8,128)S(1)}, f32[4,48,384]{2,1,0:T(8,128)S(1)}, u32[]{:S(2)}, u32[]{:S(2)}) %collective-permute-start.36) | collective-permute-done | bytes 294944 | tf_op jit(solution)/shard_map/ppermute | solution.py:699
  146.2 3.3 %collective-permute-done.35 = f32[4,48,384]{2,1,0:T(8,128)S(1)} collective-permute-done((f32[4,48,384]{2,1,0:T(8,128)S(1)}, f32[4,48,384]{2,1,0:T(8,128)S(1)}, u32[]{:S(2)}, u32[]{:S(2)}) %collective-permute-start.35) | collective-permute-done | bytes 294944 | tf_op jit(solution)/shard_map/ppermute | solution.py:699
  149.6 2.5 %collective-permute-start.40 = (f32[64,384]{1,0:T(8,128)S(1)}, f32[64,384]{1,0:T(8,128)S(1)}, u32[]{:S(2)}, u32[]{:S(2)}) collective-permute-start(f32[64,384]{1,0:T(8,128)S(1)} %get-tuple-element.255), channel_id=1, source_target_pairs={{0,6},{1,7},{2,0},{3,1},{4,2},{5,3},{6,4},{7,5},{8,14},{9,15},{10,... | collective-permute-start | bytes 294920 | tf_op jit(solution)/shard_map/ppermute | solution.py:694
  153.5 1.8 collective-permute-done.40
  155.3 6.2 %collective-permute-done.39 = f32[64,384]{1,0:T(8,128)S(1)} collective-permute-done((f32[64,384]{1,0:T(8,128)S(1)}, f32[64,384]{1,0:T(8,128)S(1)}, u32[]{:S(2)}, u32[]{:S(2)}) %collective-permute-start.39) | collective-permute-done | bytes 98336 | tf_op jit(solution)/shard_map/ppermute | solution.py:694
  162.6 1.4 collective-permute-start.48
  165.3 5.3 %collective-permute-done.47.refs_1_ = f32[160,384]{1,0:T(8,128)S(1)} collective-permute-done((f32[160,384]{1,0:T(8,128)S(1)}, f32[160,384]{1,0:T(8,128)S(1)}, u32[]{:S(2)}, u32[]{:S(2)}) %collective-permute-start.47) | collective-permute-done | bytes 245792 | tf_op jit(solution)/shard_map/ppermute | solution.py:699
  170.6 3.7 %collective-permute-done.48.refs_2_ = f32[160,384]{1,0:T(8,128)S(1)} collective-permute-done((f32[160,384]{1,0:T(8,128)S(1)}, f32[160,384]{1,0:T(8,128)S(1)}, u32[]{:S(2)}, u32[]{:S(2)}) %collective-permute-start.48) | collective-permute-done | bytes 245792 | tf_op jit(solution)/shard_map/ppermute | solution.py:699
  175.0 1.6 shard_map.270
  176.7 1.4 collective-permute-done.50
  178.2 1.3 collective-permute-start.53
  180.2 2.5 %collective-permute-start.52 = (f32[96,128]{1,0:T(8,128)S(1)}, f32[96,128]{1,0:T(8,128)S(1)}, u32[]{:S(2)}, u32[]{:S(2)}) collective-permute-start(f32[96,128]{1,0:T(8,128)S(1)} %get-tuple-element.250), channel_id=1, source_target_pairs={{0,4},{1,5},{2,6},{3,7},{4,0},{5,1},{6,2},{7,3},{8,12},{9,13},{10,... | collective-permute-start | bytes 147464 | tf_op jit(solution)/shard_map/ppermute | solution.py:694
  182.7 3.2 %collective-permute-done.51 = f32[96,128]{1,0:T(8,128)S(1)} collective-permute-done((f32[96,128]{1,0:T(8,128)S(1)}, f32[96,128]{1,0:T(8,128)S(1)}, u32[]{:S(2)}, u32[]{:S(2)}) %collective-permute-start.51) | collective-permute-done | bytes 49184 | tf_op jit(solution)/shard_map/ppermute | solution.py:694
  186.9 2.0 collective-permute-start.56
  191.5 2.4 %collective-permute-done.55 = f32[96,128]{1,0:T(8,128)S(1)} collective-permute-done((f32[96,128]{1,0:T(8,128)S(1)}, f32[96,128]{1,0:T(8,128)S(1)}, u32[]{:S(2)}, u32[]{:S(2)}) %collective-permute-start.55) | collective-permute-done | bytes 49184 | tf_op jit(solution)/shard_map/ppermute | solution.py:694
  196.3 15.4 %shard_map.271 = f32[192,384]{1,0:T(8,128)S(1)} custom-call(s32[6]{0:T(128)S(1)} %stack.42.scalars, f32[4,96,128]{2,1,0:T(8,128)S(1)} %pad_maximum_fusion.3.mine, f32[4,96,128]{2,1,0:T(8,128)S(1)} %collective-permute-done.57.other, f32[192,384]{1,0:T(8,128)S(1)} %get-tuple-element.212.own), custom_call_target="tpu_custom_call" | custom-call | flops 100000000 | bytes 262144 | tf_op jit(solution)/shard_map/pallas_call | solution.py:43
  211.7 1.8 collective-permute-start.60
  213.8 1.4 collective-permute-start.58
  217.0 5.6 %collective-permute-done.60 = f32[192,384]{1,0:T(8,128)S(1)} collective-permute-done((f32[192,384]{1,0:T(8,128)S(1)}, f32[192,384]{1,0:T(8,128)S(1)}, u32[]{:S(2)}, u32[]{:S(2)}) %collective-permute-start.60) | collective-permute-done | bytes 294944 | tf_op jit(solution)/shard_map/ppermute | solution.py:699
  222.5 5.5 %collective-permute-done.59 = f32[192,384]{1,0:T(8,128)S(1)} collective-permute-done((f32[192,384]{1,0:T(8,128)S(1)}, f32[192,384]{1,0:T(8,128)S(1)}, u32[]{:S(2)}, u32[]{:S(2)}) %collective-permute-start.59) | collective-permute-done | bytes 294944 | tf_op jit(solution)/shard_map/ppermute | solution.py:699
  (182 shorter events, 49.6 us)
Async XLA Ops:
  2.5 11.3 %collective-permute-start.2 = (f32[64,384]{1,0:T(8,128)S(1)}, f32[64,384]{1,0:T(8,128)S(1)}, u32[]{:S(2)}, u32[]{:S(2)}) collective-permute-start(f32[64,384]{1,0:T(8,128)S(1)} %maximum_maximum_fusion), channel_id=1, source_target_pairs={{0,6},{1,7},{2,0},{3,1},{4,2},{5,3},{6,4},{7,5},{8,14},{9,15},{10,... | collective-permute-start | bytes 294920 | tf_op jit(solution)/shard_map/ppermute | solution.py:694
  7.6 8.7 %collective-permute-start.1 = (f32[64,384]{1,0:T(8,128)S(1)}, f32[64,384]{1,0:T(8,128)S(1)}, u32[]{:S(2)}, u32[]{:S(2)}) collective-permute-start(f32[64,384]{1,0:T(8,128)S(1)} %maximum_maximum_fusion), channel_id=1, source_target_pairs={{0,4},{1,5},{2,6},{3,7},{4,0},{5,1},{6,2},{7,3},{8,12},{9,13},{10,... | collective-permute-start | bytes 294920 | tf_op jit(solution)/shard_map/ppermute | solution.py:694
  7.6 8.8 %collective-permute-start = (f32[64,384]{1,0:T(8,128)S(1)}, f32[64,384]{1,0:T(8,128)S(1)}, u32[]{:S(2)}, u32[]{:S(2)}) collective-permute-start(f32[64,384]{1,0:T(8,128)S(1)} %maximum_maximum_fusion), channel_id=1, source_target_pairs={{0,2},{1,3},{2,4},{3,5},{4,6},{5,7},{6,0},{7,1},{8,10},{9,11},{10,... | collective-permute-start | bytes 294920 | tf_op jit(solution)/shard_map/ppermute | solution.py:694
  9.7 6.7 %collective-permute-start.3 = (f32[200,384]{1,0:T(8,128)S(1)}, f32[200,384]{1,0:T(8,128)S(1)}, u32[]{:S(2)}, u32[]{:S(2)}) collective-permute-start(f32[200,384]{1,0:T(8,128)S(1)} %get-tuple-element.247), channel_id=1, source_target_pairs={{0,1},{1,2},{2,3},{3,4},{4,5},{5,6},{6,7},{8,9},{9,10},{10,11},{11... | collective-permute-start | bytes 921608 | tf_op jit(solution)/shard_map/ppermute | solution.py:703
  11.0 6.2 %collective-permute-start.4 = (f32[200,384]{1,0:T(8,128)S(1)}, f32[200,384]{1,0:T(8,128)S(1)}, u32[]{:S(2)}, u32[]{:S(2)}) collective-permute-start(f32[200,384]{1,0:T(8,128)S(1)} %get-tuple-element.246), channel_id=1, source_target_pairs={{1,0},{2,1},{3,2},{4,3},{5,4},{6,5},{7,6},{9,8},{10,9},{11,10},{12... | collective-permute-start | bytes 921608 | tf_op jit(solution)/shard_map/ppermute | solution.py:704
  17.2 9.3 %collective-permute-start.8 = (f32[96,384]{1,0:T(8,128)S(1)}, f32[96,384]{1,0:T(8,128)S(1)}, u32[]{:S(2)}, u32[]{:S(2)}) collective-permute-start(f32[96,384]{1,0:T(8,128)S(1)} %pad_maximum_fusion.8), channel_id=1, source_target_pairs={{0,2},{1,3},{2,4},{3,5},{4,6},{5,7},{6,0},{7,1},{8,10},{9,11},{10,... | collective-permute-start | bytes 442376 | tf_op jit(solution)/shard_map/ppermute | solution.py:694
  22.1 14.3 %collective-permute-start.5 = (f32[192,384]{1,0:T(8,128)S(1)}, f32[192,384]{1,0:T(8,128)S(1)}, u32[]{:S(2)}, u32[]{:S(2)}) collective-permute-start(f32[192,384]{1,0:T(8,128)S(1)} %pad_maximum_fusion.1.refs_0_), channel_id=1, source_target_pairs={{0,8},{8,0},{16,24},{24,16},{1,9},{9,1},{17,25},{25,17},{2,10},{10... | collective-permute-start | bytes 884744 | tf_op jit(solution)/shard_map/ppermute | solution.py:699
  23.6 15.2 %collective-permute-start.6 = (f32[192,384]{1,0:T(8,128)S(1)}, f32[192,384]{1,0:T(8,128)S(1)}, u32[]{:S(2)}, u32[]{:S(2)}) collective-permute-start(f32[192,384]{1,0:T(8,128)S(1)} %pad_maximum_fusion.1.refs_0_), channel_id=1, source_target_pairs={{0,16},{8,24},{16,0},{24,8},{1,17},{9,25},{17,1},{25,9},{2,18},{10... | collective-permute-start | bytes 884744 | tf_op jit(solution)/shard_map/ppermute | solution.py:699
  25.1 13.7 %collective-permute-start.7 = (f32[192,384]{1,0:T(8,128)S(1)}, f32[192,384]{1,0:T(8,128)S(1)}, u32[]{:S(2)}, u32[]{:S(2)}) collective-permute-start(f32[192,384]{1,0:T(8,128)S(1)} %pad_maximum_fusion.1.refs_0_), channel_id=1, source_target_pairs={{0,24},{8,16},{16,8},{24,0},{1,25},{9,17},{17,9},{25,1},{2,26},{10... | collective-permute-start | bytes 884744 | tf_op jit(solution)/shard_map/ppermute | solution.py:699
  25.6 10.3 %collective-permute-start.9 = (f32[96,384]{1,0:T(8,128)S(1)}, f32[96,384]{1,0:T(8,128)S(1)}, u32[]{:S(2)}, u32[]{:S(2)}) collective-permute-start(f32[96,384]{1,0:T(8,128)S(1)} %pad_maximum_fusion.8), channel_id=1, source_target_pairs={{0,4},{1,5},{2,6},{3,7},{4,0},{5,1},{6,2},{7,3},{8,12},{9,13},{10,... | collective-permute-start | bytes 442376 | tf_op jit(solution)/shard_map/ppermute | solution.py:694
  26.5 9.4 %collective-permute-start.10 = (f32[96,384]{1,0:T(8,128)S(1)}, f32[96,384]{1,0:T(8,128)S(1)}, u32[]{:S(2)}, u32[]{:S(2)}) collective-permute-start(f32[96,384]{1,0:T(8,128)S(1)} %pad_maximum_fusion.8), channel_id=1, source_target_pairs={{0,6},{1,7},{2,0},{3,1},{4,2},{5,3},{6,4},{7,5},{8,14},{9,15},{10,... | collective-permute-start | bytes 442376 | tf_op jit(solution)/shard_map/ppermute | solution.py:694
  35.9 6.7 %collective-permute-start.14 = (f32[192,384]{1,0:T(8,128)S(1)}, f32[192,384]{1,0:T(8,128)S(1)}, u32[]{:S(2)}, u32[]{:S(2)}) collective-permute-start(f32[192,384]{1,0:T(8,128)S(1)} %pad_maximum_fusion.1.refs_0_), channel_id=1, source_target_pairs={{0,1},{1,0},{2,3},{3,2},{4,5},{5,4},{6,7},{7,6},{8,9},{9,8},{10,11... | collective-permute-start | bytes 884744 | tf_op jit(solution)/shard_map/ppermute | solution.py:691
  35.9 5.2 %collective-permute-start.18 = (f32[64,384]{1,0:T(8,128)S(1)}, f32[64,384]{1,0:T(8,128)S(1)}, u32[]{:S(2)}, u32[]{:S(2)}) collective-permute-start(f32[64,384]{1,0:T(8,128)S(1)} %pad_maximum_fusion.9.refs_8_), channel_id=1, source_target_pairs={{0,1},{1,0},{2,3},{3,2},{4,5},{5,4},{6,7},{7,6},{8,9},{9,8},{10,11... | collective-permute-start | bytes 294920 | tf_op jit(solution)/shard_map/ppermute | solution.py:691
  39.0 23.1 %collective-permute-start.13 = (f32[384,384]{1,0:T(8,128)S(1)}, f32[384,384]{1,0:T(8,128)S(1)}, u32[]{:S(2)}, u32[]{:S(2)}) collective-permute-start(f32[384,384]{1,0:T(8,128)S(1)} %constant_dynamic-update-slice_fusion.refs_0_), channel_id=1, source_target_pairs={{0,8},{8,0},{16,24},{24,16},{1,9},{9,1},{17,25},{25,17},{2,10},{10... | collective-permute-start | bytes 1769480 | tf_op jit(solution)/shard_map/ppermute | solution.py:699
  40.3 26.5 %collective-permute-start.12 = (f32[384,384]{1,0:T(8,128)S(1)}, f32[384,384]{1,0:T(8,128)S(1)}, u32[]{:S(2)}, u32[]{:S(2)}) collective-permute-start(f32[384,384]{1,0:T(8,128)S(1)} %constant_dynamic-update-slice_fusion.refs_0_), channel_id=1, source_target_pairs={{0,16},{8,24},{16,0},{24,8},{1,17},{9,25},{17,1},{25,9},{2,18},{10... | collective-permute-start | bytes 1769480 | tf_op jit(solution)/shard_map/ppermute | solution.py:699
  41.1 27.3 %collective-permute-start.11 = (f32[384,384]{1,0:T(8,128)S(1)}, f32[384,384]{1,0:T(8,128)S(1)}, u32[]{:S(2)}, u32[]{:S(2)}) collective-permute-start(f32[384,384]{1,0:T(8,128)S(1)} %constant_dynamic-update-slice_fusion.refs_0_), channel_id=1, source_target_pairs={{0,24},{8,16},{16,8},{24,0},{1,25},{9,17},{17,9},{25,1},{2,26},{10... | collective-permute-start | bytes 1769480 | tf_op jit(solution)/shard_map/ppermute | solution.py:699
  44.1 24.8 %collective-permute-start.19 = (f32[384,384]{1,0:T(8,128)S(1)}, f32[384,384]{1,0:T(8,128)S(1)}, u32[]{:S(2)}, u32[]{:S(2)}) collective-permute-start(f32[384,384]{1,0:T(8,128)S(1)} %constant_dynamic-update-slice_fusion.refs_0_), channel_id=1, source_target_pairs={{0,1},{1,0},{2,3},{3,2},{4,5},{5,4},{6,7},{7,6},{8,9},{9,8},{10,11... | collective-permute-start | bytes 1769480 | tf_op jit(solution)/shard_map/ppermute | solution.py:691
  83.7 6.1 %collective-permute-start.23 = (f32[4,4,48,384]{3,2,1,0:T(8,128)S(1)}, f32[4,4,48,384]{3,2,1,0:T(8,128)S(1)}, u32[]{:S(2)}, u32[]{:S(2)}) collective-permute-start(f32[4,4,48,384]{3,2,1,0:T(8,128)S(1)} %get-tuple-element.140), channel_id=1, source_target_pairs={{0,1},{1,0},{2,3},{3,2},{4,5},{5,4},{6,7},{7,6},{8,9},{9,8},{10,11... | collective-permute-start | bytes 3538952 | tf_op jit(solution)/shard_map/ppermute | solution.py:691
  90.0 7.2 %collective-permute-start.24 = (f32[200,384]{1,0:T(8,128)S(1)}, f32[200,384]{1,0:T(8,128)S(1)}, u32[]{:S(2)}, u32[]{:S(2)}) collective-permute-start(f32[200,384]{1,0:T(8,128)S(1)} %get-tuple-element.245), channel_id=1, source_target_pairs={{0,1},{1,2},{2,3},{3,4},{4,5},{5,6},{6,7},{8,9},{9,10},{10,11},{11... | collective-permute-start | bytes 921608 | tf_op jit(solution)/shard_map/ppermute | solution.py:703
  97.2 13.3 %collective-permute-start.26 = (f32[4,4,48,384]{3,2,1,0:T(8,128)S(1)}, f32[4,4,48,384]{3,2,1,0:T(8,128)S(1)}, u32[]{:S(2)}, u32[]{:S(2)}) collective-permute-start(f32[4,4,48,384]{3,2,1,0:T(8,128)S(1)} %get-tuple-element.158), channel_id=1, source_target_pairs={{0,1},{1,0},{2,3},{3,2},{4,5},{5,4},{6,7},{7,6},{8,9},{9,8},{10,11... | collective-permute-start | bytes 3538952 | tf_op jit(solution)/shard_map/ppermute | solution.py:691
  101.4 11.7 %collective-permute-start.30 = (f32[4,48,384]{2,1,0:T(8,128)S(1)}, f32[4,48,384]{2,1,0:T(8,128)S(1)}, u32[]{:S(2)}, u32[]{:S(2)}) collective-permute-start(f32[4,48,384]{2,1,0:T(8,128)S(1)} %get-tuple-element.191), channel_id=1, source_target_pairs={{0,8},{8,0},{16,24},{24,16},{1,9},{9,1},{17,25},{25,17},{2,10},{10... | collective-permute-start | bytes 884744 | tf_op jit(solution)/shard_map/ppermute | solution.py:699
  102.2 27.2 %collective-permute-start.31 = (f32[4,48,384]{2,1,0:T(8,128)S(1)}, f32[4,48,384]{2,1,0:T(8,128)S(1)}, u32[]{:S(2)}, u32[]{:S(2)}) collective-permute-start(f32[4,48,384]{2,1,0:T(8,128)S(1)} %get-tuple-element.192), channel_id=1, source_target_pairs={{0,16},{8,24},{16,0},{24,8},{1,17},{9,25},{17,1},{25,9},{2,18},{10... | collective-permute-start | bytes 884744 | tf_op jit(solution)/shard_map/ppermute | solution.py:699
  103.7 25.7 %collective-permute-start.32 = (f32[4,48,384]{2,1,0:T(8,128)S(1)}, f32[4,48,384]{2,1,0:T(8,128)S(1)}, u32[]{:S(2)}, u32[]{:S(2)}) collective-permute-start(f32[4,48,384]{2,1,0:T(8,128)S(1)} %get-tuple-element.193), channel_id=1, source_target_pairs={{0,24},{8,16},{16,8},{24,0},{1,25},{9,17},{17,9},{25,1},{2,26},{10... | collective-permute-start | bytes 884744 | tf_op jit(solution)/shard_map/ppermute | solution.py:699
  110.7 18.7 %collective-permute-start.27 = (f32[4,48,384]{2,1,0:T(8,128)S(1)}, f32[4,48,384]{2,1,0:T(8,128)S(1)}, u32[]{:S(2)}, u32[]{:S(2)}) collective-permute-start(f32[4,48,384]{2,1,0:T(8,128)S(1)} %get-tuple-element.187), channel_id=1, source_target_pairs={{0,8},{8,0},{16,24},{24,16},{1,9},{9,1},{17,25},{25,17},{2,10},{10... | collective-permute-start | bytes 884744 | tf_op jit(solution)/shard_map/ppermute | solution.py:699
  111.5 18.2 %collective-permute-start.28 = (f32[4,48,384]{2,1,0:T(8,128)S(1)}, f32[4,48,384]{2,1,0:T(8,128)S(1)}, u32[]{:S(2)}, u32[]{:S(2)}) collective-permute-start(f32[4,48,384]{2,1,0:T(8,128)S(1)} %get-tuple-element.188), channel_id=1, source_target_pairs={{0,16},{8,24},{16,0},{24,8},{1,17},{9,25},{17,1},{25,9},{2,18},{10... | collective-permute-start | bytes 884744 | tf_op jit(solution)/shard_map/ppermute | solution.py:699
  113.1 16.7 %collective-permute-start.29 = (f32[4,48,384]{2,1,0:T(8,128)S(1)}, f32[4,48,384]{2,1,0:T(8,128)S(1)}, u32[]{:S(2)}, u32[]{:S(2)}) collective-permute-start(f32[4,48,384]{2,1,0:T(8,128)S(1)} %get-tuple-element.189), channel_id=1, source_target_pairs={{0,24},{8,16},{16,8},{24,0},{1,25},{9,17},{17,9},{25,1},{2,26},{10... | collective-permute-start | bytes 884744 | tf_op jit(solution)/shard_map/ppermute | solution.py:699
  129.8 6.1 %collective-permute-start.37 = (f32[16,384]{1,0:T(8,128)S(1)}, f32[16,384]{1,0:T(8,128)S(1)}, u32[]{:S(2)}, u32[]{:S(2)}) collective-permute-start(f32[16,384]{1,0:T(8,128)S(1)} %get-tuple-element.199), channel_id=1, source_target_pairs={{0,1},{1,0},{2,3},{3,2},{4,5},{5,4},{6,7},{7,6},{8,9},{9,8},{10,11... | collective-permute-start | bytes 73736 | tf_op jit(solution)/shard_map/ppermute | solution.py:691
  130.3 6.1 %collective-permute-start.46 = (f32[48,384]{1,0:T(8,128)S(1)}, f32[48,384]{1,0:T(8,128)S(1)}, u32[]{:S(2)}, u32[]{:S(2)}) collective-permute-start(f32[48,384]{1,0:T(8,128)S(1)} %get-tuple-element.222), channel_id=1, source_target_pairs={{0,6},{1,7},{2,0},{3,1},{4,2},{5,3},{6,4},{7,5},{8,14},{9,15},{10,... | collective-permute-start | bytes 221192 | tf_op jit(solution)/shard_map/ppermute | solution.py:694
  131.6 8.0 %collective-permute-start.45 = (f32[48,384]{1,0:T(8,128)S(1)}, f32[48,384]{1,0:T(8,128)S(1)}, u32[]{:S(2)}, u32[]{:S(2)}) collective-permute-start(f32[48,384]{1,0:T(8,128)S(1)} %get-tuple-element.223), channel_id=1, source_target_pairs={{0,4},{1,5},{2,6},{3,7},{4,0},{5,1},{6,2},{7,3},{8,12},{9,13},{10,... | collective-permute-start | bytes 221192 | tf_op jit(solution)/shard_map/ppermute | solution.py:694
  132.1 8.7 %collective-permute-start.44 = (f32[48,384]{1,0:T(8,128)S(1)}, f32[48,384]{1,0:T(8,128)S(1)}, u32[]{:S(2)}, u32[]{:S(2)}) collective-permute-start(f32[48,384]{1,0:T(8,128)S(1)} %get-tuple-element.221), channel_id=1, source_target_pairs={{0,2},{1,3},{2,4},{3,5},{4,6},{5,7},{6,0},{7,1},{8,10},{9,11},{10,... | collective-permute-start | bytes 221192 | tf_op jit(solution)/shard_map/ppermute | solution.py:694
  134.1 11.0 %collective-permute-start.36 = (f32[4,48,384]{2,1,0:T(8,128)S(1)}, f32[4,48,384]{2,1,0:T(8,128)S(1)}, u32[]{:S(2)}, u32[]{:S(2)}) collective-permute-start(f32[4,48,384]{2,1,0:T(8,128)S(1)} %get-tuple-element.229), channel_id=1, source_target_pairs={{0,24},{8,16},{16,8},{24,0},{1,25},{9,17},{17,9},{25,1},{2,26},{10... | collective-permute-start | bytes 884744 | tf_op jit(solution)/shard_map/ppermute | solution.py:699
  135.9 13.6 %collective-permute-start.35 = (f32[4,48,384]{2,1,0:T(8,128)S(1)}, f32[4,48,384]{2,1,0:T(8,128)S(1)}, u32[]{:S(2)}, u32[]{:S(2)}) collective-permute-start(f32[4,48,384]{2,1,0:T(8,128)S(1)} %get-tuple-element.230), channel_id=1, source_target_pairs={{0,16},{8,24},{16,0},{24,8},{1,17},{9,25},{17,1},{25,9},{2,18},{10... | collective-permute-start | bytes 884744 | tf_op jit(solution)/shard_map/ppermute | solution.py:699
  136.4 13.1 %collective-permute-start.34 = (f32[4,48,384]{2,1,0:T(8,128)S(1)}, f32[4,48,384]{2,1,0:T(8,128)S(1)}, u32[]{:S(2)}, u32[]{:S(2)}) collective-permute-start(f32[4,48,384]{2,1,0:T(8,128)S(1)} %get-tuple-element.231), channel_id=1, source_target_pairs={{0,8},{8,0},{16,24},{24,16},{1,9},{9,1},{17,25},{25,17},{2,10},{10... | collective-permute-start | bytes 884744 | tf_op jit(solution)/shard_map/ppermute | solution.py:699
  139.6 12.9 %collective-permute-start.43 = (f32[48,384]{1,0:T(8,128)S(1)}, f32[48,384]{1,0:T(8,128)S(1)}, u32[]{:S(2)}, u32[]{:S(2)}) collective-permute-start(f32[48,384]{1,0:T(8,128)S(1)} %get-tuple-element.219), channel_id=1, source_target_pairs={{0,6},{1,7},{2,0},{3,1},{4,2},{5,3},{6,4},{7,5},{8,14},{9,15},{10,... | collective-permute-start | bytes 221192 | tf_op jit(solution)/shard_map/ppermute | solution.py:694
  140.8 12.6 %collective-permute-start.42 = (f32[48,384]{1,0:T(8,128)S(1)}, f32[48,384]{1,0:T(8,128)S(1)}, u32[]{:S(2)}, u32[]{:S(2)}) collective-permute-start(f32[48,384]{1,0:T(8,128)S(1)} %get-tuple-element.220), channel_id=1, source_target_pairs={{0,4},{1,5},{2,6},{3,7},{4,0},{5,1},{6,2},{7,3},{8,12},{9,13},{10,... | collective-permute-start | bytes 221192 | tf_op jit(solution)/shard_map/ppermute | solution.py:694
  145.1 8.4 %collective-permute-start.41 = (f32[48,384]{1,0:T(8,128)S(1)}, f32[48,384]{1,0:T(8,128)S(1)}, u32[]{:S(2)}, u32[]{:S(2)}) collective-permute-start(f32[48,384]{1,0:T(8,128)S(1)} %get-tuple-element.218), channel_id=1, source_target_pairs={{0,2},{1,3},{2,4},{3,5},{4,6},{5,7},{6,0},{7,1},{8,10},{9,11},{10,... | collective-permute-start | bytes 221192 | tf_op jit(solution)/shard_map/ppermute | solution.py:694
  149.6 5.7 %collective-permute-start.40 = (f32[64,384]{1,0:T(8,128)S(1)}, f32[64,384]{1,0:T(8,128)S(1)}, u32[]{:S(2)}, u32[]{:S(2)}) collective-permute-start(f32[64,384]{1,0:T(8,128)S(1)} %get-tuple-element.255), channel_id=1, source_target_pairs={{0,6},{1,7},{2,0},{3,1},{4,2},{5,3},{6,4},{7,5},{8,14},{9,15},{10,... | collective-permute-start | bytes 294920 | tf_op jit(solution)/shard_map/ppermute | solution.py:694
  152.1 9.4 %collective-permute-start.39 = (f32[64,384]{1,0:T(8,128)S(1)}, f32[64,384]{1,0:T(8,128)S(1)}, u32[]{:S(2)}, u32[]{:S(2)}) collective-permute-start(f32[64,384]{1,0:T(8,128)S(1)} %get-tuple-element.254), channel_id=1, source_target_pairs={{0,4},{1,5},{2,6},{3,7},{4,0},{5,1},{6,2},{7,3},{8,12},{9,13},{10,... | collective-permute-start | bytes 294920 | tf_op jit(solution)/shard_map/ppermute | solution.py:694
  152.6 9.0 %collective-permute-start.38 = (f32[64,384]{1,0:T(8,128)S(1)}, f32[64,384]{1,0:T(8,128)S(1)}, u32[]{:S(2)}, u32[]{:S(2)}) collective-permute-start(f32[64,384]{1,0:T(8,128)S(1)} %get-tuple-element.253), channel_id=1, source_target_pairs={{0,2},{1,3},{2,4},{3,5},{4,6},{5,7},{6,0},{7,1},{8,10},{9,11},{10,... | collective-permute-start | bytes 294920 | tf_op jit(solution)/shard_map/ppermute | solution.py:694
  161.7 8.9 %collective-permute-start.47 = (f32[160,384]{1,0:T(8,128)S(1)}, f32[160,384]{1,0:T(8,128)S(1)}, u32[]{:S(2)}, u32[]{:S(2)}) collective-permute-start(f32[160,384]{1,0:T(8,128)S(1)} %pad_maximum_fusion.2.refs_0_), channel_id=1, source_target_pairs={{0,8},{8,0},{16,24},{24,16},{1,9},{9,1},{17,25},{25,17},{2,10},{10... | collective-permute-start | bytes 737288 | tf_op jit(solution)/shard_map/ppermute | solution.py:699
  162.6 11.6 %collective-permute-start.48 = (f32[160,384]{1,0:T(8,128)S(1)}, f32[160,384]{1,0:T(8,128)S(1)}, u32[]{:S(2)}, u32[]{:S(2)}) collective-permute-start(f32[160,384]{1,0:T(8,128)S(1)} %pad_maximum_fusion.2.refs_0_), channel_id=1, source_target_pairs={{0,16},{8,24},{16,0},{24,8},{1,17},{9,25},{17,1},{25,9},{2,18},{10... | collective-permute-start | bytes 737288 | tf_op jit(solution)/shard_map/ppermute | solution.py:699
  164.0 11.0 %collective-permute-start.49 = (f32[160,384]{1,0:T(8,128)S(1)}, f32[160,384]{1,0:T(8,128)S(1)}, u32[]{:S(2)}, u32[]{:S(2)}) collective-permute-start(f32[160,384]{1,0:T(8,128)S(1)} %pad_maximum_fusion.2.refs_0_), channel_id=1, source_target_pairs={{0,24},{8,16},{16,8},{24,0},{1,25},{9,17},{17,9},{25,1},{2,26},{10... | collective-permute-start | bytes 737288 | tf_op jit(solution)/shard_map/ppermute | solution.py:699
  179.5 6.4 %collective-permute-start.51 = (f32[96,128]{1,0:T(8,128)S(1)}, f32[96,128]{1,0:T(8,128)S(1)}, u32[]{:S(2)}, u32[]{:S(2)}) collective-permute-start(f32[96,128]{1,0:T(8,128)S(1)} %get-tuple-element.252), channel_id=1, source_target_pairs={{0,2},{1,3},{2,4},{3,5},{4,6},{5,7},{6,0},{7,1},{8,10},{9,11},{10,... | collective-permute-start | bytes 147464 | tf_op jit(solution)/shard_map/ppermute | solution.py:694
  180.2 6.6 %collective-permute-start.52 = (f32[96,128]{1,0:T(8,128)S(1)}, f32[96,128]{1,0:T(8,128)S(1)}, u32[]{:S(2)}, u32[]{:S(2)}) collective-permute-start(f32[96,128]{1,0:T(8,128)S(1)} %get-tuple-element.250), channel_id=1, source_target_pairs={{0,4},{1,5},{2,6},{3,7},{4,0},{5,1},{6,2},{7,3},{8,12},{9,13},{10,... | collective-permute-start | bytes 147464 | tf_op jit(solution)/shard_map/ppermute | solution.py:694
  188.9 5.9 %collective-permute-start.54 = (f32[96,128]{1,0:T(8,128)S(1)}, f32[96,128]{1,0:T(8,128)S(1)}, u32[]{:S(2)}, u32[]{:S(2)}) collective-permute-start(f32[96,128]{1,0:T(8,128)S(1)} %fusion.30), channel_id=1, source_target_pairs={{0,2},{1,3},{2,4},{3,5},{4,6},{5,7},{6,0},{7,1},{8,10},{9,11},{10,... | collective-permute-start | bytes 147464 | tf_op jit(solution)/shard_map/ppermute | solution.py:694
  211.7 10.9 %collective-permute-start.60 = (f32[192,384]{1,0:T(8,128)S(1)}, f32[192,384]{1,0:T(8,128)S(1)}, u32[]{:S(2)}, u32[]{:S(2)}) collective-permute-start(f32[192,384]{1,0:T(8,128)S(1)} %shard_map.271), channel_id=1, source_target_pairs={{0,24},{8,16},{16,8},{24,0},{1,25},{9,17},{17,9},{25,1},{2,26},{10... | collective-permute-start | bytes 884744 | tf_op jit(solution)/shard_map/ppermute | solution.py:699
  213.4 14.6 %collective-permute-start.59 = (f32[192,384]{1,0:T(8,128)S(1)}, f32[192,384]{1,0:T(8,128)S(1)}, u32[]{:S(2)}, u32[]{:S(2)}) collective-permute-start(f32[192,384]{1,0:T(8,128)S(1)} %shard_map.271), channel_id=1, source_target_pairs={{0,16},{8,24},{16,0},{24,8},{1,17},{9,25},{17,1},{25,9},{2,18},{10... | collective-permute-start | bytes 884744 | tf_op jit(solution)/shard_map/ppermute | solution.py:699
  213.8 14.2 %collective-permute-start.58 = (f32[192,384]{1,0:T(8,128)S(1)}, f32[192,384]{1,0:T(8,128)S(1)}, u32[]{:S(2)}, u32[]{:S(2)}) collective-permute-start(f32[192,384]{1,0:T(8,128)S(1)} %shard_map.271), channel_id=1, source_target_pairs={{0,8},{8,0},{16,24},{24,16},{1,9},{9,1},{17,25},{25,17},{2,10},{10... | collective-permute-start | bytes 884744 | tf_op jit(solution)/shard_map/ppermute | solution.py:699
  (37 other events, 409.0 us)
where the time goes:
time: 231 us; the launch traced here: 230 us
  Pallas kernels  73.2 us (32%)
  waiting for transfers between devices  72 us (31%)
  starting transfers between devices  69.8 us (30%)
  local copies, waits for them, and re-layouts  8.37 us (4%)
  other arithmetic  4.99 us (2%)
    pallas_call x12, Pallas kernels, run(): pl.pallas_call(body, out_shape=[jax.ShapeDtypeStruct(s, t) for s, t in ou...  73.2 us
    ppermute x21, waiting for transfers between devices, cross(): return lax.ppermute(x, 'replica', [(i, i ^ by) for i in range(replicas)])  36.7 us
    ppermute x21, starting transfers between devices, rotate(): lax.ppermute(x, 'group', [(i, (i + 2 * by) % group_size) for i in range(g...  32.1 us
    ppermute x21, waiting for transfers between devices, rotate(): lax.ppermute(x, 'group', [(i, (i + 2 * by) % group_size) for i in range(g...  27.8 us
    ppermute x21, starting transfers between devices, cross(): return lax.ppermute(x, 'replica', [(i, i ^ by) for i in range(replicas)])  24.7 us
    ppermute x15, waiting for transfers between devices, swap(): return lax.ppermute(x, 'group', [(i, i ^ 1) for i in range(group_size)])  6.74 us
    ppermute x15, starting transfers between devices, swap(): return lax.ppermute(x, 'group', [(i, i ^ 1) for i in range(group_size)])  6.74 us
  transfers between devices with their start and end apart: 61, of which 29 were waited for; matrix products, arithmetic and copies ran while one was open for 3% of the time, Pallas kernels for 19%

commit v1 on v0

--- a/solution.py
+++ b/solution.py
@@ -266,7 +266,10 @@
     )(scalars, mid, cot, w, vec, bias)
 
 
-def mlp_back_kernel(scalars, mid, cot, w, vec, slope, m3, dmid, d_hi, d_lo, dvec, dbias):
+def mlp_back_kernel(scalars, mid, cot, w, vec, slope, n3, m3, dmid, dvec, *rest):
+    parts, (total, d_hi, d_lo, dbias) = rest[:-4], rest[-4:]
+    if len(parts) == 1:
+        total = parts[0]
     rows = mid.shape[0]
 
     def tile_step(t, carry):
@@ -276,9 +279,11 @@
         hi, lo = halves(d_pre)
         d_hi[:, pl.ds(at, TILE)] = hi
         d_lo[:, pl.ds(at, TILE)] = lo
+        total[pl.ds(at, TILE), :] = by_tokens(hi, lo, n3)
         return carry
 
     lax.fori_loop(0, FF // TILE, tile_step, 0)
+    scatter_parts(scalars, total, parts, quarter_rows)
     d_norm = by_rows(d_hi[...], d_lo[...], w[:FF, :])
     xhat, rstd = standardized(mid[...])
     live = lax.broadcasted_iota(jnp.int32, (rows, 1), 0) < scalars[2]
@@ -294,19 +299,20 @@
     )
 
 
-def mlp_back(scalars, mid, cot, w, vec, slope, m3):
+def mlp_back(scalars, parts, mid, cot, w, vec, slope, n3, m3):
     rows = mid.shape[0]
+    outs, scratch = part_outs(parts, FF)
     return call(
         mlp_back_kernel,
-        [((rows, D), f32)] + [((rows, FF), bf16)] * 2 + [((16, D), f32)],
-        [((8, FF), f32)],
+        [((rows, D), f32), ((16, D), f32)] + outs,
+        [scratch] + [((rows, FF), bf16)] * 2 + [((8, FF), f32)],
         flops=10**8,
         data=1 << 18,
-    )(scalars, mid, cot, w, vec, slope, m3)
-
-
-def place(scalars, chips, i, j, k):
-    owner = 2 * lax.rem(scalars[4] + k, chips) + lax.bitwise_xor(scalars[5], i)
+    )(scalars, mid, cot, w, vec, slope, n3, m3)
+
+
+def place(scalars, i, j, k):
+    owner = 2 * lax.bitwise_xor(scalars[4], k) + lax.bitwise_xor(scalars[5], i)
     return owner, lax.bitwise_xor(scalars[3], j)
 
 
@@ -338,31 +344,12 @@
     chips, piece, _ = outs[0].shape
     for n in range(8):
         for k in range(chips):
-            owner, quarter = place(scalars, chips, n // 4, n % 4, k)
+            owner, quarter = place(scalars, n // 4, n % 4, k)
             rows = total[pl.ds(rows_of(owner, quarter, piece), piece), :]
             if n < 4:
                 outs[n][k] = rows
             else:
                 outs[4][n - 4, k] = rows
-
-
-def up_grads_kernel(scalars, d_hi, d_lo, n3, *rest):
-    outs, total = rest[:-1], rest[-1]
-    if len(outs) == 1:
-        total = outs[0]
-
-    def tile_step(t, carry):
-        at = pl.multiple_of(t * TILE, TILE)
-        total[pl.ds(at, TILE), :] = by_tokens(d_hi[:, pl.ds(at, TILE)], d_lo[:, pl.ds(at, TILE)], n3)
-        return carry
-
-    lax.fori_loop(0, FF // TILE, tile_step, 0)
-    scatter_parts(scalars, total, outs, quarter_rows)
-
-
-def up_grads(scalars, parts, *arrays):
-    outs, scratch = part_outs(parts, FF)
-    return call(up_grads_kernel, outs, [scratch], flops=10**8, data=1 << 18)(scalars, *arrays)
 
 
 def attend_back_kernel(first_slot, scalars, lower, own, upper, w, q2, kt2, v2, probs_hi, probs_lo, out, window):
@@ -470,13 +457,13 @@
 def unpack_kernel(rows_of, chips, piece, step, scalars, *refs):
     mine, other, rest = refs[:4], refs[4:8], refs[8:]
     if step:
-        vectors, (w, vec, bias, flat) = rest[:2], rest[2:]
+        vectors, (w, vec, bias) = rest[:2], rest[2:]
     else:
         (w,) = rest
     for i, parts in enumerate((mine, other)):
         for j in range(4):
             for k in range(chips):
-                owner, quarter = place(scalars, chips, i, j, chips - k)
+                owner, quarter = place(scalars, i, j, k)
                 at = rows_of(owner, quarter, piece)
                 at = at if isinstance(at, tuple) else (at,)
                 share = piece // len(at)
@@ -484,16 +471,20 @@
                     base = k * piece + n * share
                     store_split(w, to, parts[j][base : base + share, :])
     if step:
+        width = D // (2 * chips)
+        lane = lax.broadcasted_iota(jnp.int32, (step, D), 1)
+        sums = [jnp.zeros((step, D), f32), jnp.zeros((step, D), f32)]
         for i, parts in enumerate(vectors):
             for k in range(chips):
-                owner, _ = place(scalars, chips, i, 0, chips - k)
-                for s in range(3):
-                    flat[pl.ds(pl.multiple_of((owner * 3 + s) * step, step), step), :] = parts[
-                        k * step : (k + 1) * step, s * 128 : (s + 1) * 128
-                    ]
-        rows = jnp.transpose(flat[...])[:16, :]
-        vec[...] = rows
-        bias[...] = jnp.concatenate([rows[8 + s : 9 + s, :] for s in range(4)], axis=1)
+                owner, _ = place(scalars, i, 0, k)
+                block = parts[k * step : (k + 1) * step, :]
+                for n in range(2):
+                    mine_only = jnp.where((lane >= n * width) & (lane < (n + 1) * width), block, 0.0)
+                    shift = lax.rem((owner - n) * width + D, D)
+                    sums[n] = sums[n] + pltpu.roll(mine_only, shift, 1)
+        vec[:step, :] = sums[0]
+        vec[step:, :] = sums[1]
+        bias[...] = jnp.concatenate([sums[1][s : s + 1, :] for s in range(4)], axis=1)
 
 
 def unpack(scalars, chips, mine, other, rows_of, *vectors):
@@ -510,32 +501,27 @@
             vectors[0].shape[0] // chips if vectors else 0,
         ),
         outs,
-        [((D, 128), f32)] if vectors else [],
+        [],
         flops=10**8,
         data=1 << 18,
     )(scalars, *mine, *other, *vectors)
 
 
-def own_gradients_kernel(scalars, *refs):
-    parts, (mom, grads, new_mom, own, *gram) = refs[:4], refs[4:]
-    piece = own.shape[0] // 4
-    for j in range(4):
-        quarter = lax.bitwise_xor(scalars[3], j)
-        grads[pl.ds(pl.multiple_of(quarter * piece, piece), piece), :] = parts[j][:piece, :]
-        for n in (1, 2):
-            grads[pl.ds(pl.multiple_of((4 * n + quarter) * piece, piece), piece), :] = parts[j][
-                n * piece : (n + 1) * piece, :
-            ]
-    new_mom[...] = muon_momentum * mom[...] + grads[...]
+def own_gradients_kernel(scalars, mine, *refs):
+    others, (mom, own, keep, send, total) = refs[:3], refs[3:]
+    piece = mine.shape[0] // 3
     replica = scalars[3]
-    start = jnp.where(replica == 0, 4, jnp.where(replica == 1, 0, jnp.where(replica == 2, 8, 3)))
-    count = jnp.where(replica == 1, 3, jnp.where(replica == 3, 1, 4)) * piece
+    start = jnp.where(replica == 0, 4, jnp.where(replica == 2, 8, 0)) * piece
+    at = pl.multiple_of(jnp.where(replica == 0, 1, jnp.where(replica == 2, 2, 0)) * piece, piece)
+    own[...] = muon_momentum * mom[pl.ds(pl.multiple_of(start, piece), 4 * piece), :]
+    for j, part in enumerate((mine, *others)):
+        quarter = lax.bitwise_xor(replica, j)
+        rows = pl.ds(pl.multiple_of(quarter * piece, piece), piece)
+        own[rows, :] = own[rows, :] + (part[pl.ds(at, piece), :] if j == 0 else part[...])
     row = lax.broadcasted_iota(jnp.int32, (4 * piece, 1), 0)
-    block = jnp.where(
-        row < count, new_mom[pl.ds(pl.multiple_of(start * piece, piece), 4 * piece), :], 0.0
-    )
+    drop = ((replica == 1) & (row >= 3 * piece)) | ((replica == 3) & (row < 3 * piece))
+    block = jnp.where(drop, 0.0, own[...])
     own[...] = block
-    keep, send, total = gram
     gram = fdot(block, block, TN, precise)
     for n, (row, column) in enumerate(UPPER):
         total[n * 128 : (n + 1) * 128, :] = gram[
@@ -544,20 +530,36 @@
     chips, share, _ = keep.shape
     for i, out in enumerate((keep, send)):
         for k in range(chips):
-            at = lax.bitwise_xor(scalars[5], i) * chips + lax.rem(scalars[4] + k, chips)
+            at = lax.bitwise_xor(scalars[5], i) * chips + lax.bitwise_xor(scalars[4], k)
             out[k] = total[pl.ds(pl.multiple_of(at * share, share), share), :]
 
 
-def own_gradients(scalars, parts, mom, chips):
-    rows = mom.shape[0]
+def own_gradients(scalars, mine, others, mom, chips):
     share = 128 * len(UPPER) // (2 * chips)
     return call(
         own_gradients_kernel,
-        [((rows, D), f32)] * 2 + [((rows // 3, D), f32)] + [((chips, share, 128), f32)] * 2,
+        [((mom.shape[0] // 3, D), f32)] + [((chips, share, 128), f32)] * 2,
         [((128 * len(UPPER), 128), f32)],
         flops=10**8,
         data=1 << 18,
-    )(scalars, *parts, mom)
+    )(scalars, mine, *others, mom)
+
+
+def all_gradients_kernel(scalars, *refs):
+    parts, (mom, grads, new_mom) = refs[:4], refs[4:]
+    piece = mom.shape[0] // 12
+    for j in range(4):
+        quarter = lax.bitwise_xor(scalars[3], j)
+        for n in range(3):
+            rows = pl.ds(pl.multiple_of((4 * n + quarter) * piece, piece), piece)
+            grads[rows, :] = parts[j][n * piece : (n + 1) * piece, :]
+    new_mom[...] = muon_momentum * mom[...] + grads[...]
+
+
+def all_gradients(scalars, parts, mom):
+    return call(all_gradients_kernel, [(mom.shape, f32)] * 2, flops=10**8, data=1 << 18)(
+        scalars, *parts, mom
+    )
 
 
 def pieces(x):
@@ -617,7 +619,7 @@
     chips, share, _ = mine.shape
     for i, parts in enumerate((mine, other)):
         for k in range(chips):
-            at = lax.bitwise_xor(scalars[5], i) * chips + lax.rem(scalars[4] + chips - k, chips)
+            at = lax.bitwise_xor(scalars[5], i) * chips + lax.bitwise_xor(scalars[4], k)
             total[pl.ds(pl.multiple_of(at * share, share), share), :] = parts[k]
     blocks = {}
     for n, (row, column) in enumerate(UPPER):
@@ -649,6 +651,49 @@
         [((128 * len(UPPER), 128), f32), ((D, D), f32), (own.shape, f32)],
         flops=10**8, data=1 << 18
     )(scalars, mine, other, own)[0]
+
+
+def first_message_kernel(replica, qkv, out, vectors, message):
+    piece = message.shape[0] - 8
+    width = vectors.shape[1]
+
+    @pl.when(replica[0] < 3)
+    def _():
+        message[:piece, :] = qkv[pl.ds(pl.multiple_of(replica[0] * piece, 8), piece), :]
+
+    @pl.when(replica[0] == 3)
+    def _():
+        message[:piece, :] = out[...]
+
+    message[piece:, :] = jnp.zeros((8, D), f32)
+    message[piece:, :width] = vectors[:8, :]
+    message[piece : piece + 4, width : 2 * width] = vectors[8:, :]
+
+
+def first_message(replica, qkv, out, vectors):
+    return call(
+        first_message_kernel, [((out.shape[0] + 8, D), f32)], flops=10**6, data=1 << 16
+    )(replica, qkv, out, vectors)[0]
+
+
+def hand_out_kernel(scalars, one, two, three, four, *outs):
+    for owner, out in zip((1, 3, 0, 2), outs):
+        at = lax.bitwise_xor(scalars[3], owner)
+        rows = out.shape[0]
+        for j, part in enumerate((one, two, three, four)):
+            base = part.shape[0] - rows if owner == 3 else 0
+
+            @pl.when(at == j)
+            def _(part=part, out=out, base=base, rows=rows):
+                out[...] = part[base : base + rows, :]
+
+
+def hand_out(scalars, parts, cuts):
+    outs = [((rows, D), f32) for rows in cuts]
+    one, two, three, four = call(hand_out_kernel, outs, flops=10**8, data=1 << 18)(
+        scalars, *parts
+    )
+    return one.T, two.T, three.T, four
 
 
 def local(
@@ -690,10 +735,8 @@
     def swap(x):
         return lax.ppermute(x, "group", [(i, i ^ 1) for i in range(group_size)])
 
-    def rotate(x, by):
-        return lax.ppermute(
-            x, "group", [(i, (i + 2 * by) % group_size) for i in range(group_size)]
-        )
+    def hop(x, by):
+        return lax.ppermute(x, "group", [(i, i ^ (2 * by)) for i in range(group_size)])
 
     def cross(x, by):
         return lax.ppermute(x, "replica", [(i, i ^ by) for i in range(replicas)])
@@ -705,7 +748,7 @@
         return lower, x, upper
 
     def along_chips(x):
-        return jnp.stack([x] + [rotate(x, k) for k in range(1, chips)])
+        return jnp.stack([x] + [hop(x, k) for k in range(1, chips)])
 
     width = D // group_size
     piece = 4 * width // replicas
@@ -755,8 +798,10 @@
         block_out, slope, n3, m3, down = mlp(
             scalars, None, middle, cotangent, w_two, vec, vec[8:12].reshape(1, FF)
         )
-        d_middle, d_hi, d_lo, dvec = mlp_back(scalars, middle, cotangent, w_two, vec, slope, m3)
-        second = jnp.concatenate([up_grads(scalars, None, d_hi, d_lo, n3)[0], down], axis=0)
+        d_middle, dvec, up = mlp_back(
+            scalars, None, middle, cotangent, w_two, vec, slope, n3, m3
+        )
+        second = jnp.concatenate([up, down], axis=0)
         d_around = halo(d_middle)
         some, more = (attend_back(scalars, i, 2, d_around, w_one, *saved) for i in (0, 2))
         first, d_hi, d_lo, sums = attend_grads(
@@ -784,10 +829,6 @@
         updates = [x if i == 3 else x.T for i, x in enumerate(updates)]
         return finish(block_out, grad_tokens, grads, new_mom, dvec, updates)
 
-    vec_block = jnp.pad(vectors.T, ((0, 0), (0, 116)))
-    third = width // 3
-    vec_block = jnp.concatenate([vec_block[s * third : (s + 1) * third] for s in range(3)], axis=1)
-    my_first = lax.dynamic_slice_in_dim(first_stack, replica_index * piece, piece, 0)
     my_second = jnp.concatenate(
         [
             lax.dynamic_slice_in_dim(second_stack, (4 * n + replica_index) * piece, piece, 0)
@@ -797,17 +838,15 @@
     )
 
     others = range(1, replicas)
-    start = jnp.concatenate([my_first, vec_block], axis=0)
-    start = [start] + [rotate(start, k) for k in range(1, chips)]
+    start = first_message(replica_index.astype(jnp.int32).reshape(1), w_qkv.T, w_out.T, vectors)
+    start = [start] + [hop(start, k) for k in range(1, chips)]
     first = jnp.concatenate([x[:piece] for x in start], axis=0)
     vec_parts = jnp.concatenate([x[piece:] for x in start], axis=0)
-    first, vec_parts, my_second, lower, upper, scalars = lax.optimization_barrier(
-        (first, vec_parts, my_second, around[0], around[2], scalars)
-    )
-    around = lower, tokens, upper
+    first, vec_parts, scalars = lax.optimization_barrier((first, vec_parts, scalars))
     first_other, vec_other = [swap(first)], swap(vec_parts)
     first = [first] + [cross(first, j) for j in others]
-    second = [my_second] + [rotate(my_second, k) for k in range(1, chips)]
+    first_other[0], my_second = lax.optimization_barrier((first_other[0], my_second))
+    second = [my_second] + [hop(my_second, k) for k in range(1, chips)]
     first[1:], second = lax.optimization_barrier((first[1:], second))
     second = jnp.concatenate(second, axis=0)
     second = [second] + [cross(second, j) for j in others]
@@ -833,13 +872,14 @@
         scalars, shape, middle, cotangent, w_two, vec, bias
     )
     other = swap(send)
-    d_middle, d_hi, d_lo, dvec = mlp_back(scalars, middle, cotangent, w_two, vec, slope, m3)
-    down, d_middle, d_hi = lax.optimization_barrier((join(keep, other), d_middle, d_hi))
+    down_keep = keep
+    d_middle, dvec, *keep, send = mlp_back(
+        scalars, shape, middle, cotangent, w_two, vec, slope, n3, m3
+    )
+    down, d_middle, send = lax.optimization_barrier((join(down_keep, other), d_middle, send))
+    d_around = halo(d_middle)
+    other = swap(send)
     down = exchange(down)
-    d_around = halo(d_middle)
-    *keep, send = up_grads(scalars, shape, d_hi, d_lo, n3)
-    keep, send, d_around = lax.optimization_barrier((keep, send, d_around))
-    other = swap(send)
     some = attend_back(scalars, 0, 2, d_around, w_one, *saved)
     up, some, d_around = lax.optimization_barrier((join(keep, other), some, d_around))
     up = exchange(up)
@@ -849,45 +889,42 @@
     )
     grad_tokens, dvec = token_grads(scalars, d_hi, d_lo, w_one, tokens, d_middle, vec, sums, dvec)
     keep, send, dvec, up, down = lax.optimization_barrier((keep, send, dvec, up, down))
-    first = exchange(join(keep, swap(send)))
-    dvec = dvec + swap(dvec)
-
-    def over_chips(parts, *extra):
-        parts = [
-            jnp.concatenate([sum((x[k] for x in parts[1:]), parts[0][k]), *extra], axis=0)
-            for k in range(chips)
-        ]
-        return sum((rotate(parts[k], k) for k in range(1, chips)), parts[0])
-
-    down_sum, up_sum = over_chips(down), over_chips(up)
-    first_sum = over_chips(first, dvec)
-    sums = jnp.concatenate([first_sum[:piece], up_sum, down_sum, first_sum[piece:]], axis=0)
-    parts = [sums] + [cross(sums, j) for j in others]
-    dvec = sum((x[3 * piece :] for x in parts[1:]), parts[0][3 * piece :])
-    grads, new_mom, own, keep, send = own_gradients(scalars, parts, mom_stack, chips)
+    other, dvec = swap(send), dvec + swap(dvec)
+    first, dvec, up, down = lax.optimization_barrier((join(keep, other), dvec, up, down))
+    first = exchange(first)
+
+    def over_chips(messages):
+        return sum((hop(messages[k], k) for k in range(1, len(messages))), messages[0])
+
+    def rows_for(parts, k):
+        return sum((x[k] for x in parts[1:]), parts[0][k])
+
+    second_sum = over_chips(
+        [jnp.concatenate([rows_for(up, k), rows_for(down, k), dvec], axis=0) for k in range(chips)]
+    )
+    up_sum, down_sum, dvec = (
+        second_sum[:piece], second_sum[piece : 2 * piece], second_sum[2 * piece :]
+    )
+    first_sum = over_chips([rows_for(first, k) for k in range(chips)])
+
+    def for_replica(replica):
+        return jnp.where(replica == 0, up_sum, jnp.where(replica == 2, down_sum, first_sum))
+
+    mine = jnp.concatenate([first_sum, up_sum, down_sum], axis=0)
+    taken = [cross(for_replica(lax.bitwise_xor(replica_index, j)), j) for j in others]
+    own, keep, send = own_gradients(scalars, mine, taken, mom_stack, chips)
     t = keep + swap(send)
-    t = t[0] + sum(rotate(t[k], k) for k in range(1, chips))
+    t = t[0] + sum(hop(t[k], k) for k in range(1, chips))
     gram = along_chips(t)
     update_own = update(scalars, gram, swap(gram), own)
+    mine = jnp.concatenate([mine, dvec], axis=0)
+    parts = [mine] + [cross(mine, j) for j in others]
+    parts, update_own = lax.optimization_barrier((parts, update_own))
     updates = [update_own] + [cross(update_own, j) for j in others]
-
-    def from_replica(owner, rows):
-        at = lax.bitwise_xor(replica_index, owner)
-        return lax.select_n(at, *(x[:rows] for x in updates))
-
-    return finish(
-        block_out,
-        grad_tokens,
-        grads,
-        new_mom,
-        dvec,
-        (
-            from_replica(1, 3 * width).T,
-            from_replica(3, width).T,
-            from_replica(0, 4 * width).T,
-            from_replica(2, 4 * width),
-        ),
-    )
+    dvec = sum((x[3 * piece :] for x in parts[1:]), parts[0][3 * piece :])
+    grads, new_mom = all_gradients(scalars, parts, mom_stack)
+    updates = hand_out(scalars, updates, cuts)
+    return finish(block_out, grad_tokens, grads, new_mom, dvec, updates)
 
 
 def solution(mesh):

time: 231 us -> 223 us (0.965)
  waiting for transfers between devices: 72 us -> 58.9 us
  starting transfers between devices: 69.8 us -> 76.4 us
  Pallas kernels: 73.2 us -> 75.9 us
    ppermute x21 -> x18, waiting for transfers between devices: 27.8 us -> 17.1 us  [hop(): lax.ppermute(x, 'group', [(i, i ^ 2 * by) for i in range(group_size)])]
    ppermute x15, starting transfers between devices: 6.74 us -> 13.9 us  [swap(): return lax.ppermute(x, 'group', [(i, i ^ 1) for i in range(group_size)])]
    ppermute x21 -> x18, starting transfers between devices: 32.1 us -> 27.4 us  [hop(): lax.ppermute(x, 'group', [(i, i ^ 2 * by) for i in range(group_size)])]
    ppermute x21 -> x24, starting transfers between devices: 24.7 us -> 28.4 us  [cross(): return lax.ppermute(x, 'replica', [(i, i ^ by) for i in range(replicas)])]
    ppermute x21 -> x24, waiting for transfers between devices: 36.7 us -> 33.6 us  [cross(): return lax.ppermute(x, 'replica', [(i, i ^ by) for i in range(replicas)])]
    pallas_call x12 -> x14, Pallas kernels: 73.2 us -> 75.9 us  [run(): pl.pallas_call(body, out_shape=[jax.ShapeDtypeStruct(s, t) for s, t in ou...]
  transfers between devices with their start and end apart: 61 -> 61, of which waited for: 29 -> 23; matrix products, arithmetic and copies ran while one was open for 3% -> 3% of each run, Pallas kernels for 19% -> 27%
where the time goes in v1:
time: 223 us
  starting transfers between devices  76.4 us (34%)
  Pallas kernels  75.9 us (34%)
  waiting for transfers between devices  58.9 us (26%)
  local copies, waits for them, and re-layouts  6.63 us (3%)
  other arithmetic  3.19 us (1%)
    pallas_call x14, Pallas kernels, run(): pl.pallas_call(body, out_shape=[jax.ShapeDtypeStruct(s, t) for s, t in ou...  75.9 us
    ppermute x24, waiting for transfers between devices, cross(): return lax.ppermute(x, 'replica', [(i, i ^ by) for i in range(replicas)])  33.6 us
    ppermute x24, starting transfers between devices, cross(): return lax.ppermute(x, 'replica', [(i, i ^ by) for i in range(replicas)])  28.4 us
    ppermute x18, starting transfers between devices, hop(): lax.ppermute(x, 'group', [(i, i ^ 2 * by) for i in range(group_size)])  27.4 us
    ppermute x18, waiting for transfers between devices, hop(): lax.ppermute(x, 'group', [(i, i ^ 2 * by) for i in range(group_size)])  17.1 us
    ppermute x15, starting transfers between devices, swap(): return lax.ppermute(x, 'group', [(i, i ^ 1) for i in range(group_size)])  13.9 us
    ppermute x15, waiting for transfers between devices, swap(): return lax.ppermute(x, 'group', [(i, i ^ 1) for i in range(group_size)])  8.14 us
  transfers between devices with their start and end apart: 61, of which 23 were waited for; matrix products, arithmetic and copies ran while one was open for 3% of the time, Pallas kernels for 27%

profile of v1, /device:TPU:0, one launch (start us, length us, event | category | flops | bytes accessed | tf_op | source)
XLA Modules:
  0.0 223.1 jit_solution(14203103191160209164)
XLA Ops:
  3.3 3.0 %collective-permute-start = (f32[56,384]{1,0:T(8,128)S(1)}, f32[56,384]{1,0:T(8,128)S(1)}, u32[]{:S(2)}, u32[]{:S(2)}) collective-permute-start(f32[56,384]{1,0:T(8,128)S(1)} %shard_map.260), channel_id=1, source_target_pairs={{0,2},{1,3},{2,0},{3,1},{4,6},{5,7},{6,4},{7,5},{8,10},{9,11},{10,... | collective-permute-start | bytes 258056 | tf_op jit(solution)/shard_map/ppermute | solution.py:739
  6.3 2.6 %collective-permute-start.1 = (f32[56,384]{1,0:T(8,128)S(1)}, f32[56,384]{1,0:T(8,128)S(1)}, u32[]{:S(2)}, u32[]{:S(2)}) collective-permute-start(f32[56,384]{1,0:T(8,128)S(1)} %shard_map.260), channel_id=1, source_target_pairs={{0,4},{1,5},{2,6},{3,7},{4,0},{5,1},{6,2},{7,3},{8,12},{9,13},{10,... | collective-permute-start | bytes 258056 | tf_op jit(solution)/shard_map/ppermute | solution.py:739
  11.0 4.8 %collective-permute-done.1 = f32[56,384]{1,0:T(8,128)S(1)} collective-permute-done((f32[56,384]{1,0:T(8,128)S(1)}, f32[56,384]{1,0:T(8,128)S(1)}, u32[]{:S(2)}, u32[]{:S(2)}) %collective-permute-start.1) | collective-permute-done | bytes 86048 | tf_op jit(solution)/shard_map/ppermute | solution.py:739
  16.0 1.6 collective-permute-start.3
  17.5 1.5 collective-permute-start.4
  19.6 1.5 collective-permute-start.7
  21.1 1.6 collective-permute-start.8
  22.7 3.1 %collective-permute-done.3.refs_1_ = f32[192,384]{1,0:T(8,128)S(1)} collective-permute-done((f32[192,384]{1,0:T(8,128)S(1)}, f32[192,384]{1,0:T(8,128)S(1)}, u32[]{:S(2)}, u32[]{:S(2)}) %collective-permute-start.3) | collective-permute-done | bytes 294944 | tf_op jit(solution)/shard_map/ppermute | solution.py:742
  25.9 2.5 %collective-permute-start.9 = (f32[96,384]{1,0:T(8,128)S(1)}, f32[96,384]{1,0:T(8,128)S(1)}, u32[]{:S(2)}, u32[]{:S(2)}) collective-permute-start(f32[96,384]{1,0:T(8,128)S(1)} %pad_maximum_fusion.9), channel_id=1, source_target_pairs={{0,6},{1,7},{2,4},{3,5},{4,2},{5,3},{6,0},{7,1},{8,14},{9,15},{10,... | collective-permute-start | bytes 442376 | tf_op jit(solution)/shard_map/ppermute | solution.py:739
  28.3 4.6 %collective-permute-done.4.refs_2_ = f32[192,384]{1,0:T(8,128)S(1)} collective-permute-done((f32[192,384]{1,0:T(8,128)S(1)}, f32[192,384]{1,0:T(8,128)S(1)}, u32[]{:S(2)}, u32[]{:S(2)}) %collective-permute-start.4) | collective-permute-done | bytes 294944 | tf_op jit(solution)/shard_map/ppermute | solution.py:742
  34.1 1.6 collective-permute-start.12
  35.7 1.5 collective-permute-start.11
  37.8 1.7 collective-permute-start.13
  41.8 5.5 %collective-permute-start.19 = (f32[384,384]{1,0:T(8,128)S(1)}, f32[384,384]{1,0:T(8,128)S(1)}, u32[]{:S(2)}, u32[]{:S(2)}) collective-permute-start(f32[384,384]{1,0:T(8,128)S(1)} %constant_dynamic-update-slice_fusion.refs_0_), channel_id=1, source_target_pairs={{0,1},{1,0},{2,3},{3,2},{4,5},{5,4},{6,7},{7,6},{8,9},{9,8},{10,11... | collective-permute-start | bytes 1769480 | tf_op jit(solution)/shard_map/ppermute | solution.py:736
  47.3 13.6 %shard_map.262 = (bf16[4,6,208,128]{3,2,1,0:T(8,128)(2,1)S(1)}, bf16[4,6,128,208]{3,2,1,0:T(8,128)(2,1)S(1)}, bf16[4,6,208,128]{3,2,1,0:T(8,128)(2,1)S(1)}, bf16...) custom-call(s32[6]{0:T(128)S(1)} %stack.39.scalars, ...), custom_call_target="tpu_custom_call" | custom-call | flops 100000000 | bytes 262144 | tf_op jit(solution)/shard_map/pallas_call | solution.py:43
  60.9 2.9 %collective-permute-done.11.refs_2_ = f32[384,384]{1,0:T(8,128)S(1)} collective-permute-done((f32[384,384]{1,0:T(8,128)S(1)}, f32[384,384]{1,0:T(8,128)S(1)}, u32[]{:S(2)}, u32[]{:S(2)}) %collective-permute-start.11) | collective-permute-done | bytes 589856 | tf_op jit(solution)/shard_map/ppermute | solution.py:742
  63.8 1.9 collective-permute-start.22
  70.2 10.4 %shard_map.264 = (f32[512,384]{1,0:T(8,128)}, f32[512,1536]{1,0:T(8,128)S(1)}, bf16[512,1152]{1,0:T(8,128)(2,1)S(1)}, bf16[512,1152]{1,0:T(8,128)(2,1)S(1)}, f32...) custom-call(s32[6]{0:T(128)S(1)} %stack.39.scalars, ...), custom_call_target="tpu_custom_call" | custom-call | flops 100000000 | bytes 262144 | tf_op jit(solution)/shard_map/pallas_call | solution.py:43
  81.0 8.6 %shard_map.265 = (f32[512,384]{1,0:T(8,128)S(1)}, f32[16,384]{1,0:T(8,128)S(1)}, f32[4,48,384]{2,1,0:T(8,128)S(1)}, f32[4,48,384]{2,1,0:T(8,128)S(1)}, f32[4,48,...) custom-call(s32[6]{0:T(128)S(1)} %stack.39.scalars, ...), custom_call_target="tpu_custom_call" | custom-call | flops 100000000 | bytes 262144 | tf_op jit(solution)/shard_map/pallas_call | solution.py:43
  90.6 2.3 %collective-permute-start.25 = (f32[200,384]{1,0:T(8,128)S(1)}, f32[200,384]{1,0:T(8,128)S(1)}, u32[]{:S(2)}, u32[]{:S(2)}) collective-permute-start(f32[200,384]{1,0:T(8,128)S(1)} %get-tuple-element.268), channel_id=1, source_target_pairs={{0,1},{1,2},{2,3},{3,4},{4,5},{5,6},{6,7},{8,9},{9,10},{10,11},{11... | collective-permute-start | bytes 921608 | tf_op jit(solution)/shard_map/ppermute | solution.py:746
  92.9 1.5 collective-permute-start.26
  94.5 1.5 collective-permute-start.30
  96.0 1.5 collective-permute-start.31
  98.1 5.6 %shard_map.266.some = f32[2,208,1152]{2,1,0:T(8,128)S(1)} custom-call(s32[6]{0:T(128)S(1)} %stack.39.scalars, f32[200,384]{1,0:T(8,128)S(1)} %collective-permute-done.25.lower, f32[512,384]{1,0:T(8,128)S(1)} %get-tuple-element.172.own.d_mid, f32[200,384]{1,0:T(8,128)S(1)} %collective-permute-done.26.upper, bf16[1536,1152]{1,0:T(8,128)(2,1)S(1)} %get-tuple-element.138.w, ...), custom_call_target="tpu_custom_call" | custom-call | flops 100000000 | bytes 262144 | tf_op jit(solution)/shard_map/pallas_call | solution.py:43
  106.0 1.5 collective-permute-start.28
  108.0 5.6 %shard_map.267.more = f32[2,208,1152]{2,1,0:T(8,128)S(1)} custom-call(s32[6]{0:T(128)S(1)} %stack.39.scalars, f32[200,384]{1,0:T(8,128)S(1)} %collective-permute-done.25.lower, f32[512,384]{1,0:T(8,128)S(1)} %get-tuple-element.172.own.d_mid, f32[200,384]{1,0:T(8,128)S(1)} %collective-permute-done.26.upper, bf16[1536,1152]{1,0:T(8,128)(2,1)S(1)} %get-tuple-element.138.w, ...), custom_call_target="tpu_custom_call" | custom-call | flops 100000000 | bytes 262144 | tf_op jit(solution)/shard_map/pallas_call | solution.py:43
  113.7 7.1 %shard_map.268 = (f32[4,48,384]{2,1,0:T(8,128)S(1)}, f32[4,48,384]{2,1,0:T(8,128)S(1)}, f32[4,48,384]{2,1,0:T(8,128)S(1)}, f32[4,48,384]{2,1,0:T(8,128)S(1)}, f3...) custom-call(s32[6]{0:T(128)S(1)} %stack.39.scalars, ...), custom_call_target="tpu_custom_call" | custom-call | flops 100000000 | bytes 262144 | tf_op jit(solution)/shard_map/pallas_call | solution.py:43
  120.8 3.6 %shard_map.269 = (f32[512,384]{1,0:T(8,128)}, f32[16,384]{1,0:T(8,128)S(1)}) custom-call(s32[6]{0:T(128)S(1)} %stack.39.scalars, bf16[512,1152]{1,0:T(8,128)(2,1)S(1)} %get-tuple-element.175.d_hi, bf16[512,1152]{1,0:T(8,128)(2,1)S(1)} %get-tuple-element.176.d_lo, bf16[1536,1152]{1,0:T(8,128)(2,1)S(1)} %get-tuple-element.138.w, f32[512,384]{1,0:T(8,128)S(1)} %copy-done, ...), custom_call_target="tpu_custom_call" | custom-call | flops 100000000 | bytes 262144 | tf_op jit(solution)/shard_map/pallas_call | solution.py:43
  124.5 4.7 %collective-permute-start.33 = (f32[4,4,48,384]{3,2,1,0:T(8,128)}, f32[4,4,48,384]{3,2,1,0:T(8,128)S(1)}, u32[]{:S(2)}, u32[]{:S(2)}) collective-permute-start(f32[4,4,48,384]{3,2,1,0:T(8,128)} %get-tuple-element.195), channel_id=1, source_target_pairs={{0,1},{1,0},{2,3},{3,2},{4,5},{5,4},{6,7},{7,6},{8,9},{9,8},{10,11... | collective-permute-start | bytes 3538952 | tf_op jit(solution)/shard_map/ppermute | solution.py:736
  129.3 2.2 collective-permute-done.34
  135.9 1.6 collective-permute-start.41
  137.6 4.4 %collective-permute-done.35 = f32[4,48,384]{2,1,0:T(8,128)S(1)} collective-permute-done((f32[4,48,384]{2,1,0:T(8,128)S(1)}, f32[4,48,384]{2,1,0:T(8,128)S(1)}, u32[]{:S(2)}, u32[]{:S(2)}) %collective-permute-start.35) | collective-permute-done | bytes 294944 | tf_op jit(solution)/shard_map/ppermute | solution.py:742
  143.1 4.2 %collective-permute-done.36 = f32[4,48,384]{2,1,0:T(8,128)S(1)} collective-permute-done((f32[4,48,384]{2,1,0:T(8,128)S(1)}, f32[4,48,384]{2,1,0:T(8,128)S(1)}, u32[]{:S(2)}, u32[]{:S(2)}) %collective-permute-start.36) | collective-permute-done | bytes 294944 | tf_op jit(solution)/shard_map/ppermute | solution.py:742
  148.7 1.7 collective-permute-start.38
  150.4 2.8 %collective-permute-start.40 = (f32[48,384]{1,0:T(8,128)S(1)}, f32[48,384]{1,0:T(8,128)S(1)}, u32[]{:S(2)}, u32[]{:S(2)}) collective-permute-start(f32[48,384]{1,0:T(8,128)S(1)} %get-tuple-element.241), channel_id=1, source_target_pairs={{0,6},{1,7},{2,4},{3,5},{4,2},{5,3},{6,0},{7,1},{8,14},{9,15},{10,... | collective-permute-start | bytes 221192 | tf_op jit(solution)/shard_map/ppermute | solution.py:739
  153.3 7.2 %collective-permute-done.39 = f32[48,384]{1,0:T(8,128)S(1)} collective-permute-done((f32[48,384]{1,0:T(8,128)S(1)}, f32[48,384]{1,0:T(8,128)S(1)}, u32[]{:S(2)}, u32[]{:S(2)}) %collective-permute-start.39) | collective-permute-done | bytes 73760 | tf_op jit(solution)/shard_map/ppermute | solution.py:739
  166.3 1.7 collective-permute-done.49.refs_2_
  172.7 2.7 %collective-permute-start.53 = (f32[96,128]{1,0:T(8,128)S(1)}, f32[96,128]{1,0:T(8,128)S(1)}, u32[]{:S(2)}, u32[]{:S(2)}) collective-permute-start(f32[96,128]{1,0:T(8,128)S(1)} %get-tuple-element.276), channel_id=1, source_target_pairs={{0,6},{1,7},{2,4},{3,5},{4,2},{5,3},{6,0},{7,1},{8,14},{9,15},{10,... | collective-permute-start | bytes 147464 | tf_op jit(solution)/shard_map/ppermute | solution.py:739
  175.5 3.9 %collective-permute-done.52 = f32[96,128]{1,0:T(8,128)S(1)} collective-permute-done((f32[96,128]{1,0:T(8,128)S(1)}, f32[96,128]{1,0:T(8,128)S(1)}, u32[]{:S(2)}, u32[]{:S(2)}) %collective-permute-start.52) | collective-permute-done | bytes 49184 | tf_op jit(solution)/shard_map/ppermute | solution.py:739
  182.1 1.8 collective-permute-start.56
  183.8 1.6 collective-permute-start.44
  185.9 1.5 collective-permute-start.46
  189.5 15.3 %shard_map.271.one = f32[192,384]{1,0:T(8,128)S(1)} custom-call(s32[6]{0:T(128)S(1)} %stack.39.scalars, f32[4,96,128]{2,1,0:T(8,128)S(1)} %pad_maximum_fusion.8.mine, f32[4,96,128]{2,1,0:T(8,128)S(1)} %collective-permute-done.57.other, f32[192,384]{1,0:T(8,128)S(1)} %get-tuple-element.223.own), custom_call_target="tpu_custom_call" | custom-call | flops 100000000 | bytes 262144 | tf_op jit(solution)/shard_map/pallas_call | solution.py:43
  204.8 1.6 collective-permute-start.58
  206.9 1.5 collective-permute-start.60
  212.4 2.4 %collective-permute-done.58.two = f32[192,384]{1,0:T(8,128)S(1)} collective-permute-done((f32[192,384]{1,0:T(8,128)S(1)}, f32[192,384]{1,0:T(8,128)S(1)}, u32[]{:S(2)}, u32[]{:S(2)}) %collective-permute-start.58) | collective-permute-done | bytes 294944 | tf_op jit(solution)/shard_map/ppermute | solution.py:742
  214.8 6.8 %collective-permute-done.59.three = f32[192,384]{1,0:T(8,128)S(1)} collective-permute-done((f32[192,384]{1,0:T(8,128)S(1)}, f32[192,384]{1,0:T(8,128)S(1)}, u32[]{:S(2)}, u32[]{:S(2)}) %collective-permute-start.59) | collective-permute-done | bytes 294944 | tf_op jit(solution)/shard_map/ppermute | solution.py:742
  221.5 1.6 shard_map.273
  (187 shorter events, 45.3 us)
Async XLA Ops:
  3.3 7.7 %collective-permute-start = (f32[56,384]{1,0:T(8,128)S(1)}, f32[56,384]{1,0:T(8,128)S(1)}, u32[]{:S(2)}, u32[]{:S(2)}) collective-permute-start(f32[56,384]{1,0:T(8,128)S(1)} %shard_map.260), channel_id=1, source_target_pairs={{0,2},{1,3},{2,0},{3,1},{4,6},{5,7},{6,4},{7,5},{8,10},{9,11},{10,... | collective-permute-start | bytes 258056 | tf_op jit(solution)/shard_map/ppermute | solution.py:739
  6.3 9.5 %collective-permute-start.1 = (f32[56,384]{1,0:T(8,128)S(1)}, f32[56,384]{1,0:T(8,128)S(1)}, u32[]{:S(2)}, u32[]{:S(2)}) collective-permute-start(f32[56,384]{1,0:T(8,128)S(1)} %shard_map.260), channel_id=1, source_target_pairs={{0,4},{1,5},{2,6},{3,7},{4,0},{5,1},{6,2},{7,3},{8,12},{9,13},{10,... | collective-permute-start | bytes 258056 | tf_op jit(solution)/shard_map/ppermute | solution.py:739
  8.9 6.9 %collective-permute-start.2 = (f32[56,384]{1,0:T(8,128)S(1)}, f32[56,384]{1,0:T(8,128)S(1)}, u32[]{:S(2)}, u32[]{:S(2)}) collective-permute-start(f32[56,384]{1,0:T(8,128)S(1)} %shard_map.260), channel_id=1, source_target_pairs={{0,6},{1,7},{2,4},{3,5},{4,2},{5,3},{6,0},{7,1},{8,14},{9,15},{10,... | collective-permute-start | bytes 258056 | tf_op jit(solution)/shard_map/ppermute | solution.py:739
  16.0 9.9 %collective-permute-start.3 = (f32[192,384]{1,0:T(8,128)S(1)}, f32[192,384]{1,0:T(8,128)S(1)}, u32[]{:S(2)}, u32[]{:S(2)}) collective-permute-start(f32[192,384]{1,0:T(8,128)S(1)} %pad_maximum_fusion.5.refs_0_), channel_id=1, source_target_pairs={{0,8},{8,0},{16,24},{24,16},{1,9},{9,1},{17,25},{25,17},{2,10},{10... | collective-permute-start | bytes 884744 | tf_op jit(solution)/shard_map/ppermute | solution.py:742
  17.5 15.4 %collective-permute-start.4 = (f32[192,384]{1,0:T(8,128)S(1)}, f32[192,384]{1,0:T(8,128)S(1)}, u32[]{:S(2)}, u32[]{:S(2)}) collective-permute-start(f32[192,384]{1,0:T(8,128)S(1)} %pad_maximum_fusion.5.refs_0_), channel_id=1, source_target_pairs={{0,16},{8,24},{16,0},{24,8},{1,17},{9,25},{17,1},{25,9},{2,18},{10... | collective-permute-start | bytes 884744 | tf_op jit(solution)/shard_map/ppermute | solution.py:742
  19.1 13.9 %collective-permute-start.5 = (f32[192,384]{1,0:T(8,128)S(1)}, f32[192,384]{1,0:T(8,128)S(1)}, u32[]{:S(2)}, u32[]{:S(2)}) collective-permute-start(f32[192,384]{1,0:T(8,128)S(1)} %pad_maximum_fusion.5.refs_0_), channel_id=1, source_target_pairs={{0,24},{8,16},{16,8},{24,0},{1,25},{9,17},{17,9},{25,1},{2,26},{10... | collective-permute-start | bytes 884744 | tf_op jit(solution)/shard_map/ppermute | solution.py:742
  19.6 13.3 %collective-permute-start.7 = (f32[96,384]{1,0:T(8,128)S(1)}, f32[96,384]{1,0:T(8,128)S(1)}, u32[]{:S(2)}, u32[]{:S(2)}) collective-permute-start(f32[96,384]{1,0:T(8,128)S(1)} %pad_maximum_fusion.9), channel_id=1, source_target_pairs={{0,2},{1,3},{2,0},{3,1},{4,6},{5,7},{6,4},{7,5},{8,10},{9,11},{10,... | collective-permute-start | bytes 442376 | tf_op jit(solution)/shard_map/ppermute | solution.py:739
  21.1 12.4 %collective-permute-start.8 = (f32[96,384]{1,0:T(8,128)S(1)}, f32[96,384]{1,0:T(8,128)S(1)}, u32[]{:S(2)}, u32[]{:S(2)}) collective-permute-start(f32[96,384]{1,0:T(8,128)S(1)} %pad_maximum_fusion.9), channel_id=1, source_target_pairs={{0,4},{1,5},{2,6},{3,7},{4,0},{5,1},{6,2},{7,3},{8,12},{9,13},{10,... | collective-permute-start | bytes 442376 | tf_op jit(solution)/shard_map/ppermute | solution.py:739
  25.9 7.7 %collective-permute-start.9 = (f32[96,384]{1,0:T(8,128)S(1)}, f32[96,384]{1,0:T(8,128)S(1)}, u32[]{:S(2)}, u32[]{:S(2)}) collective-permute-start(f32[96,384]{1,0:T(8,128)S(1)} %pad_maximum_fusion.9), channel_id=1, source_target_pairs={{0,6},{1,7},{2,4},{3,5},{4,2},{5,3},{6,0},{7,1},{8,14},{9,15},{10,... | collective-permute-start | bytes 442376 | tf_op jit(solution)/shard_map/ppermute | solution.py:739
  34.1 5.4 %collective-permute-start.17 = (f32[192,384]{1,0:T(8,128)S(1)}, f32[192,384]{1,0:T(8,128)S(1)}, u32[]{:S(2)}, u32[]{:S(2)}) collective-permute-start(f32[192,384]{1,0:T(8,128)S(1)} %collective-permute-done.5.refs_3_), channel_id=1, source_target_pairs={{0,1},{1,0},{2,3},{3,2},{4,5},{5,4},{6,7},{7,6},{8,9},{9,8},{10,11... | collective-permute-start | bytes 884744 | tf_op jit(solution)/shard_map/ppermute | solution.py:736
  34.1 26.7 %collective-permute-start.12 = (f32[384,384]{1,0:T(8,128)S(1)}, f32[384,384]{1,0:T(8,128)S(1)}, u32[]{:S(2)}, u32[]{:S(2)}) collective-permute-start(f32[384,384]{1,0:T(8,128)S(1)} %constant_dynamic-update-slice_fusion.refs_0_), channel_id=1, source_target_pairs={{0,8},{8,0},{16,24},{24,16},{1,9},{9,1},{17,25},{25,17},{2,10},{10... | collective-permute-start | bytes 1769480 | tf_op jit(solution)/shard_map/ppermute | solution.py:742
  35.7 28.1 %collective-permute-start.11 = (f32[384,384]{1,0:T(8,128)S(1)}, f32[384,384]{1,0:T(8,128)S(1)}, u32[]{:S(2)}, u32[]{:S(2)}) collective-permute-start(f32[384,384]{1,0:T(8,128)S(1)} %constant_dynamic-update-slice_fusion.refs_0_), channel_id=1, source_target_pairs={{0,16},{8,24},{16,0},{24,8},{1,17},{9,25},{17,1},{25,9},{2,18},{10... | collective-permute-start | bytes 1769480 | tf_op jit(solution)/shard_map/ppermute | solution.py:742
  37.2 26.6 %collective-permute-start.10 = (f32[384,384]{1,0:T(8,128)S(1)}, f32[384,384]{1,0:T(8,128)S(1)}, u32[]{:S(2)}, u32[]{:S(2)}) collective-permute-start(f32[384,384]{1,0:T(8,128)S(1)} %constant_dynamic-update-slice_fusion.refs_0_), channel_id=1, source_target_pairs={{0,24},{8,16},{16,8},{24,0},{1,25},{9,17},{17,9},{25,1},{2,26},{10... | collective-permute-start | bytes 1769480 | tf_op jit(solution)/shard_map/ppermute | solution.py:742
  39.4 7.9 %collective-permute-start.14 = (f32[200,384]{1,0:T(8,128)S(1)}, f32[200,384]{1,0:T(8,128)S(1)}, u32[]{:S(2)}, u32[]{:S(2)}) collective-permute-start(f32[200,384]{1,0:T(8,128)S(1)} %get-tuple-element.269), channel_id=1, source_target_pairs={{1,0},{2,1},{3,2},{4,3},{5,4},{6,5},{7,6},{9,8},{10,9},{11,10},{12... | collective-permute-start | bytes 921608 | tf_op jit(solution)/shard_map/ppermute | solution.py:747
  41.8 24.4 %collective-permute-start.19 = (f32[384,384]{1,0:T(8,128)S(1)}, f32[384,384]{1,0:T(8,128)S(1)}, u32[]{:S(2)}, u32[]{:S(2)}) collective-permute-start(f32[384,384]{1,0:T(8,128)S(1)} %constant_dynamic-update-slice_fusion.refs_0_), channel_id=1, source_target_pairs={{0,1},{1,0},{2,3},{3,2},{4,5},{5,4},{6,7},{7,6},{8,9},{9,8},{10,11... | collective-permute-start | bytes 1769480 | tf_op jit(solution)/shard_map/ppermute | solution.py:736
  80.6 9.0 %collective-permute-start.23 = (f32[4,4,48,384]{3,2,1,0:T(8,128)S(1)}, f32[4,4,48,384]{3,2,1,0:T(8,128)S(1)}, u32[]{:S(2)}, u32[]{:S(2)}) collective-permute-start(f32[4,4,48,384]{3,2,1,0:T(8,128)S(1)} %get-tuple-element.154), channel_id=1, source_target_pairs={{0,1},{1,0},{2,3},{3,2},{4,5},{5,4},{6,7},{7,6},{8,9},{9,8},{10,11... | collective-permute-start | bytes 3538952 | tf_op jit(solution)/shard_map/ppermute | solution.py:736
  90.4 13.2 %collective-permute-start.24 = (f32[4,4,48,384]{3,2,1,0:T(8,128)S(1)}, f32[4,4,48,384]{3,2,1,0:T(8,128)S(1)}, u32[]{:S(2)}, u32[]{:S(2)}) collective-permute-start(f32[4,4,48,384]{3,2,1,0:T(8,128)S(1)} %get-tuple-element.160), channel_id=1, source_target_pairs={{0,1},{1,0},{2,3},{3,2},{4,5},{5,4},{6,7},{7,6},{8,9},{9,8},{10,11... | collective-permute-start | bytes 3538952 | tf_op jit(solution)/shard_map/ppermute | solution.py:736
  90.6 6.9 %collective-permute-start.25 = (f32[200,384]{1,0:T(8,128)S(1)}, f32[200,384]{1,0:T(8,128)S(1)}, u32[]{:S(2)}, u32[]{:S(2)}) collective-permute-start(f32[200,384]{1,0:T(8,128)S(1)} %get-tuple-element.268), channel_id=1, source_target_pairs={{0,1},{1,2},{2,3},{3,4},{4,5},{5,6},{6,7},{8,9},{9,10},{10,11},{11... | collective-permute-start | bytes 921608 | tf_op jit(solution)/shard_map/ppermute | solution.py:746
  92.9 5.1 %collective-permute-start.26 = (f32[200,384]{1,0:T(8,128)S(1)}, f32[200,384]{1,0:T(8,128)S(1)}, u32[]{:S(2)}, u32[]{:S(2)}) collective-permute-start(f32[200,384]{1,0:T(8,128)S(1)} %get-tuple-element.267), channel_id=1, source_target_pairs={{1,0},{2,1},{3,2},{4,3},{5,4},{6,5},{7,6},{9,8},{10,9},{11,10},{12... | collective-permute-start | bytes 921608 | tf_op jit(solution)/shard_map/ppermute | solution.py:747
  94.5 13.1 %collective-permute-start.30 = (f32[4,48,384]{2,1,0:T(8,128)S(1)}, f32[4,48,384]{2,1,0:T(8,128)S(1)}, u32[]{:S(2)}, u32[]{:S(2)}) collective-permute-start(f32[4,48,384]{2,1,0:T(8,128)S(1)} %get-tuple-element.191), channel_id=1, source_target_pairs={{0,8},{8,0},{16,24},{24,16},{1,9},{9,1},{17,25},{25,17},{2,10},{10... | collective-permute-start | bytes 884744 | tf_op jit(solution)/shard_map/ppermute | solution.py:742
  96.0 28.4 %collective-permute-start.31 = (f32[4,48,384]{2,1,0:T(8,128)S(1)}, f32[4,48,384]{2,1,0:T(8,128)S(1)}, u32[]{:S(2)}, u32[]{:S(2)}) collective-permute-start(f32[4,48,384]{2,1,0:T(8,128)S(1)} %get-tuple-element.192), channel_id=1, source_target_pairs={{0,16},{8,24},{16,0},{24,8},{1,17},{9,25},{17,1},{25,9},{2,18},{10... | collective-permute-start | bytes 884744 | tf_op jit(solution)/shard_map/ppermute | solution.py:742
  97.5 26.9 %collective-permute-start.32 = (f32[4,48,384]{2,1,0:T(8,128)S(1)}, f32[4,48,384]{2,1,0:T(8,128)S(1)}, u32[]{:S(2)}, u32[]{:S(2)}) collective-permute-start(f32[4,48,384]{2,1,0:T(8,128)S(1)} %get-tuple-element.193), channel_id=1, source_target_pairs={{0,24},{8,16},{16,8},{24,0},{1,25},{9,17},{17,9},{25,1},{2,26},{10... | collective-permute-start | bytes 884744 | tf_op jit(solution)/shard_map/ppermute | solution.py:742
  104.6 19.8 %collective-permute-start.27 = (f32[4,48,384]{2,1,0:T(8,128)S(1)}, f32[4,48,384]{2,1,0:T(8,128)S(1)}, u32[]{:S(2)}, u32[]{:S(2)}) collective-permute-start(f32[4,48,384]{2,1,0:T(8,128)S(1)} %get-tuple-element.187), channel_id=1, source_target_pairs={{0,8},{8,0},{16,24},{24,16},{1,9},{9,1},{17,25},{25,17},{2,10},{10... | collective-permute-start | bytes 884744 | tf_op jit(solution)/shard_map/ppermute | solution.py:742
  106.0 18.4 %collective-permute-start.28 = (f32[4,48,384]{2,1,0:T(8,128)S(1)}, f32[4,48,384]{2,1,0:T(8,128)S(1)}, u32[]{:S(2)}, u32[]{:S(2)}) collective-permute-start(f32[4,48,384]{2,1,0:T(8,128)S(1)} %get-tuple-element.188), channel_id=1, source_target_pairs={{0,16},{8,24},{16,0},{24,8},{1,17},{9,25},{17,1},{25,9},{2,18},{10... | collective-permute-start | bytes 884744 | tf_op jit(solution)/shard_map/ppermute | solution.py:742
  107.5 16.9 %collective-permute-start.29 = (f32[4,48,384]{2,1,0:T(8,128)S(1)}, f32[4,48,384]{2,1,0:T(8,128)S(1)}, u32[]{:S(2)}, u32[]{:S(2)}) collective-permute-start(f32[4,48,384]{2,1,0:T(8,128)S(1)} %get-tuple-element.189), channel_id=1, source_target_pairs={{0,24},{8,16},{16,8},{24,0},{1,25},{9,17},{17,9},{25,1},{2,26},{10... | collective-permute-start | bytes 884744 | tf_op jit(solution)/shard_map/ppermute | solution.py:742
  124.5 7.4 %collective-permute-start.33 = (f32[4,4,48,384]{3,2,1,0:T(8,128)}, f32[4,4,48,384]{3,2,1,0:T(8,128)S(1)}, u32[]{:S(2)}, u32[]{:S(2)}) collective-permute-start(f32[4,4,48,384]{3,2,1,0:T(8,128)} %get-tuple-element.195), channel_id=1, source_target_pairs={{0,1},{1,0},{2,3},{3,2},{4,5},{5,4},{6,7},{7,6},{8,9},{9,8},{10,11... | collective-permute-start | bytes 3538952 | tf_op jit(solution)/shard_map/ppermute | solution.py:736
  132.1 9.9 %collective-permute-start.35 = (f32[4,48,384]{2,1,0:T(8,128)S(1)}, f32[4,48,384]{2,1,0:T(8,128)S(1)}, u32[]{:S(2)}, u32[]{:S(2)}) collective-permute-start(f32[4,48,384]{2,1,0:T(8,128)S(1)} %get-tuple-element.209), channel_id=1, source_target_pairs={{0,8},{8,0},{16,24},{24,16},{1,9},{9,1},{17,25},{25,17},{2,10},{10... | collective-permute-start | bytes 884744 | tf_op jit(solution)/shard_map/ppermute | solution.py:742
  133.4 13.9 %collective-permute-start.36 = (f32[4,48,384]{2,1,0:T(8,128)S(1)}, f32[4,48,384]{2,1,0:T(8,128)S(1)}, u32[]{:S(2)}, u32[]{:S(2)}) collective-permute-start(f32[4,48,384]{2,1,0:T(8,128)S(1)} %get-tuple-element.210), channel_id=1, source_target_pairs={{0,16},{8,24},{16,0},{24,8},{1,17},{9,25},{17,1},{25,9},{2,18},{10... | collective-permute-start | bytes 884744 | tf_op jit(solution)/shard_map/ppermute | solution.py:742
  134.4 14.2 %collective-permute-start.37 = (f32[4,48,384]{2,1,0:T(8,128)S(1)}, f32[4,48,384]{2,1,0:T(8,128)S(1)}, u32[]{:S(2)}, u32[]{:S(2)}) collective-permute-start(f32[4,48,384]{2,1,0:T(8,128)S(1)} %get-tuple-element.211), channel_id=1, source_target_pairs={{0,24},{8,16},{16,8},{24,0},{1,25},{9,17},{17,9},{25,1},{2,26},{10... | collective-permute-start | bytes 884744 | tf_op jit(solution)/shard_map/ppermute | solution.py:742
  135.9 14.5 %collective-permute-start.41 = (f32[112,384]{1,0:T(8,128)S(1)}, f32[112,384]{1,0:T(8,128)S(1)}, u32[]{:S(2)}, u32[]{:S(2)}) collective-permute-start(f32[112,384]{1,0:T(8,128)S(1)} %get-tuple-element.278), channel_id=1, source_target_pairs={{0,2},{1,3},{2,0},{3,1},{4,6},{5,7},{6,4},{7,5},{8,10},{9,11},{10,... | collective-permute-start | bytes 516104 | tf_op jit(solution)/shard_map/ppermute | solution.py:739
  137.5 15.7 %collective-permute-start.42 = (f32[112,384]{1,0:T(8,128)S(1)}, f32[112,384]{1,0:T(8,128)S(1)}, u32[]{:S(2)}, u32[]{:S(2)}) collective-permute-start(f32[112,384]{1,0:T(8,128)S(1)} %get-tuple-element.279), channel_id=1, source_target_pairs={{0,4},{1,5},{2,6},{3,7},{4,0},{5,1},{6,2},{7,3},{8,12},{9,13},{10,... | collective-permute-start | bytes 516104 | tf_op jit(solution)/shard_map/ppermute | solution.py:739
  142.0 11.2 %collective-permute-start.43 = (f32[112,384]{1,0:T(8,128)S(1)}, f32[112,384]{1,0:T(8,128)S(1)}, u32[]{:S(2)}, u32[]{:S(2)}) collective-permute-start(f32[112,384]{1,0:T(8,128)S(1)} %get-tuple-element.280), channel_id=1, source_target_pairs={{0,6},{1,7},{2,4},{3,5},{4,2},{5,3},{6,0},{7,1},{8,14},{9,15},{10,... | collective-permute-start | bytes 516104 | tf_op jit(solution)/shard_map/ppermute | solution.py:739
  148.7 4.6 %collective-permute-start.38 = (f32[48,384]{1,0:T(8,128)S(1)}, f32[48,384]{1,0:T(8,128)S(1)}, u32[]{:S(2)}, u32[]{:S(2)}) collective-permute-start(f32[48,384]{1,0:T(8,128)S(1)} %get-tuple-element.240), channel_id=1, source_target_pairs={{0,2},{1,3},{2,0},{3,1},{4,6},{5,7},{6,4},{7,5},{8,10},{9,11},{10,... | collective-permute-start | bytes 221192 | tf_op jit(solution)/shard_map/ppermute | solution.py:739
  150.4 10.1 %collective-permute-start.39 = (f32[48,384]{1,0:T(8,128)S(1)}, f32[48,384]{1,0:T(8,128)S(1)}, u32[]{:S(2)}, u32[]{:S(2)}) collective-permute-start(f32[48,384]{1,0:T(8,128)S(1)} %get-tuple-element.242), channel_id=1, source_target_pairs={{0,4},{1,5},{2,6},{3,7},{4,0},{5,1},{6,2},{7,3},{8,12},{9,13},{10,... | collective-permute-start | bytes 221192 | tf_op jit(solution)/shard_map/ppermute | solution.py:739
  150.4 10.1 %collective-permute-start.40 = (f32[48,384]{1,0:T(8,128)S(1)}, f32[48,384]{1,0:T(8,128)S(1)}, u32[]{:S(2)}, u32[]{:S(2)}) collective-permute-start(f32[48,384]{1,0:T(8,128)S(1)} %get-tuple-element.241), channel_id=1, source_target_pairs={{0,6},{1,7},{2,4},{3,5},{4,2},{5,3},{6,0},{7,1},{8,14},{9,15},{10,... | collective-permute-start | bytes 221192 | tf_op jit(solution)/shard_map/ppermute | solution.py:739
  162.7 5.3 %collective-permute-start.49 = (f32[48,384]{1,0:T(8,128)S(1)}, f32[48,384]{1,0:T(8,128)S(1)}, u32[]{:S(2)}, u32[]{:S(2)}) collective-permute-start(f32[48,384]{1,0:T(8,128)S(1)} %get-tuple-element.238), channel_id=1, source_target_pairs={{0,24},{8,16},{16,8},{24,0},{1,25},{9,17},{17,9},{25,1},{2,26},{10... | collective-permute-start | bytes 221192 | tf_op jit(solution)/shard_map/ppermute | solution.py:742
  171.0 4.5 %collective-permute-start.51 = (f32[96,128]{1,0:T(8,128)S(1)}, f32[96,128]{1,0:T(8,128)S(1)}, u32[]{:S(2)}, u32[]{:S(2)}) collective-permute-start(f32[96,128]{1,0:T(8,128)S(1)} %get-tuple-element.277), channel_id=1, source_target_pairs={{0,2},{1,3},{2,0},{3,1},{4,6},{5,7},{6,4},{7,5},{8,10},{9,11},{10,... | collective-permute-start | bytes 147464 | tf_op jit(solution)/shard_map/ppermute | solution.py:739
  172.4 6.9 %collective-permute-start.52 = (f32[96,128]{1,0:T(8,128)S(1)}, f32[96,128]{1,0:T(8,128)S(1)}, u32[]{:S(2)}, u32[]{:S(2)}) collective-permute-start(f32[96,128]{1,0:T(8,128)S(1)} %get-tuple-element.275), channel_id=1, source_target_pairs={{0,4},{1,5},{2,6},{3,7},{4,0},{5,1},{6,2},{7,3},{8,12},{9,13},{10,... | collective-permute-start | bytes 147464 | tf_op jit(solution)/shard_map/ppermute | solution.py:739
  172.7 6.6 %collective-permute-start.53 = (f32[96,128]{1,0:T(8,128)S(1)}, f32[96,128]{1,0:T(8,128)S(1)}, u32[]{:S(2)}, u32[]{:S(2)}) collective-permute-start(f32[96,128]{1,0:T(8,128)S(1)} %get-tuple-element.276), channel_id=1, source_target_pairs={{0,6},{1,7},{2,4},{3,5},{4,2},{5,3},{6,0},{7,1},{8,14},{9,15},{10,... | collective-permute-start | bytes 147464 | tf_op jit(solution)/shard_map/ppermute | solution.py:739
  179.4 6.6 %collective-permute-start.54 = (f32[96,128]{1,0:T(8,128)S(1)}, f32[96,128]{1,0:T(8,128)S(1)}, u32[]{:S(2)}, u32[]{:S(2)}) collective-permute-start(f32[96,128]{1,0:T(8,128)S(1)} %fusion.24), channel_id=1, source_target_pairs={{0,2},{1,3},{2,0},{3,1},{4,6},{5,7},{6,4},{7,5},{8,10},{9,11},{10,... | collective-permute-start | bytes 147464 | tf_op jit(solution)/shard_map/ppermute | solution.py:739
  180.6 6.8 %collective-permute-start.55 = (f32[96,128]{1,0:T(8,128)S(1)}, f32[96,128]{1,0:T(8,128)S(1)}, u32[]{:S(2)}, u32[]{:S(2)}) collective-permute-start(f32[96,128]{1,0:T(8,128)S(1)} %fusion.24), channel_id=1, source_target_pairs={{0,4},{1,5},{2,6},{3,7},{4,0},{5,1},{6,2},{7,3},{8,12},{9,13},{10,... | collective-permute-start | bytes 147464 | tf_op jit(solution)/shard_map/ppermute | solution.py:739
  182.1 5.9 %collective-permute-start.56 = (f32[96,128]{1,0:T(8,128)S(1)}, f32[96,128]{1,0:T(8,128)S(1)}, u32[]{:S(2)}, u32[]{:S(2)}) collective-permute-start(f32[96,128]{1,0:T(8,128)S(1)} %fusion.24), channel_id=1, source_target_pairs={{0,6},{1,7},{2,4},{3,5},{4,2},{5,3},{6,0},{7,1},{8,14},{9,15},{10,... | collective-permute-start | bytes 147464 | tf_op jit(solution)/shard_map/ppermute | solution.py:739
  183.8 21.0 %collective-permute-start.44 = (f32[160,384]{1,0:T(8,128)S(1)}, f32[160,384]{1,0:T(8,128)S(1)}, u32[]{:S(2)}, u32[]{:S(2)}) collective-permute-start(f32[160,384]{1,0:T(8,128)S(1)} %pad_maximum_fusion.6.refs_0_), channel_id=1, source_target_pairs={{0,8},{8,0},{16,24},{24,16},{1,9},{9,1},{17,25},{25,17},{2,10},{10... | collective-permute-start | bytes 737288 | tf_op jit(solution)/shard_map/ppermute | solution.py:742
  185.4 19.4 %collective-permute-start.45 = (f32[160,384]{1,0:T(8,128)S(1)}, f32[160,384]{1,0:T(8,128)S(1)}, u32[]{:S(2)}, u32[]{:S(2)}) collective-permute-start(f32[160,384]{1,0:T(8,128)S(1)} %pad_maximum_fusion.6.refs_0_), channel_id=1, source_target_pairs={{0,16},{8,24},{16,0},{24,8},{1,17},{9,25},{17,1},{25,9},{2,18},{10... | collective-permute-start | bytes 737288 | tf_op jit(solution)/shard_map/ppermute | solution.py:742
  185.9 18.9 %collective-permute-start.46 = (f32[160,384]{1,0:T(8,128)S(1)}, f32[160,384]{1,0:T(8,128)S(1)}, u32[]{:S(2)}, u32[]{:S(2)}) collective-permute-start(f32[160,384]{1,0:T(8,128)S(1)} %pad_maximum_fusion.6.refs_0_), channel_id=1, source_target_pairs={{0,24},{8,16},{16,8},{24,0},{1,25},{9,17},{17,9},{25,1},{2,26},{10... | collective-permute-start | bytes 737288 | tf_op jit(solution)/shard_map/ppermute | solution.py:742
  204.8 9.9 %collective-permute-start.58 = (f32[192,384]{1,0:T(8,128)S(1)}, f32[192,384]{1,0:T(8,128)S(1)}, u32[]{:S(2)}, u32[]{:S(2)}) collective-permute-start(f32[192,384]{1,0:T(8,128)S(1)} %shard_map.271.one), channel_id=1, source_target_pairs={{0,8},{8,0},{16,24},{24,16},{1,9},{9,1},{17,25},{25,17},{2,10},{10... | collective-permute-start | bytes 884744 | tf_op jit(solution)/shard_map/ppermute | solution.py:742
  206.4 15.1 %collective-permute-start.59 = (f32[192,384]{1,0:T(8,128)S(1)}, f32[192,384]{1,0:T(8,128)S(1)}, u32[]{:S(2)}, u32[]{:S(2)}) collective-permute-start(f32[192,384]{1,0:T(8,128)S(1)} %shard_map.271.one), channel_id=1, source_target_pairs={{0,16},{8,24},{16,0},{24,8},{1,17},{9,25},{17,1},{25,9},{2,18},{10... | collective-permute-start | bytes 884744 | tf_op jit(solution)/shard_map/ppermute | solution.py:742
  206.9 14.6 %collective-permute-start.60 = (f32[192,384]{1,0:T(8,128)S(1)}, f32[192,384]{1,0:T(8,128)S(1)}, u32[]{:S(2)}, u32[]{:S(2)}) collective-permute-start(f32[192,384]{1,0:T(8,128)S(1)} %shard_map.271.one), channel_id=1, source_target_pairs={{0,24},{8,16},{16,8},{24,0},{1,25},{9,17},{17,9},{25,1},{2,26},{10... | collective-permute-start | bytes 884744 | tf_op jit(solution)/shard_map/ppermute | solution.py:742
  (39 other events, 205.5 us)

commit v2 on v1

--- a/solution.py
+++ b/solution.py
@@ -104,11 +104,12 @@
     return aligned, start - aligned
 
 
-def fill_window(window, lower, own, upper):
+def fill_window(window, scalars, inside, own, outside):
     rows = own.shape[0]
-    window[:HALO, :] = lower[...]
+    even = scalars[5] == 0
+    window[:HALO, :] = jnp.where(even, outside[...], inside[...])
     window[HALO : HALO + rows, :] = own[...]
-    window[HALO + rows : 2 * HALO + rows, :] = upper[...]
+    window[HALO + rows : 2 * HALO + rows, :] = jnp.where(even, inside[...], outside[...])
     window[2 * HALO + rows :, :] = jnp.zeros((window.shape[0] - 2 * HALO - rows, D), f32)
 
 
@@ -163,7 +164,7 @@
     scalars, lower, own, upper, w, vec, q2, kt2, v2, probs_hi, probs_lo, a3, middle, window, proj, att_win
 ):
     rows = own.shape[0]
-    fill_window(window, lower, own, upper)
+    fill_window(window, scalars, lower, own, upper)
     step = (2 * HALO + rows) // 3
 
     def project_step(t, carry):
@@ -354,7 +355,7 @@
 
 def attend_back_kernel(first_slot, scalars, lower, own, upper, w, q2, kt2, v2, probs_hi, probs_lo, out, window):
     rows = own.shape[0]
-    fill_window(window, lower, own, upper)
+    fill_window(window, scalars, lower, own, upper)
 
     def slot_step(step, carry):
         slot = first_slot + step
@@ -742,10 +743,14 @@
         return lax.ppermute(x, "replica", [(i, i ^ by) for i in range(replicas)])
 
     def halo(x):
-        ends = group_size - 1
-        lower = lax.ppermute(x[tok_rows - HALO :], "group", [(i, i + 1) for i in range(ends)])
-        upper = lax.ppermute(x[:HALO], "group", [(i + 1, i) for i in range(ends)])
-        return lower, x, upper
+        head, tail = x[:HALO], x[tok_rows - HALO :]
+        even = group_index % 2 == 0
+        pairs = [(i, i + 1) for i in range(1, group_size - 1, 2)]
+        inside = swap(jnp.where(even, tail, head))
+        outside = lax.ppermute(
+            jnp.where(even, head, tail), "group", pairs + [(j, i) for i, j in pairs]
+        )
+        return inside, x, outside
 
     def along_chips(x):
         return jnp.stack([x] + [hop(x, k) for k in range(1, chips)])
@@ -829,36 +834,45 @@
         updates = [x if i == 3 else x.T for i, x in enumerate(updates)]
         return finish(block_out, grad_tokens, grads, new_mom, dvec, updates)
 
-    my_second = jnp.concatenate(
-        [
-            lax.dynamic_slice_in_dim(second_stack, (4 * n + replica_index) * piece, piece, 0)
-            for n in range(2)
-        ],
-        axis=0,
-    )
-
+    def second_quarter(quarter):
+        return jnp.concatenate(
+            [
+                lax.dynamic_slice_in_dim(second_stack, (4 * n + quarter) * piece, piece, 0)
+                for n in range(2)
+            ],
+            axis=0,
+        )
+
+    my_second = second_quarter(replica_index)
+    diagonal = second_quarter(lax.bitwise_xor(replica_index, 3))
     others = range(1, replicas)
     start = first_message(replica_index.astype(jnp.int32).reshape(1), w_qkv.T, w_out.T, vectors)
     start = [start] + [hop(start, k) for k in range(1, chips)]
     first = jnp.concatenate([x[:piece] for x in start], axis=0)
     vec_parts = jnp.concatenate([x[piece:] for x in start], axis=0)
-    first, vec_parts, scalars = lax.optimization_barrier((first, vec_parts, scalars))
+    first, vec_parts, scalars, lower, upper = lax.optimization_barrier(
+        (first, vec_parts, scalars, around[0], around[2])
+    )
+    around = lower, tokens, upper
     first_other, vec_other = [swap(first)], swap(vec_parts)
     first = [first] + [cross(first, j) for j in others]
-    first_other[0], my_second = lax.optimization_barrier((first_other[0], my_second))
+    first_other[0], vec_other, my_second = lax.optimization_barrier(
+        (first_other[0], vec_other, my_second)
+    )
     second = [my_second] + [hop(my_second, k) for k in range(1, chips)]
     first[1:], second = lax.optimization_barrier((first[1:], second))
     second = jnp.concatenate(second, axis=0)
-    second = [second] + [cross(second, j) for j in others]
-    second_other = [swap(second[0])]
     first_other += [swap(first[j]) for j in others]
+    diagonal, second, first_other = lax.optimization_barrier((diagonal, second, first_other))
+    diagonal = [diagonal] + [hop(diagonal, k) for k in range(1, chips)]
+    second = [second, cross(second, 1), cross(second, 2)]
     w_one, vec, bias = unpack(
         scalars, chips, first, first_other, first_rows, vec_parts, vec_other
     )
     *saved, a3, middle = attend(scalars, *around, w_one, vec)
-    for j in others:
-        second[j], middle = lax.optimization_barrier((second[j], middle))
-        second_other.append(swap(second[j]))
+    second[1:], diagonal, middle = lax.optimization_barrier((second[1:], diagonal, middle))
+    second.append(jnp.concatenate(diagonal, axis=0))
+    second_other = [swap(x) for x in second]
     w_two = unpack(scalars, chips, second, second_other, second_rows)[0]
     shape = (chips, piece, D)
 

time: 223 us -> 219 us (0.982)
  waiting for transfers between devices: 58.9 us -> 54.4 us
  other arithmetic: 3.19 us -> 5.72 us
    ppermute x24 -> x23, waiting for transfers between devices: 33.6 us -> 22.5 us  [cross(): return lax.ppermute(x, 'replica', [(i, i ^ by) for i in range(replicas)])]
    ppermute x18 -> x21, starting transfers between devices: 27.4 us -> 38 us  [hop(): lax.ppermute(x, 'group', [(i, i ^ 2 * by) for i in range(group_size)])]
    ppermute x4 -> x2, starting transfers between devices: 6.77 us -> 1.35 us  [halo(): lax.ppermute(jnp.where(even, head, tail), 'group', pairs + [(j, i) for i,...]
    ppermute x15 -> x17, starting transfers between devices: 13.9 us -> 9.37 us  [swap(): return lax.ppermute(x, 'group', [(i, i ^ 1) for i in range(group_size)])]
    ppermute x15 -> x17, waiting for transfers between devices: 8.14 us -> 12.5 us  [swap(): return lax.ppermute(x, 'group', [(i, i ^ 1) for i in range(group_size)])]
    ppermute x18 -> x21, waiting for transfers between devices: 17.1 us -> 19.4 us  [hop(): lax.ppermute(x, 'group', [(i, i ^ 2 * by) for i in range(group_size)])]
    ppermute x24 -> x23, starting transfers between devices: 28.4 us -> 26.9 us  [cross(): return lax.ppermute(x, 'replica', [(i, i ^ by) for i in range(replicas)])]
  transfers between devices with their start and end apart: 61 -> 63, of which waited for: 23 -> 29; matrix products, arithmetic and copies ran while one was open for 3% -> 3% of each run, Pallas kernels for 27% -> 28%
where the time goes in v2:
time: 219 us
  starting transfers between devices  75.6 us (35%)
  Pallas kernels  75.1 us (34%)
  waiting for transfers between devices  54.4 us (25%)
  local copies, waits for them, and re-layouts  5.94 us (3%)
  other arithmetic  5.72 us (3%)
  between operations  2.25 us (1%)
    pallas_call x14, Pallas kernels, run(): pl.pallas_call(body, out_shape=[jax.ShapeDtypeStruct(s, t) for s, t in ou...  75.1 us
    ppermute x21, starting transfers between devices, hop(): lax.ppermute(x, 'group', [(i, i ^ 2 * by) for i in range(group_size)])  38 us
    ppermute x23, starting transfers between devices, cross(): return lax.ppermute(x, 'replica', [(i, i ^ by) for i in range(replicas)])  26.9 us
    ppermute x23, waiting for transfers between devices, cross(): return lax.ppermute(x, 'replica', [(i, i ^ by) for i in range(replicas)])  22.5 us
    ppermute x21, waiting for transfers between devices, hop(): lax.ppermute(x, 'group', [(i, i ^ 2 * by) for i in range(group_size)])  19.4 us
    ppermute x17, waiting for transfers between devices, swap(): return lax.ppermute(x, 'group', [(i, i ^ 1) for i in range(group_size)])  12.5 us
    ppermute x17, starting transfers between devices, swap(): return lax.ppermute(x, 'group', [(i, i ^ 1) for i in range(group_size)])  9.37 us
  transfers between devices with their start and end apart: 63, of which 29 were waited for; matrix products, arithmetic and copies ran while one was open for 3% of the time, Pallas kernels for 28%

profile of v2, /device:TPU:0, one launch (start us, length us, event | category | flops | bytes accessed | tf_op | source)
XLA Modules:
  0.0 218.9 jit_solution(7279941788780451291)
XLA Ops:
  3.3 3.0 %collective-permute-start = (f32[56,384]{1,0:T(8,128)S(1)}, f32[56,384]{1,0:T(8,128)S(1)}, u32[]{:S(2)}, u32[]{:S(2)}) collective-permute-start(f32[56,384]{1,0:T(8,128)S(1)} %shard_map.260), channel_id=1, source_target_pairs={{0,2},{1,3},{2,0},{3,1},{4,6},{5,7},{6,4},{7,5},{8,10},{9,11},{10,... | collective-permute-start | bytes 258056 | tf_op jit(solution)/shard_map/ppermute | solution.py:740
  6.3 2.6 %collective-permute-start.1 = (f32[56,384]{1,0:T(8,128)S(1)}, f32[56,384]{1,0:T(8,128)S(1)}, u32[]{:S(2)}, u32[]{:S(2)}) collective-permute-start(f32[56,384]{1,0:T(8,128)S(1)} %shard_map.260), channel_id=1, source_target_pairs={{0,4},{1,5},{2,6},{3,7},{4,0},{5,1},{6,2},{7,3},{8,12},{9,13},{10,... | collective-permute-start | bytes 258056 | tf_op jit(solution)/shard_map/ppermute | solution.py:740
  12.3 3.6 %collective-permute-done.1 = f32[56,384]{1,0:T(8,128)S(1)} collective-permute-done((f32[56,384]{1,0:T(8,128)S(1)}, f32[56,384]{1,0:T(8,128)S(1)}, u32[]{:S(2)}, u32[]{:S(2)}) %collective-permute-start.1) | collective-permute-done | bytes 86048 | tf_op jit(solution)/shard_map/ppermute | solution.py:740
  16.0 2.9 %collective-permute-start.8 = (f32[192,384]{1,0:T(8,128)S(1)}, f32[192,384]{1,0:T(8,128)S(1)}, u32[]{:S(2)}, u32[]{:S(2)}) collective-permute-start(f32[192,384]{1,0:T(8,128)S(1)} %pad_maximum_fusion.6.refs_0_), channel_id=1, source_target_pairs={{0,1},{1,0},{2,3},{3,2},{4,5},{5,4},{6,7},{7,6},{8,9},{9,8},{10,11... | collective-permute-start | bytes 884744 | tf_op jit(solution)/shard_map/ppermute | solution.py:737
  18.9 1.6 collective-permute-start.5
  20.5 1.5 collective-permute-start.6
  23.8 1.5 collective-permute-start.10
  25.3 2.3 %collective-permute-start.11 = (f32[96,384]{1,0:T(8,128)S(1)}, f32[96,384]{1,0:T(8,128)S(1)}, u32[]{:S(2)}, u32[]{:S(2)}) collective-permute-start(f32[96,384]{1,0:T(8,128)S(1)} %pad_maximum_fusion.11), channel_id=1, source_target_pairs={{0,4},{1,5},{2,6},{3,7},{4,0},{5,1},{6,2},{7,3},{8,12},{9,13},{10,... | collective-permute-start | bytes 442376 | tf_op jit(solution)/shard_map/ppermute | solution.py:740
  28.8 3.2 %collective-permute-start.12 = (f32[96,384]{1,0:T(8,128)S(1)}, f32[96,384]{1,0:T(8,128)S(1)}, u32[]{:S(2)}, u32[]{:S(2)}) collective-permute-start(f32[96,384]{1,0:T(8,128)S(1)} %pad_maximum_fusion.11), channel_id=1, source_target_pairs={{0,6},{1,7},{2,4},{3,5},{4,2},{5,3},{6,0},{7,1},{8,14},{9,15},{10,... | collective-permute-start | bytes 442376 | tf_op jit(solution)/shard_map/ppermute | solution.py:740
  31.9 3.5 %collective-permute-done.6.refs_2_ = f32[192,384]{1,0:T(8,128)S(1)} collective-permute-done((f32[192,384]{1,0:T(8,128)S(1)}, f32[192,384]{1,0:T(8,128)S(1)}, u32[]{:S(2)}, u32[]{:S(2)}) %collective-permute-start.6) | collective-permute-done | bytes 294944 | tf_op jit(solution)/shard_map/ppermute | solution.py:743
  35.5 3.2 %collective-permute-done.11 = f32[96,384]{1,0:T(8,128)S(1)} collective-permute-done((f32[96,384]{1,0:T(8,128)S(1)}, f32[96,384]{1,0:T(8,128)S(1)}, u32[]{:S(2)}, u32[]{:S(2)}) %collective-permute-start.11) | collective-permute-done | bytes 147488 | tf_op jit(solution)/shard_map/ppermute | solution.py:740
  41.1 1.5 collective-permute-start.16
  42.6 1.5 collective-permute-start.17
  44.1 3.2 %collective-permute-start.18 = (f32[96,384]{1,0:T(8,128)S(1)}, f32[96,384]{1,0:T(8,128)S(1)}, u32[]{:S(2)}, u32[]{:S(2)}) collective-permute-start(f32[96,384]{1,0:T(8,128)S(1)} %pad_maximum_fusion.10), channel_id=1, source_target_pairs={{0,2},{1,3},{2,0},{3,1},{4,6},{5,7},{6,4},{7,5},{8,10},{9,11},{10,... | collective-permute-start | bytes 442376 | tf_op jit(solution)/shard_map/ppermute | solution.py:740
  48.5 1.5 collective-permute-start.20
  51.0 13.6 %shard_map.262 = (bf16[4,6,208,128]{3,2,1,0:T(8,128)(2,1)S(1)}, bf16[4,6,128,208]{3,2,1,0:T(8,128)(2,1)S(1)}, bf16[4,6,208,128]{3,2,1,0:T(8,128)(2,1)S(1)}, bf16...) custom-call(s32[6]{0:T(128)S(1)} %stack.39.scalars, ...), custom_call_target="tpu_custom_call" | custom-call | flops 100000000 | bytes 262144 | tf_op jit(solution)/shard_map/pallas_call | solution.py:43
  70.4 10.4 %shard_map.264 = (f32[512,384]{1,0:T(8,128)}, f32[512,1536]{1,0:T(8,128)S(1)}, bf16[512,1152]{1,0:T(8,128)(2,1)S(1)}, bf16[512,1152]{1,0:T(8,128)(2,1)S(1)}, f32...) custom-call(s32[6]{0:T(128)S(1)} %stack.39.scalars, ...), custom_call_target="tpu_custom_call" | custom-call | flops 100000000 | bytes 262144 | tf_op jit(solution)/shard_map/pallas_call | solution.py:43
  80.9 8.7 %shard_map.265 = (f32[512,384]{1,0:T(8,128)S(1)}, f32[16,384]{1,0:T(8,128)S(1)}, f32[4,48,384]{2,1,0:T(8,128)S(1)}, f32[4,48,384]{2,1,0:T(8,128)S(1)}, f32[4,48,...) custom-call(s32[6]{0:T(128)S(1)} %stack.39.scalars, ...), custom_call_target="tpu_custom_call" | custom-call | flops 100000000 | bytes 262144 | tf_op jit(solution)/shard_map/pallas_call | solution.py:43
  93.8 1.6 collective-permute-start.34
  95.3 5.6 %shard_map.266.some = f32[2,208,1152]{2,1,0:T(8,128)S(1)} custom-call(s32[6]{0:T(128)S(1)} %stack.39.scalars, f32[200,384]{1,0:T(8,128)S(1)} %collective-permute-done.27.lower, f32[512,384]{1,0:T(8,128)S(1)} %get-tuple-element.192.own.d_mid, f32[200,384]{1,0:T(8,128)S(1)} %collective-permute-done.28.upper, bf16[1536,1152]{1,0:T(8,128)(2,1)S(1)} %get-tuple-element.157.w, ...), custom_call_target="tpu_custom_call" | custom-call | flops 100000000 | bytes 262144 | tf_op jit(solution)/shard_map/pallas_call | solution.py:43
  103.8 1.5 collective-permute-start.31
  105.3 5.6 %shard_map.267.more = f32[2,208,1152]{2,1,0:T(8,128)S(1)} custom-call(s32[6]{0:T(128)S(1)} %stack.39.scalars, f32[200,384]{1,0:T(8,128)S(1)} %collective-permute-done.27.lower, f32[512,384]{1,0:T(8,128)S(1)} %get-tuple-element.192.own.d_mid, f32[200,384]{1,0:T(8,128)S(1)} %collective-permute-done.28.upper, bf16[1536,1152]{1,0:T(8,128)(2,1)S(1)} %get-tuple-element.157.w, ...), custom_call_target="tpu_custom_call" | custom-call | flops 100000000 | bytes 262144 | tf_op jit(solution)/shard_map/pallas_call | solution.py:43
  111.0 6.1 %shard_map.268 = (f32[4,48,384]{2,1,0:T(8,128)S(1)}, f32[4,48,384]{2,1,0:T(8,128)S(1)}, f32[4,48,384]{2,1,0:T(8,128)S(1)}, f32[4,48,384]{2,1,0:T(8,128)S(1)}, f3...) custom-call(s32[6]{0:T(128)S(1)} %stack.39.scalars, ...), custom_call_target="tpu_custom_call" | custom-call | flops 100000000 | bytes 262144 | tf_op jit(solution)/shard_map/pallas_call | solution.py:43
  117.2 3.6 %shard_map.269 = (f32[512,384]{1,0:T(8,128)}, f32[16,384]{1,0:T(8,128)S(1)}) custom-call(s32[6]{0:T(128)S(1)} %stack.39.scalars, bf16[512,1152]{1,0:T(8,128)(2,1)S(1)} %get-tuple-element.195.d_hi, bf16[512,1152]{1,0:T(8,128)(2,1)S(1)} %get-tuple-element.196.d_lo, bf16[1536,1152]{1,0:T(8,128)(2,1)S(1)} %get-tuple-element.157.w, f32[512,384]{1,0:T(8,128)S(1)} %copy-done, ...), custom_call_target="tpu_custom_call" | custom-call | flops 100000000 | bytes 262144 | tf_op jit(solution)/shard_map/pallas_call | solution.py:43
  120.8 3.8 %collective-permute-start.35 = (f32[4,4,48,384]{3,2,1,0:T(8,128)S(1)}, f32[4,4,48,384]{3,2,1,0:T(8,128)}, u32[]{:S(2)}, u32[]{:S(2)}) collective-permute-start(f32[4,4,48,384]{3,2,1,0:T(8,128)S(1)} %get-tuple-element.215), channel_id=1, source_target_pairs={{0,1},{1,0},{2,3},{3,2},{4,5},{5,4},{6,7},{7,6},{8,9},{9,8},{10,11... | collective-permute-start | bytes 3538952 | tf_op jit(solution)/shard_map/ppermute | solution.py:737
  124.9 2.1 collective-permute-done.36
  129.9 2.5 %collective-permute-start.39 = (f32[4,48,384]{2,1,0:T(8,128)S(1)}, f32[4,48,384]{2,1,0:T(8,128)S(1)}, u32[]{:S(2)}, u32[]{:S(2)}) collective-permute-start(f32[4,48,384]{2,1,0:T(8,128)S(1)} %get-tuple-element.231), channel_id=1, source_target_pairs={{0,24},{8,16},{16,8},{24,0},{1,25},{9,17},{17,9},{25,1},{2,26},{10... | collective-permute-start | bytes 884744 | tf_op jit(solution)/shard_map/ppermute | solution.py:743
  134.0 2.0 collective-permute-start.44
  136.0 2.7 %collective-permute-done.37 = f32[4,48,384]{2,1,0:T(8,128)S(1)} collective-permute-done((f32[4,48,384]{2,1,0:T(8,128)S(1)}, f32[4,48,384]{2,1,0:T(8,128)S(1)}, u32[]{:S(2)}, u32[]{:S(2)}) %collective-permute-start.37) | collective-permute-done | bytes 294944 | tf_op jit(solution)/shard_map/ppermute | solution.py:743
  138.7 2.8 %collective-permute-start.45 = (f32[112,384]{1,0:T(8,128)S(1)}, f32[112,384]{1,0:T(8,128)S(1)}, u32[]{:S(2)}, u32[]{:S(2)}) collective-permute-start(f32[112,384]{1,0:T(8,128)S(1)} %get-tuple-element.302), channel_id=1, source_target_pairs={{0,6},{1,7},{2,4},{3,5},{4,2},{5,3},{6,0},{7,1},{8,14},{9,15},{10,... | collective-permute-start | bytes 516104 | tf_op jit(solution)/shard_map/ppermute | solution.py:740
  141.4 3.1 %collective-permute-done.38 = f32[4,48,384]{2,1,0:T(8,128)S(1)} collective-permute-done((f32[4,48,384]{2,1,0:T(8,128)S(1)}, f32[4,48,384]{2,1,0:T(8,128)S(1)}, u32[]{:S(2)}, u32[]{:S(2)}) %collective-permute-start.38) | collective-permute-done | bytes 294944 | tf_op jit(solution)/shard_map/ppermute | solution.py:743
  146.0 2.0 collective-permute-start.41
  149.5 7.1 %collective-permute-done.41 = f32[48,384]{1,0:T(8,128)S(1)} collective-permute-done((f32[48,384]{1,0:T(8,128)S(1)}, f32[48,384]{1,0:T(8,128)S(1)}, u32[]{:S(2)}, u32[]{:S(2)}) %collective-permute-start.41) | collective-permute-done | bytes 73760 | tf_op jit(solution)/shard_map/ppermute | solution.py:740
  157.8 2.5 %collective-permute-start.51 = (f32[48,384]{1,0:T(8,128)S(1)}, f32[48,384]{1,0:T(8,128)S(1)}, u32[]{:S(2)}, u32[]{:S(2)}) collective-permute-start(f32[48,384]{1,0:T(8,128)S(1)} %get-tuple-element.258), channel_id=1, source_target_pairs={{0,24},{8,16},{16,8},{24,0},{1,25},{9,17},{17,9},{25,1},{2,26},{10... | collective-permute-start | bytes 221192 | tf_op jit(solution)/shard_map/ppermute | solution.py:743
  163.1 1.5 shard_map.270
  166.1 1.6 collective-permute-start.53
  167.8 1.8 collective-permute-start.54
  170.6 3.6 %collective-permute-done.54 = f32[96,128]{1,0:T(8,128)S(1)} collective-permute-done((f32[96,128]{1,0:T(8,128)S(1)}, f32[96,128]{1,0:T(8,128)S(1)}, u32[]{:S(2)}, u32[]{:S(2)}) %collective-permute-start.54) | collective-permute-done | bytes 49184 | tf_op jit(solution)/shard_map/ppermute | solution.py:740
  175.6 2.3 %collective-permute-start.57 = (f32[96,128]{1,0:T(8,128)S(1)}, f32[96,128]{1,0:T(8,128)S(1)}, u32[]{:S(2)}, u32[]{:S(2)}) collective-permute-start(f32[96,128]{1,0:T(8,128)S(1)} %fusion.26), channel_id=1, source_target_pairs={{0,4},{1,5},{2,6},{3,7},{4,0},{5,1},{6,2},{7,3},{8,12},{9,13},{10,... | collective-permute-start | bytes 147464 | tf_op jit(solution)/shard_map/ppermute | solution.py:740
  177.9 2.0 collective-permute-start.58
  180.0 1.6 collective-permute-start.46
  181.5 1.5 collective-permute-start.47
  185.3 15.4 %shard_map.271.one = f32[192,384]{1,0:T(8,128)S(1)} custom-call(s32[6]{0:T(128)S(1)} %stack.39.scalars, f32[4,96,128]{2,1,0:T(8,128)S(1)} %pad_maximum_fusion.9.mine, f32[4,96,128]{2,1,0:T(8,128)S(1)} %collective-permute-done.59.other, f32[192,384]{1,0:T(8,128)S(1)} %get-tuple-element.243.own), custom_call_target="tpu_custom_call" | custom-call | flops 100000000 | bytes 262144 | tf_op jit(solution)/shard_map/pallas_call | solution.py:43
  200.7 1.6 collective-permute-start.60
  202.3 1.5 collective-permute-start.61
  208.2 2.4 %collective-permute-done.60.two = f32[192,384]{1,0:T(8,128)S(1)} collective-permute-done((f32[192,384]{1,0:T(8,128)S(1)}, f32[192,384]{1,0:T(8,128)S(1)}, u32[]{:S(2)}, u32[]{:S(2)}) %collective-permute-start.60) | collective-permute-done | bytes 294944 | tf_op jit(solution)/shard_map/ppermute | solution.py:743
  210.6 6.7 %collective-permute-done.61.three = f32[192,384]{1,0:T(8,128)S(1)} collective-permute-done((f32[192,384]{1,0:T(8,128)S(1)}, f32[192,384]{1,0:T(8,128)S(1)}, u32[]{:S(2)}, u32[]{:S(2)}) %collective-permute-start.61) | collective-permute-done | bytes 294944 | tf_op jit(solution)/shard_map/ppermute | solution.py:743
  217.3 1.6 shard_map.273
  (207 shorter events, 47.7 us)
Async XLA Ops:
  3.3 9.0 %collective-permute-start = (f32[56,384]{1,0:T(8,128)S(1)}, f32[56,384]{1,0:T(8,128)S(1)}, u32[]{:S(2)}, u32[]{:S(2)}) collective-permute-start(f32[56,384]{1,0:T(8,128)S(1)} %shard_map.260), channel_id=1, source_target_pairs={{0,2},{1,3},{2,0},{3,1},{4,6},{5,7},{6,4},{7,5},{8,10},{9,11},{10,... | collective-permute-start | bytes 258056 | tf_op jit(solution)/shard_map/ppermute | solution.py:740
  6.3 9.6 %collective-permute-start.1 = (f32[56,384]{1,0:T(8,128)S(1)}, f32[56,384]{1,0:T(8,128)S(1)}, u32[]{:S(2)}, u32[]{:S(2)}) collective-permute-start(f32[56,384]{1,0:T(8,128)S(1)} %shard_map.260), channel_id=1, source_target_pairs={{0,4},{1,5},{2,6},{3,7},{4,0},{5,1},{6,2},{7,3},{8,12},{9,13},{10,... | collective-permute-start | bytes 258056 | tf_op jit(solution)/shard_map/ppermute | solution.py:740
  8.9 7.0 %collective-permute-start.2 = (f32[56,384]{1,0:T(8,128)S(1)}, f32[56,384]{1,0:T(8,128)S(1)}, u32[]{:S(2)}, u32[]{:S(2)}) collective-permute-start(f32[56,384]{1,0:T(8,128)S(1)} %shard_map.260), channel_id=1, source_target_pairs={{0,6},{1,7},{2,4},{3,5},{4,2},{5,3},{6,0},{7,1},{8,14},{9,15},{10,... | collective-permute-start | bytes 258056 | tf_op jit(solution)/shard_map/ppermute | solution.py:740
  10.1 5.9 %collective-permute-start.3 = (f32[200,384]{1,0:T(8,128)S(1)}, f32[200,384]{1,0:T(8,128)S(1)}, u32[]{:S(2)}, u32[]{:S(2)}) collective-permute-start(f32[200,384]{1,0:T(8,128)S(1)} %get-tuple-element.290), channel_id=1, source_target_pairs={{0,1},{1,0},{2,3},{3,2},{4,5},{5,4},{6,7},{7,6},{8,9},{9,8},{10,11... | collective-permute-start | bytes 921608 | tf_op jit(solution)/shard_map/ppermute | solution.py:737
  10.1 5.9 %collective-permute-start.4 = (f32[200,384]{1,0:T(8,128)S(1)}, f32[200,384]{1,0:T(8,128)S(1)}, u32[]{:S(2)}, u32[]{:S(2)}) collective-permute-start(f32[200,384]{1,0:T(8,128)S(1)} %get-tuple-element.289), channel_id=1, source_target_pairs={{1,2},{3,4},{5,6},{2,1},{4,3},{6,5},{9,10},{11,12},{13,14},{10,9},... | collective-permute-start | bytes 921608 | tf_op jit(solution)/shard_map/ppermute | solution.py:750
  16.0 7.7 %collective-permute-start.8 = (f32[192,384]{1,0:T(8,128)S(1)}, f32[192,384]{1,0:T(8,128)S(1)}, u32[]{:S(2)}, u32[]{:S(2)}) collective-permute-start(f32[192,384]{1,0:T(8,128)S(1)} %pad_maximum_fusion.6.refs_0_), channel_id=1, source_target_pairs={{0,1},{1,0},{2,3},{3,2},{4,5},{5,4},{6,7},{7,6},{8,9},{9,8},{10,11... | collective-permute-start | bytes 884744 | tf_op jit(solution)/shard_map/ppermute | solution.py:737
  18.9 9.9 %collective-permute-start.5 = (f32[192,384]{1,0:T(8,128)S(1)}, f32[192,384]{1,0:T(8,128)S(1)}, u32[]{:S(2)}, u32[]{:S(2)}) collective-permute-start(f32[192,384]{1,0:T(8,128)S(1)} %pad_maximum_fusion.6.refs_0_), channel_id=1, source_target_pairs={{0,8},{8,0},{16,24},{24,16},{1,9},{9,1},{17,25},{25,17},{2,10},{10... | collective-permute-start | bytes 884744 | tf_op jit(solution)/shard_map/ppermute | solution.py:743
  20.5 15.0 %collective-permute-start.6 = (f32[192,384]{1,0:T(8,128)S(1)}, f32[192,384]{1,0:T(8,128)S(1)}, u32[]{:S(2)}, u32[]{:S(2)}) collective-permute-start(f32[192,384]{1,0:T(8,128)S(1)} %pad_maximum_fusion.6.refs_0_), channel_id=1, source_target_pairs={{0,16},{8,24},{16,0},{24,8},{1,17},{9,25},{17,1},{25,9},{2,18},{10... | collective-permute-start | bytes 884744 | tf_op jit(solution)/shard_map/ppermute | solution.py:743
  22.0 13.4 %collective-permute-start.7 = (f32[192,384]{1,0:T(8,128)S(1)}, f32[192,384]{1,0:T(8,128)S(1)}, u32[]{:S(2)}, u32[]{:S(2)}) collective-permute-start(f32[192,384]{1,0:T(8,128)S(1)} %pad_maximum_fusion.6.refs_0_), channel_id=1, source_target_pairs={{0,24},{8,16},{16,8},{24,0},{1,25},{9,17},{17,9},{25,1},{2,26},{10... | collective-permute-start | bytes 884744 | tf_op jit(solution)/shard_map/ppermute | solution.py:743
  23.8 11.7 %collective-permute-start.10 = (f32[96,384]{1,0:T(8,128)S(1)}, f32[96,384]{1,0:T(8,128)S(1)}, u32[]{:S(2)}, u32[]{:S(2)}) collective-permute-start(f32[96,384]{1,0:T(8,128)S(1)} %pad_maximum_fusion.11), channel_id=1, source_target_pairs={{0,2},{1,3},{2,0},{3,1},{4,6},{5,7},{6,4},{7,5},{8,10},{9,11},{10,... | collective-permute-start | bytes 442376 | tf_op jit(solution)/shard_map/ppermute | solution.py:740
  25.3 13.4 %collective-permute-start.11 = (f32[96,384]{1,0:T(8,128)S(1)}, f32[96,384]{1,0:T(8,128)S(1)}, u32[]{:S(2)}, u32[]{:S(2)}) collective-permute-start(f32[96,384]{1,0:T(8,128)S(1)} %pad_maximum_fusion.11), channel_id=1, source_target_pairs={{0,4},{1,5},{2,6},{3,7},{4,0},{5,1},{6,2},{7,3},{8,12},{9,13},{10,... | collective-permute-start | bytes 442376 | tf_op jit(solution)/shard_map/ppermute | solution.py:740
  28.8 9.8 %collective-permute-start.12 = (f32[96,384]{1,0:T(8,128)S(1)}, f32[96,384]{1,0:T(8,128)S(1)}, u32[]{:S(2)}, u32[]{:S(2)}) collective-permute-start(f32[96,384]{1,0:T(8,128)S(1)} %pad_maximum_fusion.11), channel_id=1, source_target_pairs={{0,6},{1,7},{2,4},{3,5},{4,2},{5,3},{6,0},{7,1},{8,14},{9,15},{10,... | collective-permute-start | bytes 442376 | tf_op jit(solution)/shard_map/ppermute | solution.py:740
  41.1 23.6 %collective-permute-start.16 = (f32[384,384]{1,0:T(8,128)S(1)}, f32[384,384]{1,0:T(8,128)S(1)}, u32[]{:S(2)}, u32[]{:S(2)}) collective-permute-start(f32[384,384]{1,0:T(8,128)S(1)} %pad_maximum_fusion.1.refs_0_), channel_id=1, source_target_pairs={{0,8},{8,0},{16,24},{24,16},{1,9},{9,1},{17,25},{25,17},{2,10},{10... | collective-permute-start | bytes 1769480 | tf_op jit(solution)/shard_map/ppermute | solution.py:743
  42.6 22.2 %collective-permute-start.17 = (f32[384,384]{1,0:T(8,128)S(1)}, f32[384,384]{1,0:T(8,128)S(1)}, u32[]{:S(2)}, u32[]{:S(2)}) collective-permute-start(f32[384,384]{1,0:T(8,128)S(1)} %pad_maximum_fusion.1.refs_0_), channel_id=1, source_target_pairs={{0,16},{8,24},{16,0},{24,8},{1,17},{9,25},{17,1},{25,9},{2,18},{10... | collective-permute-start | bytes 1769480 | tf_op jit(solution)/shard_map/ppermute | solution.py:743
  44.1 20.5 %collective-permute-start.18 = (f32[96,384]{1,0:T(8,128)S(1)}, f32[96,384]{1,0:T(8,128)S(1)}, u32[]{:S(2)}, u32[]{:S(2)}) collective-permute-start(f32[96,384]{1,0:T(8,128)S(1)} %pad_maximum_fusion.10), channel_id=1, source_target_pairs={{0,2},{1,3},{2,0},{3,1},{4,6},{5,7},{6,4},{7,5},{8,10},{9,11},{10,... | collective-permute-start | bytes 442376 | tf_op jit(solution)/shard_map/ppermute | solution.py:740
  47.3 17.4 %collective-permute-start.19 = (f32[96,384]{1,0:T(8,128)S(1)}, f32[96,384]{1,0:T(8,128)S(1)}, u32[]{:S(2)}, u32[]{:S(2)}) collective-permute-start(f32[96,384]{1,0:T(8,128)S(1)} %pad_maximum_fusion.10), channel_id=1, source_target_pairs={{0,4},{1,5},{2,6},{3,7},{4,0},{5,1},{6,2},{7,3},{8,12},{9,13},{10,... | collective-permute-start | bytes 442376 | tf_op jit(solution)/shard_map/ppermute | solution.py:740
  48.5 16.2 %collective-permute-start.20 = (f32[96,384]{1,0:T(8,128)S(1)}, f32[96,384]{1,0:T(8,128)S(1)}, u32[]{:S(2)}, u32[]{:S(2)}) collective-permute-start(f32[96,384]{1,0:T(8,128)S(1)} %pad_maximum_fusion.10), channel_id=1, source_target_pairs={{0,6},{1,7},{2,4},{3,5},{4,2},{5,3},{6,0},{7,1},{8,14},{9,15},{10,... | collective-permute-start | bytes 442376 | tf_op jit(solution)/shard_map/ppermute | solution.py:740
  80.8 8.8 %collective-permute-start.25 = (f32[4,4,48,384]{3,2,1,0:T(8,128)S(1)}, f32[4,4,48,384]{3,2,1,0:T(8,128)S(1)}, u32[]{:S(2)}, u32[]{:S(2)}) collective-permute-start(f32[4,4,48,384]{3,2,1,0:T(8,128)S(1)} %get-tuple-element.174), channel_id=1, source_target_pairs={{0,1},{1,0},{2,3},{3,2},{4,5},{5,4},{6,7},{7,6},{8,9},{9,8},{10,11... | collective-permute-start | bytes 3538952 | tf_op jit(solution)/shard_map/ppermute | solution.py:737
  90.5 10.5 %collective-permute-start.26 = (f32[4,4,48,384]{3,2,1,0:T(8,128)S(1)}, f32[4,4,48,384]{3,2,1,0:T(8,128)S(1)}, u32[]{:S(2)}, u32[]{:S(2)}) collective-permute-start(f32[4,4,48,384]{3,2,1,0:T(8,128)S(1)} %get-tuple-element.180), channel_id=1, source_target_pairs={{0,1},{1,0},{2,3},{3,2},{4,5},{5,4},{6,7},{7,6},{8,9},{9,8},{10,11... | collective-permute-start | bytes 3538952 | tf_op jit(solution)/shard_map/ppermute | solution.py:737
  91.8 12.0 %collective-permute-start.32 = (f32[4,48,384]{2,1,0:T(8,128)S(1)}, f32[4,48,384]{2,1,0:T(8,128)S(1)}, u32[]{:S(2)}, u32[]{:S(2)}) collective-permute-start(f32[4,48,384]{2,1,0:T(8,128)S(1)} %get-tuple-element.211), channel_id=1, source_target_pairs={{0,8},{8,0},{16,24},{24,16},{1,9},{9,1},{17,25},{25,17},{2,10},{10... | collective-permute-start | bytes 884744 | tf_op jit(solution)/shard_map/ppermute | solution.py:743
  92.4 28.4 %collective-permute-start.33 = (f32[4,48,384]{2,1,0:T(8,128)S(1)}, f32[4,48,384]{2,1,0:T(8,128)S(1)}, u32[]{:S(2)}, u32[]{:S(2)}) collective-permute-start(f32[4,48,384]{2,1,0:T(8,128)S(1)} %get-tuple-element.212), channel_id=1, source_target_pairs={{0,16},{8,24},{16,0},{24,8},{1,17},{9,25},{17,1},{25,9},{2,18},{10... | collective-permute-start | bytes 884744 | tf_op jit(solution)/shard_map/ppermute | solution.py:743
  93.8 27.0 %collective-permute-start.34 = (f32[4,48,384]{2,1,0:T(8,128)S(1)}, f32[4,48,384]{2,1,0:T(8,128)S(1)}, u32[]{:S(2)}, u32[]{:S(2)}) collective-permute-start(f32[4,48,384]{2,1,0:T(8,128)S(1)} %get-tuple-element.213), channel_id=1, source_target_pairs={{0,24},{8,16},{16,8},{24,0},{1,25},{9,17},{17,9},{25,1},{2,26},{10... | collective-permute-start | bytes 884744 | tf_op jit(solution)/shard_map/ppermute | solution.py:743
  101.8 18.9 %collective-permute-start.29 = (f32[4,48,384]{2,1,0:T(8,128)S(1)}, f32[4,48,384]{2,1,0:T(8,128)S(1)}, u32[]{:S(2)}, u32[]{:S(2)}) collective-permute-start(f32[4,48,384]{2,1,0:T(8,128)S(1)} %get-tuple-element.207), channel_id=1, source_target_pairs={{0,8},{8,0},{16,24},{24,16},{1,9},{9,1},{17,25},{25,17},{2,10},{10... | collective-permute-start | bytes 884744 | tf_op jit(solution)/shard_map/ppermute | solution.py:743
  102.4 18.4 %collective-permute-start.30 = (f32[4,48,384]{2,1,0:T(8,128)S(1)}, f32[4,48,384]{2,1,0:T(8,128)S(1)}, u32[]{:S(2)}, u32[]{:S(2)}) collective-permute-start(f32[4,48,384]{2,1,0:T(8,128)S(1)} %get-tuple-element.208), channel_id=1, source_target_pairs={{0,16},{8,24},{16,0},{24,8},{1,17},{9,25},{17,1},{25,9},{2,18},{10... | collective-permute-start | bytes 884744 | tf_op jit(solution)/shard_map/ppermute | solution.py:743
  103.8 17.0 %collective-permute-start.31 = (f32[4,48,384]{2,1,0:T(8,128)S(1)}, f32[4,48,384]{2,1,0:T(8,128)S(1)}, u32[]{:S(2)}, u32[]{:S(2)}) collective-permute-start(f32[4,48,384]{2,1,0:T(8,128)S(1)} %get-tuple-element.209), channel_id=1, source_target_pairs={{0,24},{8,16},{16,8},{24,0},{1,25},{9,17},{17,9},{25,1},{2,26},{10... | collective-permute-start | bytes 884744 | tf_op jit(solution)/shard_map/ppermute | solution.py:743
  120.8 6.4 %collective-permute-start.35 = (f32[4,4,48,384]{3,2,1,0:T(8,128)S(1)}, f32[4,4,48,384]{3,2,1,0:T(8,128)}, u32[]{:S(2)}, u32[]{:S(2)}) collective-permute-start(f32[4,4,48,384]{3,2,1,0:T(8,128)S(1)} %get-tuple-element.215), channel_id=1, source_target_pairs={{0,1},{1,0},{2,3},{3,2},{4,5},{5,4},{6,7},{7,6},{8,9},{9,8},{10,11... | collective-permute-start | bytes 3538952 | tf_op jit(solution)/shard_map/ppermute | solution.py:737
  128.8 9.9 %collective-permute-start.37 = (f32[4,48,384]{2,1,0:T(8,128)S(1)}, f32[4,48,384]{2,1,0:T(8,128)S(1)}, u32[]{:S(2)}, u32[]{:S(2)}) collective-permute-start(f32[4,48,384]{2,1,0:T(8,128)S(1)} %get-tuple-element.229), channel_id=1, source_target_pairs={{0,8},{8,0},{16,24},{24,16},{1,9},{9,1},{17,25},{25,17},{2,10},{10... | collective-permute-start | bytes 884744 | tf_op jit(solution)/shard_map/ppermute | solution.py:743
  129.4 15.2 %collective-permute-start.38 = (f32[4,48,384]{2,1,0:T(8,128)S(1)}, f32[4,48,384]{2,1,0:T(8,128)S(1)}, u32[]{:S(2)}, u32[]{:S(2)}) collective-permute-start(f32[4,48,384]{2,1,0:T(8,128)S(1)} %get-tuple-element.230), channel_id=1, source_target_pairs={{0,16},{8,24},{16,0},{24,8},{1,17},{9,25},{17,1},{25,9},{2,18},{10... | collective-permute-start | bytes 884744 | tf_op jit(solution)/shard_map/ppermute | solution.py:743
  129.9 14.7 %collective-permute-start.39 = (f32[4,48,384]{2,1,0:T(8,128)S(1)}, f32[4,48,384]{2,1,0:T(8,128)S(1)}, u32[]{:S(2)}, u32[]{:S(2)}) collective-permute-start(f32[4,48,384]{2,1,0:T(8,128)S(1)} %get-tuple-element.231), channel_id=1, source_target_pairs={{0,24},{8,16},{16,8},{24,0},{1,25},{9,17},{17,9},{25,1},{2,26},{10... | collective-permute-start | bytes 884744 | tf_op jit(solution)/shard_map/ppermute | solution.py:743
  132.6 15.4 %collective-permute-start.43 = (f32[112,384]{1,0:T(8,128)S(1)}, f32[112,384]{1,0:T(8,128)S(1)}, u32[]{:S(2)}, u32[]{:S(2)}) collective-permute-start(f32[112,384]{1,0:T(8,128)S(1)} %get-tuple-element.300), channel_id=1, source_target_pairs={{0,2},{1,3},{2,0},{3,1},{4,6},{5,7},{6,4},{7,5},{8,10},{9,11},{10,... | collective-permute-start | bytes 516104 | tf_op jit(solution)/shard_map/ppermute | solution.py:740
  134.0 15.2 %collective-permute-start.44 = (f32[112,384]{1,0:T(8,128)S(1)}, f32[112,384]{1,0:T(8,128)S(1)}, u32[]{:S(2)}, u32[]{:S(2)}) collective-permute-start(f32[112,384]{1,0:T(8,128)S(1)} %get-tuple-element.301), channel_id=1, source_target_pairs={{0,4},{1,5},{2,6},{3,7},{4,0},{5,1},{6,2},{7,3},{8,12},{9,13},{10,... | collective-permute-start | bytes 516104 | tf_op jit(solution)/shard_map/ppermute | solution.py:740
  138.7 10.4 %collective-permute-start.45 = (f32[112,384]{1,0:T(8,128)S(1)}, f32[112,384]{1,0:T(8,128)S(1)}, u32[]{:S(2)}, u32[]{:S(2)}) collective-permute-start(f32[112,384]{1,0:T(8,128)S(1)} %get-tuple-element.302), channel_id=1, source_target_pairs={{0,6},{1,7},{2,4},{3,5},{4,2},{5,3},{6,0},{7,1},{8,14},{9,15},{10,... | collective-permute-start | bytes 516104 | tf_op jit(solution)/shard_map/ppermute | solution.py:740
  144.7 4.9 %collective-permute-start.40 = (f32[48,384]{1,0:T(8,128)S(1)}, f32[48,384]{1,0:T(8,128)S(1)}, u32[]{:S(2)}, u32[]{:S(2)}) collective-permute-start(f32[48,384]{1,0:T(8,128)S(1)} %get-tuple-element.260), channel_id=1, source_target_pairs={{0,2},{1,3},{2,0},{3,1},{4,6},{5,7},{6,4},{7,5},{8,10},{9,11},{10,... | collective-permute-start | bytes 221192 | tf_op jit(solution)/shard_map/ppermute | solution.py:740
  146.0 10.6 %collective-permute-start.41 = (f32[48,384]{1,0:T(8,128)S(1)}, f32[48,384]{1,0:T(8,128)S(1)}, u32[]{:S(2)}, u32[]{:S(2)}) collective-permute-start(f32[48,384]{1,0:T(8,128)S(1)} %get-tuple-element.262), channel_id=1, source_target_pairs={{0,4},{1,5},{2,6},{3,7},{4,0},{5,1},{6,2},{7,3},{8,12},{9,13},{10,... | collective-permute-start | bytes 221192 | tf_op jit(solution)/shard_map/ppermute | solution.py:740
  148.0 8.6 %collective-permute-start.42 = (f32[48,384]{1,0:T(8,128)S(1)}, f32[48,384]{1,0:T(8,128)S(1)}, u32[]{:S(2)}, u32[]{:S(2)}) collective-permute-start(f32[48,384]{1,0:T(8,128)S(1)} %get-tuple-element.261), channel_id=1, source_target_pairs={{0,6},{1,7},{2,4},{3,5},{4,2},{5,3},{6,0},{7,1},{8,14},{9,15},{10,... | collective-permute-start | bytes 221192 | tf_op jit(solution)/shard_map/ppermute | solution.py:740
  156.7 4.7 %collective-permute-start.49 = (f32[48,384]{1,0:T(8,128)S(1)}, f32[48,384]{1,0:T(8,128)S(1)}, u32[]{:S(2)}, u32[]{:S(2)}) collective-permute-start(f32[48,384]{1,0:T(8,128)S(1)} %get-tuple-element.296), channel_id=1, source_target_pairs={{0,8},{8,0},{16,24},{24,16},{1,9},{9,1},{17,25},{25,17},{2,10},{10... | collective-permute-start | bytes 221192 | tf_op jit(solution)/shard_map/ppermute | solution.py:743
  157.8 5.3 %collective-permute-start.51 = (f32[48,384]{1,0:T(8,128)S(1)}, f32[48,384]{1,0:T(8,128)S(1)}, u32[]{:S(2)}, u32[]{:S(2)}) collective-permute-start(f32[48,384]{1,0:T(8,128)S(1)} %get-tuple-element.258), channel_id=1, source_target_pairs={{0,24},{8,16},{16,8},{24,0},{1,25},{9,17},{17,9},{25,1},{2,26},{10... | collective-permute-start | bytes 221192 | tf_op jit(solution)/shard_map/ppermute | solution.py:743
  167.8 6.4 %collective-permute-start.54 = (f32[96,128]{1,0:T(8,128)S(1)}, f32[96,128]{1,0:T(8,128)S(1)}, u32[]{:S(2)}, u32[]{:S(2)}) collective-permute-start(f32[96,128]{1,0:T(8,128)S(1)} %get-tuple-element.297), channel_id=1, source_target_pairs={{0,4},{1,5},{2,6},{3,7},{4,0},{5,1},{6,2},{7,3},{8,12},{9,13},{10,... | collective-permute-start | bytes 147464 | tf_op jit(solution)/shard_map/ppermute | solution.py:740
  169.6 5.9 %collective-permute-start.55 = (f32[96,128]{1,0:T(8,128)S(1)}, f32[96,128]{1,0:T(8,128)S(1)}, u32[]{:S(2)}, u32[]{:S(2)}) collective-permute-start(f32[96,128]{1,0:T(8,128)S(1)} %get-tuple-element.298), channel_id=1, source_target_pairs={{0,6},{1,7},{2,4},{3,5},{4,2},{5,3},{6,0},{7,1},{8,14},{9,15},{10,... | collective-permute-start | bytes 147464 | tf_op jit(solution)/shard_map/ppermute | solution.py:740
  175.5 7.5 %collective-permute-start.56 = (f32[96,128]{1,0:T(8,128)S(1)}, f32[96,128]{1,0:T(8,128)S(1)}, u32[]{:S(2)}, u32[]{:S(2)}) collective-permute-start(f32[96,128]{1,0:T(8,128)S(1)} %fusion.26), channel_id=1, source_target_pairs={{0,2},{1,3},{2,0},{3,1},{4,6},{5,7},{6,4},{7,5},{8,10},{9,11},{10,... | collective-permute-start | bytes 147464 | tf_op jit(solution)/shard_map/ppermute | solution.py:740
  175.6 7.9 %collective-permute-start.57 = (f32[96,128]{1,0:T(8,128)S(1)}, f32[96,128]{1,0:T(8,128)S(1)}, u32[]{:S(2)}, u32[]{:S(2)}) collective-permute-start(f32[96,128]{1,0:T(8,128)S(1)} %fusion.26), channel_id=1, source_target_pairs={{0,4},{1,5},{2,6},{3,7},{4,0},{5,1},{6,2},{7,3},{8,12},{9,13},{10,... | collective-permute-start | bytes 147464 | tf_op jit(solution)/shard_map/ppermute | solution.py:740
  177.9 5.9 %collective-permute-start.58 = (f32[96,128]{1,0:T(8,128)S(1)}, f32[96,128]{1,0:T(8,128)S(1)}, u32[]{:S(2)}, u32[]{:S(2)}) collective-permute-start(f32[96,128]{1,0:T(8,128)S(1)} %fusion.26), channel_id=1, source_target_pairs={{0,6},{1,7},{2,4},{3,5},{4,2},{5,3},{6,0},{7,1},{8,14},{9,15},{10,... | collective-permute-start | bytes 147464 | tf_op jit(solution)/shard_map/ppermute | solution.py:740
  180.0 20.7 %collective-permute-start.46 = (f32[160,384]{1,0:T(8,128)S(1)}, f32[160,384]{1,0:T(8,128)S(1)}, u32[]{:S(2)}, u32[]{:S(2)}) collective-permute-start(f32[160,384]{1,0:T(8,128)S(1)} %pad_maximum_fusion.7.refs_0_), channel_id=1, source_target_pairs={{0,8},{8,0},{16,24},{24,16},{1,9},{9,1},{17,25},{25,17},{2,10},{10... | collective-permute-start | bytes 737288 | tf_op jit(solution)/shard_map/ppermute | solution.py:743
  181.5 19.2 %collective-permute-start.47 = (f32[160,384]{1,0:T(8,128)S(1)}, f32[160,384]{1,0:T(8,128)S(1)}, u32[]{:S(2)}, u32[]{:S(2)}) collective-permute-start(f32[160,384]{1,0:T(8,128)S(1)} %pad_maximum_fusion.7.refs_0_), channel_id=1, source_target_pairs={{0,16},{8,24},{16,0},{24,8},{1,17},{9,25},{17,1},{25,9},{2,18},{10... | collective-permute-start | bytes 737288 | tf_op jit(solution)/shard_map/ppermute | solution.py:743
  183.0 17.7 %collective-permute-start.48 = (f32[160,384]{1,0:T(8,128)S(1)}, f32[160,384]{1,0:T(8,128)S(1)}, u32[]{:S(2)}, u32[]{:S(2)}) collective-permute-start(f32[160,384]{1,0:T(8,128)S(1)} %pad_maximum_fusion.7.refs_0_), channel_id=1, source_target_pairs={{0,24},{8,16},{16,8},{24,0},{1,25},{9,17},{17,9},{25,1},{2,26},{10... | collective-permute-start | bytes 737288 | tf_op jit(solution)/shard_map/ppermute | solution.py:743
  200.7 9.9 %collective-permute-start.60 = (f32[192,384]{1,0:T(8,128)S(1)}, f32[192,384]{1,0:T(8,128)S(1)}, u32[]{:S(2)}, u32[]{:S(2)}) collective-permute-start(f32[192,384]{1,0:T(8,128)S(1)} %shard_map.271.one), channel_id=1, source_target_pairs={{0,8},{8,0},{16,24},{24,16},{1,9},{9,1},{17,25},{25,17},{2,10},{10... | collective-permute-start | bytes 884744 | tf_op jit(solution)/shard_map/ppermute | solution.py:743
  202.3 15.1 %collective-permute-start.61 = (f32[192,384]{1,0:T(8,128)S(1)}, f32[192,384]{1,0:T(8,128)S(1)}, u32[]{:S(2)}, u32[]{:S(2)}) collective-permute-start(f32[192,384]{1,0:T(8,128)S(1)} %shard_map.271.one), channel_id=1, source_target_pairs={{0,16},{8,24},{16,0},{24,8},{1,17},{9,25},{17,1},{25,9},{2,18},{10... | collective-permute-start | bytes 884744 | tf_op jit(solution)/shard_map/ppermute | solution.py:743
  203.8 13.6 %collective-permute-start.62 = (f32[192,384]{1,0:T(8,128)S(1)}, f32[192,384]{1,0:T(8,128)S(1)}, u32[]{:S(2)}, u32[]{:S(2)}) collective-permute-start(f32[192,384]{1,0:T(8,128)S(1)} %shard_map.271.one), channel_id=1, source_target_pairs={{0,24},{8,16},{16,8},{24,0},{1,25},{9,17},{17,9},{25,1},{2,26},{10... | collective-permute-start | bytes 884744 | tf_op jit(solution)/shard_map/ppermute | solution.py:743
  (48 other events, 273.1 us)

commit v3 on v2

--- a/solution.py
+++ b/solution.py
@@ -610,10 +610,14 @@
 
 
 def polar(gram, block):
-    state = polar_start(gram, block)
-    for _ in range(NS_STEPS - 1):
-        state = polar_step(*state)
-    return polar_end(*state)
+    gram, block = polar_start(gram, block)
+    for step_index in range(NS_STEPS):
+        square = fdot(gram, gram, NN, precise)
+        poly = ns_coeffs[1] * gram + ns_coeffs[2] * square + ns_coeffs[0] * identity()
+        if step_index + 1 < NS_STEPS:
+            gram = fdot(poly, fdot(poly, gram, NN, precise), NN, precise)
+        block = fdot(block, poly, NN, precise)
+    return block
 
 
 def update_kernel(scalars, mine, other, own, out, total, gram, block):
@@ -787,8 +791,9 @@
             rows = jnp.concatenate(
                 [parts[:, :inner].reshape(-1, D), parts[:, inner:].reshape(-1, D)], axis=0
             )
-            hi, lo = halves(rows)
-            return jnp.concatenate([hi, lo, hi], axis=1)
+            hi = lax.reduce_precision(rows, 8, 7)
+            lo = lax.reduce_precision(rows - hi, 8, 7)
+            return jnp.concatenate([hi, lo, hi], axis=1).astype(bf16)
 
         def shares_of(total, cut, inner):
             one, two = total[:cut], total[cut:]

time: 219 us -> 219 us (level)
  no operation moved by 1% of the time
where the time goes in v3:
time: 219 us
  starting transfers between devices  75.6 us (35%)
  Pallas kernels  75.1 us (34%)
  waiting for transfers between devices  54.4 us (25%)
  local copies, waits for them, and re-layouts  5.94 us (3%)
  other arithmetic  5.72 us (3%)
  between operations  2.25 us (1%)
    pallas_call x14, Pallas kernels, run(): pl.pallas_call(body, out_shape=[jax.ShapeDtypeStruct(s, t) for s, t in ou...  75.1 us
    ppermute x21, starting transfers between devices, hop(): lax.ppermute(x, 'group', [(i, i ^ 2 * by) for i in range(group_size)])  38 us
    ppermute x23, starting transfers between devices, cross(): return lax.ppermute(x, 'replica', [(i, i ^ by) for i in range(replicas)])  26.9 us
    ppermute x23, waiting for transfers between devices, cross(): return lax.ppermute(x, 'replica', [(i, i ^ by) for i in range(replicas)])  22.5 us
    ppermute x21, waiting for transfers between devices, hop(): lax.ppermute(x, 'group', [(i, i ^ 2 * by) for i in range(group_size)])  19.4 us
    ppermute x17, waiting for transfers between devices, swap(): return lax.ppermute(x, 'group', [(i, i ^ 1) for i in range(group_size)])  12.5 us
    ppermute x17, starting transfers between devices, swap(): return lax.ppermute(x, 'group', [(i, i ^ 1) for i in range(group_size)])  9.37 us
  transfers between devices with their start and end apart: 63, of which 29 were waited for; matrix products, arithmetic and copies ran while one was open for 3% of the time, Pallas kernels for 28%

profile of v3, /device:TPU:0, one launch (start us, length us, event | category | flops | bytes accessed | tf_op | source)
XLA Modules:
  0.0 218.9 jit_solution(7279941788780451291)
XLA Ops:
  3.3 3.0 %collective-permute-start = (f32[56,384]{1,0:T(8,128)S(1)}, f32[56,384]{1,0:T(8,128)S(1)}, u32[]{:S(2)}, u32[]{:S(2)}) collective-permute-start(f32[56,384]{1,0:T(8,128)S(1)} %shard_map.260), channel_id=1, source_target_pairs={{0,2},{1,3},{2,0},{3,1},{4,6},{5,7},{6,4},{7,5},{8,10},{9,11},{10,... | collective-permute-start | bytes 258056 | tf_op jit(solution)/shard_map/ppermute | solution.py:744
  6.3 2.6 %collective-permute-start.1 = (f32[56,384]{1,0:T(8,128)S(1)}, f32[56,384]{1,0:T(8,128)S(1)}, u32[]{:S(2)}, u32[]{:S(2)}) collective-permute-start(f32[56,384]{1,0:T(8,128)S(1)} %shard_map.260), channel_id=1, source_target_pairs={{0,4},{1,5},{2,6},{3,7},{4,0},{5,1},{6,2},{7,3},{8,12},{9,13},{10,... | collective-permute-start | bytes 258056 | tf_op jit(solution)/shard_map/ppermute | solution.py:744
  12.3 3.6 %collective-permute-done.1 = f32[56,384]{1,0:T(8,128)S(1)} collective-permute-done((f32[56,384]{1,0:T(8,128)S(1)}, f32[56,384]{1,0:T(8,128)S(1)}, u32[]{:S(2)}, u32[]{:S(2)}) %collective-permute-start.1) | collective-permute-done | bytes 86048 | tf_op jit(solution)/shard_map/ppermute | solution.py:744
  16.0 2.9 %collective-permute-start.8 = (f32[192,384]{1,0:T(8,128)S(1)}, f32[192,384]{1,0:T(8,128)S(1)}, u32[]{:S(2)}, u32[]{:S(2)}) collective-permute-start(f32[192,384]{1,0:T(8,128)S(1)} %pad_maximum_fusion.6.refs_0_), channel_id=1, source_target_pairs={{0,1},{1,0},{2,3},{3,2},{4,5},{5,4},{6,7},{7,6},{8,9},{9,8},{10,11... | collective-permute-start | bytes 884744 | tf_op jit(solution)/shard_map/ppermute | solution.py:741
  18.9 1.6 collective-permute-start.5
  20.5 1.5 collective-permute-start.6
  23.8 1.5 collective-permute-start.10
  25.3 2.3 %collective-permute-start.11 = (f32[96,384]{1,0:T(8,128)S(1)}, f32[96,384]{1,0:T(8,128)S(1)}, u32[]{:S(2)}, u32[]{:S(2)}) collective-permute-start(f32[96,384]{1,0:T(8,128)S(1)} %pad_maximum_fusion.11), channel_id=1, source_target_pairs={{0,4},{1,5},{2,6},{3,7},{4,0},{5,1},{6,2},{7,3},{8,12},{9,13},{10,... | collective-permute-start | bytes 442376 | tf_op jit(solution)/shard_map/ppermute | solution.py:744
  28.8 3.2 %collective-permute-start.12 = (f32[96,384]{1,0:T(8,128)S(1)}, f32[96,384]{1,0:T(8,128)S(1)}, u32[]{:S(2)}, u32[]{:S(2)}) collective-permute-start(f32[96,384]{1,0:T(8,128)S(1)} %pad_maximum_fusion.11), channel_id=1, source_target_pairs={{0,6},{1,7},{2,4},{3,5},{4,2},{5,3},{6,0},{7,1},{8,14},{9,15},{10,... | collective-permute-start | bytes 442376 | tf_op jit(solution)/shard_map/ppermute | solution.py:744
  31.9 3.5 %collective-permute-done.6.refs_2_ = f32[192,384]{1,0:T(8,128)S(1)} collective-permute-done((f32[192,384]{1,0:T(8,128)S(1)}, f32[192,384]{1,0:T(8,128)S(1)}, u32[]{:S(2)}, u32[]{:S(2)}) %collective-permute-start.6) | collective-permute-done | bytes 294944 | tf_op jit(solution)/shard_map/ppermute | solution.py:747
  35.5 3.2 %collective-permute-done.11 = f32[96,384]{1,0:T(8,128)S(1)} collective-permute-done((f32[96,384]{1,0:T(8,128)S(1)}, f32[96,384]{1,0:T(8,128)S(1)}, u32[]{:S(2)}, u32[]{:S(2)}) %collective-permute-start.11) | collective-permute-done | bytes 147488 | tf_op jit(solution)/shard_map/ppermute | solution.py:744
  41.1 1.5 collective-permute-start.16
  42.6 1.5 collective-permute-start.17
  44.1 3.2 %collective-permute-start.18 = (f32[96,384]{1,0:T(8,128)S(1)}, f32[96,384]{1,0:T(8,128)S(1)}, u32[]{:S(2)}, u32[]{:S(2)}) collective-permute-start(f32[96,384]{1,0:T(8,128)S(1)} %pad_maximum_fusion.10), channel_id=1, source_target_pairs={{0,2},{1,3},{2,0},{3,1},{4,6},{5,7},{6,4},{7,5},{8,10},{9,11},{10,... | collective-permute-start | bytes 442376 | tf_op jit(solution)/shard_map/ppermute | solution.py:744
  48.5 1.5 collective-permute-start.20
  51.0 13.6 %shard_map.262 = (bf16[4,6,208,128]{3,2,1,0:T(8,128)(2,1)S(1)}, bf16[4,6,128,208]{3,2,1,0:T(8,128)(2,1)S(1)}, bf16[4,6,208,128]{3,2,1,0:T(8,128)(2,1)S(1)}, bf16...) custom-call(s32[6]{0:T(128)S(1)} %stack.39.scalars, ...), custom_call_target="tpu_custom_call" | custom-call | flops 100000000 | bytes 262144 | tf_op jit(solution)/shard_map/pallas_call | solution.py:43
  70.4 10.4 %shard_map.264 = (f32[512,384]{1,0:T(8,128)}, f32[512,1536]{1,0:T(8,128)S(1)}, bf16[512,1152]{1,0:T(8,128)(2,1)S(1)}, bf16[512,1152]{1,0:T(8,128)(2,1)S(1)}, f32...) custom-call(s32[6]{0:T(128)S(1)} %stack.39.scalars, ...), custom_call_target="tpu_custom_call" | custom-call | flops 100000000 | bytes 262144 | tf_op jit(solution)/shard_map/pallas_call | solution.py:43
  80.9 8.7 %shard_map.265 = (f32[512,384]{1,0:T(8,128)S(1)}, f32[16,384]{1,0:T(8,128)S(1)}, f32[4,48,384]{2,1,0:T(8,128)S(1)}, f32[4,48,384]{2,1,0:T(8,128)S(1)}, f32[4,48,...) custom-call(s32[6]{0:T(128)S(1)} %stack.39.scalars, ...), custom_call_target="tpu_custom_call" | custom-call | flops 100000000 | bytes 262144 | tf_op jit(solution)/shard_map/pallas_call | solution.py:43
  93.8 1.6 collective-permute-start.34
  95.3 5.6 %shard_map.266.some = f32[2,208,1152]{2,1,0:T(8,128)S(1)} custom-call(s32[6]{0:T(128)S(1)} %stack.39.scalars, f32[200,384]{1,0:T(8,128)S(1)} %collective-permute-done.27.lower, f32[512,384]{1,0:T(8,128)S(1)} %get-tuple-element.192.own.d_mid, f32[200,384]{1,0:T(8,128)S(1)} %collective-permute-done.28.upper, bf16[1536,1152]{1,0:T(8,128)(2,1)S(1)} %get-tuple-element.157.w, ...), custom_call_target="tpu_custom_call" | custom-call | flops 100000000 | bytes 262144 | tf_op jit(solution)/shard_map/pallas_call | solution.py:43
  103.8 1.5 collective-permute-start.31
  105.3 5.6 %shard_map.267.more = f32[2,208,1152]{2,1,0:T(8,128)S(1)} custom-call(s32[6]{0:T(128)S(1)} %stack.39.scalars, f32[200,384]{1,0:T(8,128)S(1)} %collective-permute-done.27.lower, f32[512,384]{1,0:T(8,128)S(1)} %get-tuple-element.192.own.d_mid, f32[200,384]{1,0:T(8,128)S(1)} %collective-permute-done.28.upper, bf16[1536,1152]{1,0:T(8,128)(2,1)S(1)} %get-tuple-element.157.w, ...), custom_call_target="tpu_custom_call" | custom-call | flops 100000000 | bytes 262144 | tf_op jit(solution)/shard_map/pallas_call | solution.py:43
  111.0 6.1 %shard_map.268 = (f32[4,48,384]{2,1,0:T(8,128)S(1)}, f32[4,48,384]{2,1,0:T(8,128)S(1)}, f32[4,48,384]{2,1,0:T(8,128)S(1)}, f32[4,48,384]{2,1,0:T(8,128)S(1)}, f3...) custom-call(s32[6]{0:T(128)S(1)} %stack.39.scalars, ...), custom_call_target="tpu_custom_call" | custom-call | flops 100000000 | bytes 262144 | tf_op jit(solution)/shard_map/pallas_call | solution.py:43
  117.2 3.6 %shard_map.269 = (f32[512,384]{1,0:T(8,128)}, f32[16,384]{1,0:T(8,128)S(1)}) custom-call(s32[6]{0:T(128)S(1)} %stack.39.scalars, bf16[512,1152]{1,0:T(8,128)(2,1)S(1)} %get-tuple-element.195.d_hi, bf16[512,1152]{1,0:T(8,128)(2,1)S(1)} %get-tuple-element.196.d_lo, bf16[1536,1152]{1,0:T(8,128)(2,1)S(1)} %get-tuple-element.157.w, f32[512,384]{1,0:T(8,128)S(1)} %copy-done, ...), custom_call_target="tpu_custom_call" | custom-call | flops 100000000 | bytes 262144 | tf_op jit(solution)/shard_map/pallas_call | solution.py:43
  120.8 3.8 %collective-permute-start.35 = (f32[4,4,48,384]{3,2,1,0:T(8,128)S(1)}, f32[4,4,48,384]{3,2,1,0:T(8,128)}, u32[]{:S(2)}, u32[]{:S(2)}) collective-permute-start(f32[4,4,48,384]{3,2,1,0:T(8,128)S(1)} %get-tuple-element.215), channel_id=1, source_target_pairs={{0,1},{1,0},{2,3},{3,2},{4,5},{5,4},{6,7},{7,6},{8,9},{9,8},{10,11... | collective-permute-start | bytes 3538952 | tf_op jit(solution)/shard_map/ppermute | solution.py:741
  124.9 2.1 collective-permute-done.36
  129.9 2.5 %collective-permute-start.39 = (f32[4,48,384]{2,1,0:T(8,128)S(1)}, f32[4,48,384]{2,1,0:T(8,128)S(1)}, u32[]{:S(2)}, u32[]{:S(2)}) collective-permute-start(f32[4,48,384]{2,1,0:T(8,128)S(1)} %get-tuple-element.231), channel_id=1, source_target_pairs={{0,24},{8,16},{16,8},{24,0},{1,25},{9,17},{17,9},{25,1},{2,26},{10... | collective-permute-start | bytes 884744 | tf_op jit(solution)/shard_map/ppermute | solution.py:747
  134.0 2.0 collective-permute-start.44
  136.0 2.7 %collective-permute-done.37 = f32[4,48,384]{2,1,0:T(8,128)S(1)} collective-permute-done((f32[4,48,384]{2,1,0:T(8,128)S(1)}, f32[4,48,384]{2,1,0:T(8,128)S(1)}, u32[]{:S(2)}, u32[]{:S(2)}) %collective-permute-start.37) | collective-permute-done | bytes 294944 | tf_op jit(solution)/shard_map/ppermute | solution.py:747
  138.7 2.8 %collective-permute-start.45 = (f32[112,384]{1,0:T(8,128)S(1)}, f32[112,384]{1,0:T(8,128)S(1)}, u32[]{:S(2)}, u32[]{:S(2)}) collective-permute-start(f32[112,384]{1,0:T(8,128)S(1)} %get-tuple-element.302), channel_id=1, source_target_pairs={{0,6},{1,7},{2,4},{3,5},{4,2},{5,3},{6,0},{7,1},{8,14},{9,15},{10,... | collective-permute-start | bytes 516104 | tf_op jit(solution)/shard_map/ppermute | solution.py:744
  141.4 3.1 %collective-permute-done.38 = f32[4,48,384]{2,1,0:T(8,128)S(1)} collective-permute-done((f32[4,48,384]{2,1,0:T(8,128)S(1)}, f32[4,48,384]{2,1,0:T(8,128)S(1)}, u32[]{:S(2)}, u32[]{:S(2)}) %collective-permute-start.38) | collective-permute-done | bytes 294944 | tf_op jit(solution)/shard_map/ppermute | solution.py:747
  146.0 2.0 collective-permute-start.41
  149.5 7.1 %collective-permute-done.41 = f32[48,384]{1,0:T(8,128)S(1)} collective-permute-done((f32[48,384]{1,0:T(8,128)S(1)}, f32[48,384]{1,0:T(8,128)S(1)}, u32[]{:S(2)}, u32[]{:S(2)}) %collective-permute-start.41) | collective-permute-done | bytes 73760 | tf_op jit(solution)/shard_map/ppermute | solution.py:744
  157.8 2.5 %collective-permute-start.51 = (f32[48,384]{1,0:T(8,128)S(1)}, f32[48,384]{1,0:T(8,128)S(1)}, u32[]{:S(2)}, u32[]{:S(2)}) collective-permute-start(f32[48,384]{1,0:T(8,128)S(1)} %get-tuple-element.258), channel_id=1, source_target_pairs={{0,24},{8,16},{16,8},{24,0},{1,25},{9,17},{17,9},{25,1},{2,26},{10... | collective-permute-start | bytes 221192 | tf_op jit(solution)/shard_map/ppermute | solution.py:747
  163.1 1.5 shard_map.270
  166.1 1.6 collective-permute-start.53
  167.8 1.8 collective-permute-start.54
  170.6 3.6 %collective-permute-done.54 = f32[96,128]{1,0:T(8,128)S(1)} collective-permute-done((f32[96,128]{1,0:T(8,128)S(1)}, f32[96,128]{1,0:T(8,128)S(1)}, u32[]{:S(2)}, u32[]{:S(2)}) %collective-permute-start.54) | collective-permute-done | bytes 49184 | tf_op jit(solution)/shard_map/ppermute | solution.py:744
  175.6 2.3 %collective-permute-start.57 = (f32[96,128]{1,0:T(8,128)S(1)}, f32[96,128]{1,0:T(8,128)S(1)}, u32[]{:S(2)}, u32[]{:S(2)}) collective-permute-start(f32[96,128]{1,0:T(8,128)S(1)} %fusion.26), channel_id=1, source_target_pairs={{0,4},{1,5},{2,6},{3,7},{4,0},{5,1},{6,2},{7,3},{8,12},{9,13},{10,... | collective-permute-start | bytes 147464 | tf_op jit(solution)/shard_map/ppermute | solution.py:744
  177.9 2.0 collective-permute-start.58
  180.0 1.6 collective-permute-start.46
  181.5 1.5 collective-permute-start.47
  185.3 15.4 %shard_map.271.one = f32[192,384]{1,0:T(8,128)S(1)} custom-call(s32[6]{0:T(128)S(1)} %stack.39.scalars, f32[4,96,128]{2,1,0:T(8,128)S(1)} %pad_maximum_fusion.9.mine, f32[4,96,128]{2,1,0:T(8,128)S(1)} %collective-permute-done.59.other, f32[192,384]{1,0:T(8,128)S(1)} %get-tuple-element.243.own), custom_call_target="tpu_custom_call" | custom-call | flops 100000000 | bytes 262144 | tf_op jit(solution)/shard_map/pallas_call | solution.py:43
  200.7 1.6 collective-permute-start.60
  202.3 1.5 collective-permute-start.61
  208.2 2.4 %collective-permute-done.60.two = f32[192,384]{1,0:T(8,128)S(1)} collective-permute-done((f32[192,384]{1,0:T(8,128)S(1)}, f32[192,384]{1,0:T(8,128)S(1)}, u32[]{:S(2)}, u32[]{:S(2)}) %collective-permute-start.60) | collective-permute-done | bytes 294944 | tf_op jit(solution)/shard_map/ppermute | solution.py:747
  210.6 6.7 %collective-permute-done.61.three = f32[192,384]{1,0:T(8,128)S(1)} collective-permute-done((f32[192,384]{1,0:T(8,128)S(1)}, f32[192,384]{1,0:T(8,128)S(1)}, u32[]{:S(2)}, u32[]{:S(2)}) %collective-permute-start.61) | collective-permute-done | bytes 294944 | tf_op jit(solution)/shard_map/ppermute | solution.py:747
  217.3 1.6 shard_map.273
  (207 shorter events, 47.7 us)
Async XLA Ops:
  3.3 9.0 %collective-permute-start = (f32[56,384]{1,0:T(8,128)S(1)}, f32[56,384]{1,0:T(8,128)S(1)}, u32[]{:S(2)}, u32[]{:S(2)}) collective-permute-start(f32[56,384]{1,0:T(8,128)S(1)} %shard_map.260), channel_id=1, source_target_pairs={{0,2},{1,3},{2,0},{3,1},{4,6},{5,7},{6,4},{7,5},{8,10},{9,11},{10,... | collective-permute-start | bytes 258056 | tf_op jit(solution)/shard_map/ppermute | solution.py:744
  6.3 9.6 %collective-permute-start.1 = (f32[56,384]{1,0:T(8,128)S(1)}, f32[56,384]{1,0:T(8,128)S(1)}, u32[]{:S(2)}, u32[]{:S(2)}) collective-permute-start(f32[56,384]{1,0:T(8,128)S(1)} %shard_map.260), channel_id=1, source_target_pairs={{0,4},{1,5},{2,6},{3,7},{4,0},{5,1},{6,2},{7,3},{8,12},{9,13},{10,... | collective-permute-start | bytes 258056 | tf_op jit(solution)/shard_map/ppermute | solution.py:744
  8.9 7.0 %collective-permute-start.2 = (f32[56,384]{1,0:T(8,128)S(1)}, f32[56,384]{1,0:T(8,128)S(1)}, u32[]{:S(2)}, u32[]{:S(2)}) collective-permute-start(f32[56,384]{1,0:T(8,128)S(1)} %shard_map.260), channel_id=1, source_target_pairs={{0,6},{1,7},{2,4},{3,5},{4,2},{5,3},{6,0},{7,1},{8,14},{9,15},{10,... | collective-permute-start | bytes 258056 | tf_op jit(solution)/shard_map/ppermute | solution.py:744
  10.1 5.9 %collective-permute-start.3 = (f32[200,384]{1,0:T(8,128)S(1)}, f32[200,384]{1,0:T(8,128)S(1)}, u32[]{:S(2)}, u32[]{:S(2)}) collective-permute-start(f32[200,384]{1,0:T(8,128)S(1)} %get-tuple-element.290), channel_id=1, source_target_pairs={{0,1},{1,0},{2,3},{3,2},{4,5},{5,4},{6,7},{7,6},{8,9},{9,8},{10,11... | collective-permute-start | bytes 921608 | tf_op jit(solution)/shard_map/ppermute | solution.py:741
  10.1 5.9 %collective-permute-start.4 = (f32[200,384]{1,0:T(8,128)S(1)}, f32[200,384]{1,0:T(8,128)S(1)}, u32[]{:S(2)}, u32[]{:S(2)}) collective-permute-start(f32[200,384]{1,0:T(8,128)S(1)} %get-tuple-element.289), channel_id=1, source_target_pairs={{1,2},{3,4},{5,6},{2,1},{4,3},{6,5},{9,10},{11,12},{13,14},{10,9},... | collective-permute-start | bytes 921608 | tf_op jit(solution)/shard_map/ppermute | solution.py:754
  16.0 7.7 %collective-permute-start.8 = (f32[192,384]{1,0:T(8,128)S(1)}, f32[192,384]{1,0:T(8,128)S(1)}, u32[]{:S(2)}, u32[]{:S(2)}) collective-permute-start(f32[192,384]{1,0:T(8,128)S(1)} %pad_maximum_fusion.6.refs_0_), channel_id=1, source_target_pairs={{0,1},{1,0},{2,3},{3,2},{4,5},{5,4},{6,7},{7,6},{8,9},{9,8},{10,11... | collective-permute-start | bytes 884744 | tf_op jit(solution)/shard_map/ppermute | solution.py:741
  18.9 9.9 %collective-permute-start.5 = (f32[192,384]{1,0:T(8,128)S(1)}, f32[192,384]{1,0:T(8,128)S(1)}, u32[]{:S(2)}, u32[]{:S(2)}) collective-permute-start(f32[192,384]{1,0:T(8,128)S(1)} %pad_maximum_fusion.6.refs_0_), channel_id=1, source_target_pairs={{0,8},{8,0},{16,24},{24,16},{1,9},{9,1},{17,25},{25,17},{2,10},{10... | collective-permute-start | bytes 884744 | tf_op jit(solution)/shard_map/ppermute | solution.py:747
  20.5 15.0 %collective-permute-start.6 = (f32[192,384]{1,0:T(8,128)S(1)}, f32[192,384]{1,0:T(8,128)S(1)}, u32[]{:S(2)}, u32[]{:S(2)}) collective-permute-start(f32[192,384]{1,0:T(8,128)S(1)} %pad_maximum_fusion.6.refs_0_), channel_id=1, source_target_pairs={{0,16},{8,24},{16,0},{24,8},{1,17},{9,25},{17,1},{25,9},{2,18},{10... | collective-permute-start | bytes 884744 | tf_op jit(solution)/shard_map/ppermute | solution.py:747
  22.0 13.4 %collective-permute-start.7 = (f32[192,384]{1,0:T(8,128)S(1)}, f32[192,384]{1,0:T(8,128)S(1)}, u32[]{:S(2)}, u32[]{:S(2)}) collective-permute-start(f32[192,384]{1,0:T(8,128)S(1)} %pad_maximum_fusion.6.refs_0_), channel_id=1, source_target_pairs={{0,24},{8,16},{16,8},{24,0},{1,25},{9,17},{17,9},{25,1},{2,26},{10... | collective-permute-start | bytes 884744 | tf_op jit(solution)/shard_map/ppermute | solution.py:747
  23.8 11.7 %collective-permute-start.10 = (f32[96,384]{1,0:T(8,128)S(1)}, f32[96,384]{1,0:T(8,128)S(1)}, u32[]{:S(2)}, u32[]{:S(2)}) collective-permute-start(f32[96,384]{1,0:T(8,128)S(1)} %pad_maximum_fusion.11), channel_id=1, source_target_pairs={{0,2},{1,3},{2,0},{3,1},{4,6},{5,7},{6,4},{7,5},{8,10},{9,11},{10,... | collective-permute-start | bytes 442376 | tf_op jit(solution)/shard_map/ppermute | solution.py:744
  25.3 13.4 %collective-permute-start.11 = (f32[96,384]{1,0:T(8,128)S(1)}, f32[96,384]{1,0:T(8,128)S(1)}, u32[]{:S(2)}, u32[]{:S(2)}) collective-permute-start(f32[96,384]{1,0:T(8,128)S(1)} %pad_maximum_fusion.11), channel_id=1, source_target_pairs={{0,4},{1,5},{2,6},{3,7},{4,0},{5,1},{6,2},{7,3},{8,12},{9,13},{10,... | collective-permute-start | bytes 442376 | tf_op jit(solution)/shard_map/ppermute | solution.py:744
  28.8 9.8 %collective-permute-start.12 = (f32[96,384]{1,0:T(8,128)S(1)}, f32[96,384]{1,0:T(8,128)S(1)}, u32[]{:S(2)}, u32[]{:S(2)}) collective-permute-start(f32[96,384]{1,0:T(8,128)S(1)} %pad_maximum_fusion.11), channel_id=1, source_target_pairs={{0,6},{1,7},{2,4},{3,5},{4,2},{5,3},{6,0},{7,1},{8,14},{9,15},{10,... | collective-permute-start | bytes 442376 | tf_op jit(solution)/shard_map/ppermute | solution.py:744
  41.1 23.6 %collective-permute-start.16 = (f32[384,384]{1,0:T(8,128)S(1)}, f32[384,384]{1,0:T(8,128)S(1)}, u32[]{:S(2)}, u32[]{:S(2)}) collective-permute-start(f32[384,384]{1,0:T(8,128)S(1)} %pad_maximum_fusion.1.refs_0_), channel_id=1, source_target_pairs={{0,8},{8,0},{16,24},{24,16},{1,9},{9,1},{17,25},{25,17},{2,10},{10... | collective-permute-start | bytes 1769480 | tf_op jit(solution)/shard_map/ppermute | solution.py:747
  42.6 22.2 %collective-permute-start.17 = (f32[384,384]{1,0:T(8,128)S(1)}, f32[384,384]{1,0:T(8,128)S(1)}, u32[]{:S(2)}, u32[]{:S(2)}) collective-permute-start(f32[384,384]{1,0:T(8,128)S(1)} %pad_maximum_fusion.1.refs_0_), channel_id=1, source_target_pairs={{0,16},{8,24},{16,0},{24,8},{1,17},{9,25},{17,1},{25,9},{2,18},{10... | collective-permute-start | bytes 1769480 | tf_op jit(solution)/shard_map/ppermute | solution.py:747
  44.1 20.5 %collective-permute-start.18 = (f32[96,384]{1,0:T(8,128)S(1)}, f32[96,384]{1,0:T(8,128)S(1)}, u32[]{:S(2)}, u32[]{:S(2)}) collective-permute-start(f32[96,384]{1,0:T(8,128)S(1)} %pad_maximum_fusion.10), channel_id=1, source_target_pairs={{0,2},{1,3},{2,0},{3,1},{4,6},{5,7},{6,4},{7,5},{8,10},{9,11},{10,... | collective-permute-start | bytes 442376 | tf_op jit(solution)/shard_map/ppermute | solution.py:744
  47.3 17.4 %collective-permute-start.19 = (f32[96,384]{1,0:T(8,128)S(1)}, f32[96,384]{1,0:T(8,128)S(1)}, u32[]{:S(2)}, u32[]{:S(2)}) collective-permute-start(f32[96,384]{1,0:T(8,128)S(1)} %pad_maximum_fusion.10), channel_id=1, source_target_pairs={{0,4},{1,5},{2,6},{3,7},{4,0},{5,1},{6,2},{7,3},{8,12},{9,13},{10,... | collective-permute-start | bytes 442376 | tf_op jit(solution)/shard_map/ppermute | solution.py:744
  48.5 16.2 %collective-permute-start.20 = (f32[96,384]{1,0:T(8,128)S(1)}, f32[96,384]{1,0:T(8,128)S(1)}, u32[]{:S(2)}, u32[]{:S(2)}) collective-permute-start(f32[96,384]{1,0:T(8,128)S(1)} %pad_maximum_fusion.10), channel_id=1, source_target_pairs={{0,6},{1,7},{2,4},{3,5},{4,2},{5,3},{6,0},{7,1},{8,14},{9,15},{10,... | collective-permute-start | bytes 442376 | tf_op jit(solution)/shard_map/ppermute | solution.py:744
  80.8 8.8 %collective-permute-start.25 = (f32[4,4,48,384]{3,2,1,0:T(8,128)S(1)}, f32[4,4,48,384]{3,2,1,0:T(8,128)S(1)}, u32[]{:S(2)}, u32[]{:S(2)}) collective-permute-start(f32[4,4,48,384]{3,2,1,0:T(8,128)S(1)} %get-tuple-element.174), channel_id=1, source_target_pairs={{0,1},{1,0},{2,3},{3,2},{4,5},{5,4},{6,7},{7,6},{8,9},{9,8},{10,11... | collective-permute-start | bytes 3538952 | tf_op jit(solution)/shard_map/ppermute | solution.py:741
  90.5 10.5 %collective-permute-start.26 = (f32[4,4,48,384]{3,2,1,0:T(8,128)S(1)}, f32[4,4,48,384]{3,2,1,0:T(8,128)S(1)}, u32[]{:S(2)}, u32[]{:S(2)}) collective-permute-start(f32[4,4,48,384]{3,2,1,0:T(8,128)S(1)} %get-tuple-element.180), channel_id=1, source_target_pairs={{0,1},{1,0},{2,3},{3,2},{4,5},{5,4},{6,7},{7,6},{8,9},{9,8},{10,11... | collective-permute-start | bytes 3538952 | tf_op jit(solution)/shard_map/ppermute | solution.py:741
  91.8 12.0 %collective-permute-start.32 = (f32[4,48,384]{2,1,0:T(8,128)S(1)}, f32[4,48,384]{2,1,0:T(8,128)S(1)}, u32[]{:S(2)}, u32[]{:S(2)}) collective-permute-start(f32[4,48,384]{2,1,0:T(8,128)S(1)} %get-tuple-element.211), channel_id=1, source_target_pairs={{0,8},{8,0},{16,24},{24,16},{1,9},{9,1},{17,25},{25,17},{2,10},{10... | collective-permute-start | bytes 884744 | tf_op jit(solution)/shard_map/ppermute | solution.py:747
  92.4 28.4 %collective-permute-start.33 = (f32[4,48,384]{2,1,0:T(8,128)S(1)}, f32[4,48,384]{2,1,0:T(8,128)S(1)}, u32[]{:S(2)}, u32[]{:S(2)}) collective-permute-start(f32[4,48,384]{2,1,0:T(8,128)S(1)} %get-tuple-element.212), channel_id=1, source_target_pairs={{0,16},{8,24},{16,0},{24,8},{1,17},{9,25},{17,1},{25,9},{2,18},{10... | collective-permute-start | bytes 884744 | tf_op jit(solution)/shard_map/ppermute | solution.py:747
  93.8 27.0 %collective-permute-start.34 = (f32[4,48,384]{2,1,0:T(8,128)S(1)}, f32[4,48,384]{2,1,0:T(8,128)S(1)}, u32[]{:S(2)}, u32[]{:S(2)}) collective-permute-start(f32[4,48,384]{2,1,0:T(8,128)S(1)} %get-tuple-element.213), channel_id=1, source_target_pairs={{0,24},{8,16},{16,8},{24,0},{1,25},{9,17},{17,9},{25,1},{2,26},{10... | collective-permute-start | bytes 884744 | tf_op jit(solution)/shard_map/ppermute | solution.py:747
  101.8 18.9 %collective-permute-start.29 = (f32[4,48,384]{2,1,0:T(8,128)S(1)}, f32[4,48,384]{2,1,0:T(8,128)S(1)}, u32[]{:S(2)}, u32[]{:S(2)}) collective-permute-start(f32[4,48,384]{2,1,0:T(8,128)S(1)} %get-tuple-element.207), channel_id=1, source_target_pairs={{0,8},{8,0},{16,24},{24,16},{1,9},{9,1},{17,25},{25,17},{2,10},{10... | collective-permute-start | bytes 884744 | tf_op jit(solution)/shard_map/ppermute | solution.py:747
  102.4 18.4 %collective-permute-start.30 = (f32[4,48,384]{2,1,0:T(8,128)S(1)}, f32[4,48,384]{2,1,0:T(8,128)S(1)}, u32[]{:S(2)}, u32[]{:S(2)}) collective-permute-start(f32[4,48,384]{2,1,0:T(8,128)S(1)} %get-tuple-element.208), channel_id=1, source_target_pairs={{0,16},{8,24},{16,0},{24,8},{1,17},{9,25},{17,1},{25,9},{2,18},{10... | collective-permute-start | bytes 884744 | tf_op jit(solution)/shard_map/ppermute | solution.py:747
  103.8 17.0 %collective-permute-start.31 = (f32[4,48,384]{2,1,0:T(8,128)S(1)}, f32[4,48,384]{2,1,0:T(8,128)S(1)}, u32[]{:S(2)}, u32[]{:S(2)}) collective-permute-start(f32[4,48,384]{2,1,0:T(8,128)S(1)} %get-tuple-element.209), channel_id=1, source_target_pairs={{0,24},{8,16},{16,8},{24,0},{1,25},{9,17},{17,9},{25,1},{2,26},{10... | collective-permute-start | bytes 884744 | tf_op jit(solution)/shard_map/ppermute | solution.py:747
  120.8 6.4 %collective-permute-start.35 = (f32[4,4,48,384]{3,2,1,0:T(8,128)S(1)}, f32[4,4,48,384]{3,2,1,0:T(8,128)}, u32[]{:S(2)}, u32[]{:S(2)}) collective-permute-start(f32[4,4,48,384]{3,2,1,0:T(8,128)S(1)} %get-tuple-element.215), channel_id=1, source_target_pairs={{0,1},{1,0},{2,3},{3,2},{4,5},{5,4},{6,7},{7,6},{8,9},{9,8},{10,11... | collective-permute-start | bytes 3538952 | tf_op jit(solution)/shard_map/ppermute | solution.py:741
  128.8 9.9 %collective-permute-start.37 = (f32[4,48,384]{2,1,0:T(8,128)S(1)}, f32[4,48,384]{2,1,0:T(8,128)S(1)}, u32[]{:S(2)}, u32[]{:S(2)}) collective-permute-start(f32[4,48,384]{2,1,0:T(8,128)S(1)} %get-tuple-element.229), channel_id=1, source_target_pairs={{0,8},{8,0},{16,24},{24,16},{1,9},{9,1},{17,25},{25,17},{2,10},{10... | collective-permute-start | bytes 884744 | tf_op jit(solution)/shard_map/ppermute | solution.py:747
  129.4 15.2 %collective-permute-start.38 = (f32[4,48,384]{2,1,0:T(8,128)S(1)}, f32[4,48,384]{2,1,0:T(8,128)S(1)}, u32[]{:S(2)}, u32[]{:S(2)}) collective-permute-start(f32[4,48,384]{2,1,0:T(8,128)S(1)} %get-tuple-element.230), channel_id=1, source_target_pairs={{0,16},{8,24},{16,0},{24,8},{1,17},{9,25},{17,1},{25,9},{2,18},{10... | collective-permute-start | bytes 884744 | tf_op jit(solution)/shard_map/ppermute | solution.py:747
  129.9 14.7 %collective-permute-start.39 = (f32[4,48,384]{2,1,0:T(8,128)S(1)}, f32[4,48,384]{2,1,0:T(8,128)S(1)}, u32[]{:S(2)}, u32[]{:S(2)}) collective-permute-start(f32[4,48,384]{2,1,0:T(8,128)S(1)} %get-tuple-element.231), channel_id=1, source_target_pairs={{0,24},{8,16},{16,8},{24,0},{1,25},{9,17},{17,9},{25,1},{2,26},{10... | collective-permute-start | bytes 884744 | tf_op jit(solution)/shard_map/ppermute | solution.py:747
  132.6 15.4 %collective-permute-start.43 = (f32[112,384]{1,0:T(8,128)S(1)}, f32[112,384]{1,0:T(8,128)S(1)}, u32[]{:S(2)}, u32[]{:S(2)}) collective-permute-start(f32[112,384]{1,0:T(8,128)S(1)} %get-tuple-element.300), channel_id=1, source_target_pairs={{0,2},{1,3},{2,0},{3,1},{4,6},{5,7},{6,4},{7,5},{8,10},{9,11},{10,... | collective-permute-start | bytes 516104 | tf_op jit(solution)/shard_map/ppermute | solution.py:744
  134.0 15.2 %collective-permute-start.44 = (f32[112,384]{1,0:T(8,128)S(1)}, f32[112,384]{1,0:T(8,128)S(1)}, u32[]{:S(2)}, u32[]{:S(2)}) collective-permute-start(f32[112,384]{1,0:T(8,128)S(1)} %get-tuple-element.301), channel_id=1, source_target_pairs={{0,4},{1,5},{2,6},{3,7},{4,0},{5,1},{6,2},{7,3},{8,12},{9,13},{10,... | collective-permute-start | bytes 516104 | tf_op jit(solution)/shard_map/ppermute | solution.py:744
  138.7 10.4 %collective-permute-start.45 = (f32[112,384]{1,0:T(8,128)S(1)}, f32[112,384]{1,0:T(8,128)S(1)}, u32[]{:S(2)}, u32[]{:S(2)}) collective-permute-start(f32[112,384]{1,0:T(8,128)S(1)} %get-tuple-element.302), channel_id=1, source_target_pairs={{0,6},{1,7},{2,4},{3,5},{4,2},{5,3},{6,0},{7,1},{8,14},{9,15},{10,... | collective-permute-start | bytes 516104 | tf_op jit(solution)/shard_map/ppermute | solution.py:744
  144.7 4.9 %collective-permute-start.40 = (f32[48,384]{1,0:T(8,128)S(1)}, f32[48,384]{1,0:T(8,128)S(1)}, u32[]{:S(2)}, u32[]{:S(2)}) collective-permute-start(f32[48,384]{1,0:T(8,128)S(1)} %get-tuple-element.260), channel_id=1, source_target_pairs={{0,2},{1,3},{2,0},{3,1},{4,6},{5,7},{6,4},{7,5},{8,10},{9,11},{10,... | collective-permute-start | bytes 221192 | tf_op jit(solution)/shard_map/ppermute | solution.py:744
  146.0 10.6 %collective-permute-start.41 = (f32[48,384]{1,0:T(8,128)S(1)}, f32[48,384]{1,0:T(8,128)S(1)}, u32[]{:S(2)}, u32[]{:S(2)}) collective-permute-start(f32[48,384]{1,0:T(8,128)S(1)} %get-tuple-element.262), channel_id=1, source_target_pairs={{0,4},{1,5},{2,6},{3,7},{4,0},{5,1},{6,2},{7,3},{8,12},{9,13},{10,... | collective-permute-start | bytes 221192 | tf_op jit(solution)/shard_map/ppermute | solution.py:744
  148.0 8.6 %collective-permute-start.42 = (f32[48,384]{1,0:T(8,128)S(1)}, f32[48,384]{1,0:T(8,128)S(1)}, u32[]{:S(2)}, u32[]{:S(2)}) collective-permute-start(f32[48,384]{1,0:T(8,128)S(1)} %get-tuple-element.261), channel_id=1, source_target_pairs={{0,6},{1,7},{2,4},{3,5},{4,2},{5,3},{6,0},{7,1},{8,14},{9,15},{10,... | collective-permute-start | bytes 221192 | tf_op jit(solution)/shard_map/ppermute | solution.py:744
  156.7 4.7 %collective-permute-start.49 = (f32[48,384]{1,0:T(8,128)S(1)}, f32[48,384]{1,0:T(8,128)S(1)}, u32[]{:S(2)}, u32[]{:S(2)}) collective-permute-start(f32[48,384]{1,0:T(8,128)S(1)} %get-tuple-element.296), channel_id=1, source_target_pairs={{0,8},{8,0},{16,24},{24,16},{1,9},{9,1},{17,25},{25,17},{2,10},{10... | collective-permute-start | bytes 221192 | tf_op jit(solution)/shard_map/ppermute | solution.py:747
  157.8 5.3 %collective-permute-start.51 = (f32[48,384]{1,0:T(8,128)S(1)}, f32[48,384]{1,0:T(8,128)S(1)}, u32[]{:S(2)}, u32[]{:S(2)}) collective-permute-start(f32[48,384]{1,0:T(8,128)S(1)} %get-tuple-element.258), channel_id=1, source_target_pairs={{0,24},{8,16},{16,8},{24,0},{1,25},{9,17},{17,9},{25,1},{2,26},{10... | collective-permute-start | bytes 221192 | tf_op jit(solution)/shard_map/ppermute | solution.py:747
  167.8 6.4 %collective-permute-start.54 = (f32[96,128]{1,0:T(8,128)S(1)}, f32[96,128]{1,0:T(8,128)S(1)}, u32[]{:S(2)}, u32[]{:S(2)}) collective-permute-start(f32[96,128]{1,0:T(8,128)S(1)} %get-tuple-element.297), channel_id=1, source_target_pairs={{0,4},{1,5},{2,6},{3,7},{4,0},{5,1},{6,2},{7,3},{8,12},{9,13},{10,... | collective-permute-start | bytes 147464 | tf_op jit(solution)/shard_map/ppermute | solution.py:744
  169.6 5.9 %collective-permute-start.55 = (f32[96,128]{1,0:T(8,128)S(1)}, f32[96,128]{1,0:T(8,128)S(1)}, u32[]{:S(2)}, u32[]{:S(2)}) collective-permute-start(f32[96,128]{1,0:T(8,128)S(1)} %get-tuple-element.298), channel_id=1, source_target_pairs={{0,6},{1,7},{2,4},{3,5},{4,2},{5,3},{6,0},{7,1},{8,14},{9,15},{10,... | collective-permute-start | bytes 147464 | tf_op jit(solution)/shard_map/ppermute | solution.py:744
  175.5 7.5 %collective-permute-start.56 = (f32[96,128]{1,0:T(8,128)S(1)}, f32[96,128]{1,0:T(8,128)S(1)}, u32[]{:S(2)}, u32[]{:S(2)}) collective-permute-start(f32[96,128]{1,0:T(8,128)S(1)} %fusion.26), channel_id=1, source_target_pairs={{0,2},{1,3},{2,0},{3,1},{4,6},{5,7},{6,4},{7,5},{8,10},{9,11},{10,... | collective-permute-start | bytes 147464 | tf_op jit(solution)/shard_map/ppermute | solution.py:744
  175.6 7.9 %collective-permute-start.57 = (f32[96,128]{1,0:T(8,128)S(1)}, f32[96,128]{1,0:T(8,128)S(1)}, u32[]{:S(2)}, u32[]{:S(2)}) collective-permute-start(f32[96,128]{1,0:T(8,128)S(1)} %fusion.26), channel_id=1, source_target_pairs={{0,4},{1,5},{2,6},{3,7},{4,0},{5,1},{6,2},{7,3},{8,12},{9,13},{10,... | collective-permute-start | bytes 147464 | tf_op jit(solution)/shard_map/ppermute | solution.py:744
  177.9 5.9 %collective-permute-start.58 = (f32[96,128]{1,0:T(8,128)S(1)}, f32[96,128]{1,0:T(8,128)S(1)}, u32[]{:S(2)}, u32[]{:S(2)}) collective-permute-start(f32[96,128]{1,0:T(8,128)S(1)} %fusion.26), channel_id=1, source_target_pairs={{0,6},{1,7},{2,4},{3,5},{4,2},{5,3},{6,0},{7,1},{8,14},{9,15},{10,... | collective-permute-start | bytes 147464 | tf_op jit(solution)/shard_map/ppermute | solution.py:744
  180.0 20.7 %collective-permute-start.46 = (f32[160,384]{1,0:T(8,128)S(1)}, f32[160,384]{1,0:T(8,128)S(1)}, u32[]{:S(2)}, u32[]{:S(2)}) collective-permute-start(f32[160,384]{1,0:T(8,128)S(1)} %pad_maximum_fusion.7.refs_0_), channel_id=1, source_target_pairs={{0,8},{8,0},{16,24},{24,16},{1,9},{9,1},{17,25},{25,17},{2,10},{10... | collective-permute-start | bytes 737288 | tf_op jit(solution)/shard_map/ppermute | solution.py:747
  181.5 19.2 %collective-permute-start.47 = (f32[160,384]{1,0:T(8,128)S(1)}, f32[160,384]{1,0:T(8,128)S(1)}, u32[]{:S(2)}, u32[]{:S(2)}) collective-permute-start(f32[160,384]{1,0:T(8,128)S(1)} %pad_maximum_fusion.7.refs_0_), channel_id=1, source_target_pairs={{0,16},{8,24},{16,0},{24,8},{1,17},{9,25},{17,1},{25,9},{2,18},{10... | collective-permute-start | bytes 737288 | tf_op jit(solution)/shard_map/ppermute | solution.py:747
  183.0 17.7 %collective-permute-start.48 = (f32[160,384]{1,0:T(8,128)S(1)}, f32[160,384]{1,0:T(8,128)S(1)}, u32[]{:S(2)}, u32[]{:S(2)}) collective-permute-start(f32[160,384]{1,0:T(8,128)S(1)} %pad_maximum_fusion.7.refs_0_), channel_id=1, source_target_pairs={{0,24},{8,16},{16,8},{24,0},{1,25},{9,17},{17,9},{25,1},{2,26},{10... | collective-permute-start | bytes 737288 | tf_op jit(solution)/shard_map/ppermute | solution.py:747
  200.7 9.9 %collective-permute-start.60 = (f32[192,384]{1,0:T(8,128)S(1)}, f32[192,384]{1,0:T(8,128)S(1)}, u32[]{:S(2)}, u32[]{:S(2)}) collective-permute-start(f32[192,384]{1,0:T(8,128)S(1)} %shard_map.271.one), channel_id=1, source_target_pairs={{0,8},{8,0},{16,24},{24,16},{1,9},{9,1},{17,25},{25,17},{2,10},{10... | collective-permute-start | bytes 884744 | tf_op jit(solution)/shard_map/ppermute | solution.py:747
  202.3 15.1 %collective-permute-start.61 = (f32[192,384]{1,0:T(8,128)S(1)}, f32[192,384]{1,0:T(8,128)S(1)}, u32[]{:S(2)}, u32[]{:S(2)}) collective-permute-start(f32[192,384]{1,0:T(8,128)S(1)} %shard_map.271.one), channel_id=1, source_target_pairs={{0,16},{8,24},{16,0},{24,8},{1,17},{9,25},{17,1},{25,9},{2,18},{10... | collective-permute-start | bytes 884744 | tf_op jit(solution)/shard_map/ppermute | solution.py:747
  203.8 13.6 %collective-permute-start.62 = (f32[192,384]{1,0:T(8,128)S(1)}, f32[192,384]{1,0:T(8,128)S(1)}, u32[]{:S(2)}, u32[]{:S(2)}) collective-permute-start(f32[192,384]{1,0:T(8,128)S(1)} %shard_map.271.one), channel_id=1, source_target_pairs={{0,24},{8,16},{16,8},{24,0},{1,25},{9,17},{17,9},{25,1},{2,26},{10... | collective-permute-start | bytes 884744 | tf_op jit(solution)/shard_map/ppermute | solution.py:747
  (48 other events, 273.1 us)

commit v4 on v3

--- a/solution.py
+++ b/solution.py
@@ -658,27 +658,39 @@
     )(scalars, mine, other, own)[0]
 
 
-def first_message_kernel(replica, qkv, out, vectors, message):
-    piece = message.shape[0] - 8
+def first_message_kernel(replica, qkv, out, vectors, message, rows, arrived):
+    piece = out.shape[0]
     width = vectors.shape[1]
+    small = pltpu.make_async_copy(vectors, rows, arrived.at[1])
+    small.start()
 
     @pl.when(replica[0] < 3)
     def _():
-        message[:piece, :] = qkv[pl.ds(pl.multiple_of(replica[0] * piece, 8), piece), :]
+        source = qkv.at[pl.ds(pl.multiple_of(replica[0] * piece, piece), piece), :]
+        copy = pltpu.make_async_copy(source, message.at[pl.ds(0, piece), :], arrived.at[0])
+        copy.start()
+        copy.wait()
 
     @pl.when(replica[0] == 3)
     def _():
-        message[:piece, :] = out[...]
-
+        copy = pltpu.make_async_copy(out, message.at[pl.ds(0, piece), :], arrived.at[0])
+        copy.start()
+        copy.wait()
+
+    small.wait()
     message[piece:, :] = jnp.zeros((8, D), f32)
-    message[piece:, :width] = vectors[:8, :]
-    message[piece : piece + 4, width : 2 * width] = vectors[8:, :]
+    message[piece:, :width] = rows[:8, :]
+    message[piece : piece + 4, width : 2 * width] = rows[8:, :]
 
 
 def first_message(replica, qkv, out, vectors):
-    return call(
-        first_message_kernel, [((out.shape[0] + 8, D), f32)], flops=10**6, data=1 << 16
-    )(replica, qkv, out, vectors)[0]
+    return pl.pallas_call(
+        first_message_kernel,
+        out_shape=jax.ShapeDtypeStruct((out.shape[0] + 8, D), f32),
+        in_specs=[SMEM] + [pl.BlockSpec(memory_space=pltpu.HBM)] * 3,
+        out_specs=VMEM,
+        scratch_shapes=[pltpu.VMEM(vectors.shape, f32), pltpu.SemaphoreType.DMA((2,))],
+    )(replica, qkv, out, vectors)
 
 
 def hand_out_kernel(scalars, one, two, three, four, *outs):

time: 219 us -> 219 us (level)
    pallas_call x14 -> x13, Pallas kernels: 75.1 us -> 75 us  [run(): pl.pallas_call(body, out_shape=[jax.ShapeDtypeStruct(s, t) for s, t in ou...]
where the time goes in v4:
time: 219 us
  Pallas kernels  76.6 us (35%)
  starting transfers between devices  75.2 us (34%)
  waiting for transfers between devices  55.1 us (25%)
  other arithmetic  5.81 us (3%)
  local copies, waits for them, and re-layouts  4.14 us (2%)
  between operations  2.27 us (1%)
    pallas_call x13, Pallas kernels, run(): pl.pallas_call(body, out_shape=[jax.ShapeDtypeStruct(s, t) for s, t in ou...  75 us
    ppermute x21, starting transfers between devices, hop(): lax.ppermute(x, 'group', [(i, i ^ 2 * by) for i in range(group_size)])  37.8 us
    ppermute x23, starting transfers between devices, cross(): return lax.ppermute(x, 'replica', [(i, i ^ by) for i in range(replicas)])  26.9 us
    ppermute x23, waiting for transfers between devices, cross(): return lax.ppermute(x, 'replica', [(i, i ^ by) for i in range(replicas)])  22.8 us
    ppermute x21, waiting for transfers between devices, hop(): lax.ppermute(x, 'group', [(i, i ^ 2 * by) for i in range(group_size)])  19.8 us
    ppermute x17, waiting for transfers between devices, swap(): return lax.ppermute(x, 'group', [(i, i ^ 1) for i in range(group_size)])  12.5 us
    ppermute x17, starting transfers between devices, swap(): return lax.ppermute(x, 'group', [(i, i ^ 1) for i in range(group_size)])  9.2 us
  transfers between devices with their start and end apart: 63, of which 29 were waited for; matrix products, arithmetic and copies ran while one was open for 3% of the time, Pallas kernels for 28%

profile of v4, /device:TPU:0, one launch (start us, length us, event | category | flops | bytes accessed | tf_op | source)
XLA Modules:
  0.0 219.1 jit_solution(13122157317384524827)
XLA Ops:
  0.7 1.6 shard_map.260
  2.3 3.1 %collective-permute-start = (f32[56,384]{1,0:T(8,128)}, f32[56,384]{1,0:T(8,128)S(1)}, u32[]{:S(2)}, u32[]{:S(2)}) collective-permute-start(f32[56,384]{1,0:T(8,128)} %shard_map.260), channel_id=1, source_target_pairs={{0,2},{1,3},{2,0},{3,1},{4,6},{5,7},{6,4},{7,5},{8,10},{9,11},{10,... | collective-permute-start | bytes 258056 | tf_op jit(solution)/shard_map/ppermute | solution.py:756
  5.4 2.6 %collective-permute-start.1 = (f32[56,384]{1,0:T(8,128)}, f32[56,384]{1,0:T(8,128)S(1)}, u32[]{:S(2)}, u32[]{:S(2)}) collective-permute-start(f32[56,384]{1,0:T(8,128)} %shard_map.260), channel_id=1, source_target_pairs={{0,4},{1,5},{2,6},{3,7},{4,0},{5,1},{6,2},{7,3},{8,12},{9,13},{10,... | collective-permute-start | bytes 258056 | tf_op jit(solution)/shard_map/ppermute | solution.py:756
  11.4 3.8 %collective-permute-done.1 = f32[56,384]{1,0:T(8,128)S(1)} collective-permute-done((f32[56,384]{1,0:T(8,128)}, f32[56,384]{1,0:T(8,128)S(1)}, u32[]{:S(2)}, u32[]{:S(2)}) %collective-permute-start.1) | collective-permute-done | bytes 86048 | tf_op jit(solution)/shard_map/ppermute | solution.py:756
  15.4 2.7 %collective-permute-start.8 = (f32[192,384]{1,0:T(8,128)S(1)}, f32[192,384]{1,0:T(8,128)S(1)}, u32[]{:S(2)}, u32[]{:S(2)}) collective-permute-start(f32[192,384]{1,0:T(8,128)S(1)} %pad_maximum_fusion.6.refs_0_), channel_id=1, source_target_pairs={{0,1},{1,0},{2,3},{3,2},{4,5},{5,4},{6,7},{7,6},{8,9},{9,8},{10,11... | collective-permute-start | bytes 884744 | tf_op jit(solution)/shard_map/ppermute | solution.py:753
  18.1 1.6 collective-permute-start.5
  19.7 1.5 collective-permute-start.6
  23.0 1.6 collective-permute-start.10
  24.6 2.1 collective-permute-start.11
  28.0 3.1 %collective-permute-start.12 = (f32[96,384]{1,0:T(8,128)S(1)}, f32[96,384]{1,0:T(8,128)S(1)}, u32[]{:S(2)}, u32[]{:S(2)}) collective-permute-start(f32[96,384]{1,0:T(8,128)S(1)} %pad_maximum_fusion.11), channel_id=1, source_target_pairs={{0,6},{1,7},{2,4},{3,5},{4,2},{5,3},{6,0},{7,1},{8,14},{9,15},{10,... | collective-permute-start | bytes 442376 | tf_op jit(solution)/shard_map/ppermute | solution.py:756
  31.1 3.6 %collective-permute-done.6.refs_2_ = f32[192,384]{1,0:T(8,128)S(1)} collective-permute-done((f32[192,384]{1,0:T(8,128)S(1)}, f32[192,384]{1,0:T(8,128)S(1)}, u32[]{:S(2)}, u32[]{:S(2)}) %collective-permute-start.6) | collective-permute-done | bytes 294944 | tf_op jit(solution)/shard_map/ppermute | solution.py:759
  34.7 3.3 %collective-permute-done.11 = f32[96,384]{1,0:T(8,128)S(1)} collective-permute-done((f32[96,384]{1,0:T(8,128)S(1)}, f32[96,384]{1,0:T(8,128)S(1)}, u32[]{:S(2)}, u32[]{:S(2)}) %collective-permute-start.11) | collective-permute-done | bytes 147488 | tf_op jit(solution)/shard_map/ppermute | solution.py:756
  40.4 1.5 collective-permute-start.16
  41.9 1.5 collective-permute-start.17
  43.4 3.2 %collective-permute-start.18 = (f32[96,384]{1,0:T(8,128)S(1)}, f32[96,384]{1,0:T(8,128)S(1)}, u32[]{:S(2)}, u32[]{:S(2)}) collective-permute-start(f32[96,384]{1,0:T(8,128)S(1)} %pad_maximum_fusion.10), channel_id=1, source_target_pairs={{0,2},{1,3},{2,0},{3,1},{4,6},{5,7},{6,4},{7,5},{8,10},{9,11},{10,... | collective-permute-start | bytes 442376 | tf_op jit(solution)/shard_map/ppermute | solution.py:756
  50.3 13.6 %shard_map.262 = (bf16[4,6,208,128]{3,2,1,0:T(8,128)(2,1)S(1)}, bf16[4,6,128,208]{3,2,1,0:T(8,128)(2,1)S(1)}, bf16[4,6,208,128]{3,2,1,0:T(8,128)(2,1)S(1)}, bf16...) custom-call(s32[6]{0:T(128)S(1)} %stack.39.scalars, ...), custom_call_target="tpu_custom_call" | custom-call | flops 100000000 | bytes 262144 | tf_op jit(solution)/shard_map/pallas_call | solution.py:43
  69.7 10.4 %shard_map.264 = (f32[512,384]{1,0:T(8,128)}, f32[512,1536]{1,0:T(8,128)S(1)}, bf16[512,1152]{1,0:T(8,128)(2,1)S(1)}, bf16[512,1152]{1,0:T(8,128)(2,1)S(1)}, f32...) custom-call(s32[6]{0:T(128)S(1)} %stack.39.scalars, ...), custom_call_target="tpu_custom_call" | custom-call | flops 100000000 | bytes 262144 | tf_op jit(solution)/shard_map/pallas_call | solution.py:43
  80.3 8.7 %shard_map.265 = (f32[512,384]{1,0:T(8,128)S(1)}, f32[16,384]{1,0:T(8,128)S(1)}, f32[4,48,384]{2,1,0:T(8,128)S(1)}, f32[4,48,384]{2,1,0:T(8,128)S(1)}, f32[4,48,...) custom-call(s32[6]{0:T(128)S(1)} %stack.39.scalars, ...), custom_call_target="tpu_custom_call" | custom-call | flops 100000000 | bytes 262144 | tf_op jit(solution)/shard_map/pallas_call | solution.py:43
  93.2 1.6 collective-permute-start.34
  94.7 5.6 %shard_map.266.some = f32[2,208,1152]{2,1,0:T(8,128)S(1)} custom-call(s32[6]{0:T(128)S(1)} %stack.39.scalars, f32[200,384]{1,0:T(8,128)S(1)} %collective-permute-done.27.lower, f32[512,384]{1,0:T(8,128)S(1)} %get-tuple-element.192.own.d_mid, f32[200,384]{1,0:T(8,128)S(1)} %collective-permute-done.28.upper, bf16[1536,1152]{1,0:T(8,128)(2,1)S(1)} %get-tuple-element.157.w, ...), custom_call_target="tpu_custom_call" | custom-call | flops 100000000 | bytes 262144 | tf_op jit(solution)/shard_map/pallas_call | solution.py:43
  103.9 1.6 collective-permute-start.31
  105.5 5.6 %shard_map.267.more = f32[2,208,1152]{2,1,0:T(8,128)S(1)} custom-call(s32[6]{0:T(128)S(1)} %stack.39.scalars, f32[200,384]{1,0:T(8,128)S(1)} %collective-permute-done.27.lower, f32[512,384]{1,0:T(8,128)S(1)} %get-tuple-element.192.own.d_mid, f32[200,384]{1,0:T(8,128)S(1)} %collective-permute-done.28.upper, bf16[1536,1152]{1,0:T(8,128)(2,1)S(1)} %get-tuple-element.157.w, ...), custom_call_target="tpu_custom_call" | custom-call | flops 100000000 | bytes 262144 | tf_op jit(solution)/shard_map/pallas_call | solution.py:43
  111.1 6.1 %shard_map.268 = (f32[4,48,384]{2,1,0:T(8,128)S(1)}, f32[4,48,384]{2,1,0:T(8,128)S(1)}, f32[4,48,384]{2,1,0:T(8,128)S(1)}, f32[4,48,384]{2,1,0:T(8,128)S(1)}, f3...) custom-call(s32[6]{0:T(128)S(1)} %stack.39.scalars, ...), custom_call_target="tpu_custom_call" | custom-call | flops 100000000 | bytes 262144 | tf_op jit(solution)/shard_map/pallas_call | solution.py:43
  117.3 3.5 %shard_map.269 = (f32[512,384]{1,0:T(8,128)}, f32[16,384]{1,0:T(8,128)S(1)}) custom-call(s32[6]{0:T(128)S(1)} %stack.39.scalars, bf16[512,1152]{1,0:T(8,128)(2,1)S(1)} %get-tuple-element.195.d_hi, bf16[512,1152]{1,0:T(8,128)(2,1)S(1)} %get-tuple-element.196.d_lo, bf16[1536,1152]{1,0:T(8,128)(2,1)S(1)} %get-tuple-element.157.w, f32[512,384]{1,0:T(8,128)S(1)} %copy-done, ...), custom_call_target="tpu_custom_call" | custom-call | flops 100000000 | bytes 262144 | tf_op jit(solution)/shard_map/pallas_call | solution.py:43
  120.9 3.7 %collective-permute-start.35 = (f32[4,4,48,384]{3,2,1,0:T(8,128)S(1)}, f32[4,4,48,384]{3,2,1,0:T(8,128)}, u32[]{:S(2)}, u32[]{:S(2)}) collective-permute-start(f32[4,4,48,384]{3,2,1,0:T(8,128)S(1)} %get-tuple-element.215), channel_id=1, source_target_pairs={{0,1},{1,0},{2,3},{3,2},{4,5},{5,4},{6,7},{7,6},{8,9},{9,8},{10,11... | collective-permute-start | bytes 3538952 | tf_op jit(solution)/shard_map/ppermute | solution.py:753
  124.9 2.1 collective-permute-done.36
  127.3 1.5 fusion
  130.0 2.4 %collective-permute-start.39 = (f32[4,48,384]{2,1,0:T(8,128)S(1)}, f32[4,48,384]{2,1,0:T(8,128)S(1)}, u32[]{:S(2)}, u32[]{:S(2)}) collective-permute-start(f32[4,48,384]{2,1,0:T(8,128)S(1)} %get-tuple-element.231), channel_id=1, source_target_pairs={{0,24},{8,16},{16,8},{24,0},{1,25},{9,17},{17,9},{25,1},{2,26},{10... | collective-permute-start | bytes 884744 | tf_op jit(solution)/shard_map/ppermute | solution.py:759
  134.1 2.0 collective-permute-start.44
  136.1 2.7 %collective-permute-done.37 = f32[4,48,384]{2,1,0:T(8,128)S(1)} collective-permute-done((f32[4,48,384]{2,1,0:T(8,128)S(1)}, f32[4,48,384]{2,1,0:T(8,128)S(1)}, u32[]{:S(2)}, u32[]{:S(2)}) %collective-permute-start.37) | collective-permute-done | bytes 294944 | tf_op jit(solution)/shard_map/ppermute | solution.py:759
  138.8 2.8 %collective-permute-start.45 = (f32[112,384]{1,0:T(8,128)S(1)}, f32[112,384]{1,0:T(8,128)S(1)}, u32[]{:S(2)}, u32[]{:S(2)}) collective-permute-start(f32[112,384]{1,0:T(8,128)S(1)} %get-tuple-element.302), channel_id=1, source_target_pairs={{0,6},{1,7},{2,4},{3,5},{4,2},{5,3},{6,0},{7,1},{8,14},{9,15},{10,... | collective-permute-start | bytes 516104 | tf_op jit(solution)/shard_map/ppermute | solution.py:756
  141.5 3.1 %collective-permute-done.38 = f32[4,48,384]{2,1,0:T(8,128)S(1)} collective-permute-done((f32[4,48,384]{2,1,0:T(8,128)S(1)}, f32[4,48,384]{2,1,0:T(8,128)S(1)}, u32[]{:S(2)}, u32[]{:S(2)}) %collective-permute-start.38) | collective-permute-done | bytes 294944 | tf_op jit(solution)/shard_map/ppermute | solution.py:759
  146.1 2.0 collective-permute-start.41
  149.7 7.2 %collective-permute-done.41 = f32[48,384]{1,0:T(8,128)S(1)} collective-permute-done((f32[48,384]{1,0:T(8,128)S(1)}, f32[48,384]{1,0:T(8,128)S(1)}, u32[]{:S(2)}, u32[]{:S(2)}) %collective-permute-start.41) | collective-permute-done | bytes 73760 | tf_op jit(solution)/shard_map/ppermute | solution.py:756
  158.1 2.4 %collective-permute-start.51 = (f32[48,384]{1,0:T(8,128)S(1)}, f32[48,384]{1,0:T(8,128)S(1)}, u32[]{:S(2)}, u32[]{:S(2)}) collective-permute-start(f32[48,384]{1,0:T(8,128)S(1)} %get-tuple-element.258), channel_id=1, source_target_pairs={{0,24},{8,16},{16,8},{24,0},{1,25},{9,17},{17,9},{25,1},{2,26},{10... | collective-permute-start | bytes 221192 | tf_op jit(solution)/shard_map/ppermute | solution.py:759
  166.3 1.6 collective-permute-start.53
  167.9 1.7 collective-permute-start.54
  170.8 3.5 %collective-permute-done.54 = f32[96,128]{1,0:T(8,128)S(1)} collective-permute-done((f32[96,128]{1,0:T(8,128)S(1)}, f32[96,128]{1,0:T(8,128)S(1)}, u32[]{:S(2)}, u32[]{:S(2)}) %collective-permute-start.54) | collective-permute-done | bytes 49184 | tf_op jit(solution)/shard_map/ppermute | solution.py:756
  175.7 2.4 %collective-permute-start.57 = (f32[96,128]{1,0:T(8,128)S(1)}, f32[96,128]{1,0:T(8,128)S(1)}, u32[]{:S(2)}, u32[]{:S(2)}) collective-permute-start(f32[96,128]{1,0:T(8,128)S(1)} %fusion.26), channel_id=1, source_target_pairs={{0,4},{1,5},{2,6},{3,7},{4,0},{5,1},{6,2},{7,3},{8,12},{9,13},{10,... | collective-permute-start | bytes 147464 | tf_op jit(solution)/shard_map/ppermute | solution.py:756
  178.0 2.0 collective-permute-start.58
  180.0 1.6 collective-permute-start.46
  181.6 1.5 collective-permute-start.47
  185.4 15.3 %shard_map.271.one = f32[192,384]{1,0:T(8,128)S(1)} custom-call(s32[6]{0:T(128)S(1)} %stack.39.scalars, f32[4,96,128]{2,1,0:T(8,128)S(1)} %pad_maximum_fusion.9.mine, f32[4,96,128]{2,1,0:T(8,128)S(1)} %collective-permute-done.59.other, f32[192,384]{1,0:T(8,128)S(1)} %get-tuple-element.243.own), custom_call_target="tpu_custom_call" | custom-call | flops 100000000 | bytes 262144 | tf_op jit(solution)/shard_map/pallas_call | solution.py:43
  200.8 1.6 collective-permute-start.60
  202.4 1.5 collective-permute-start.61
  208.3 2.4 %collective-permute-done.60.two = f32[192,384]{1,0:T(8,128)S(1)} collective-permute-done((f32[192,384]{1,0:T(8,128)S(1)}, f32[192,384]{1,0:T(8,128)S(1)}, u32[]{:S(2)}, u32[]{:S(2)}) %collective-permute-start.60) | collective-permute-done | bytes 294944 | tf_op jit(solution)/shard_map/ppermute | solution.py:759
  210.7 6.8 %collective-permute-done.61.three = f32[192,384]{1,0:T(8,128)S(1)} collective-permute-done((f32[192,384]{1,0:T(8,128)S(1)}, f32[192,384]{1,0:T(8,128)S(1)}, u32[]{:S(2)}, u32[]{:S(2)}) %collective-permute-start.61) | collective-permute-done | bytes 294944 | tf_op jit(solution)/shard_map/ppermute | solution.py:759
  217.5 1.6 shard_map.273
  (203 shorter events, 47.7 us)
Async XLA Ops:
  2.3 9.1 %collective-permute-start = (f32[56,384]{1,0:T(8,128)}, f32[56,384]{1,0:T(8,128)S(1)}, u32[]{:S(2)}, u32[]{:S(2)}) collective-permute-start(f32[56,384]{1,0:T(8,128)} %shard_map.260), channel_id=1, source_target_pairs={{0,2},{1,3},{2,0},{3,1},{4,6},{5,7},{6,4},{7,5},{8,10},{9,11},{10,... | collective-permute-start | bytes 258056 | tf_op jit(solution)/shard_map/ppermute | solution.py:756
  5.4 9.8 %collective-permute-start.1 = (f32[56,384]{1,0:T(8,128)}, f32[56,384]{1,0:T(8,128)S(1)}, u32[]{:S(2)}, u32[]{:S(2)}) collective-permute-start(f32[56,384]{1,0:T(8,128)} %shard_map.260), channel_id=1, source_target_pairs={{0,4},{1,5},{2,6},{3,7},{4,0},{5,1},{6,2},{7,3},{8,12},{9,13},{10,... | collective-permute-start | bytes 258056 | tf_op jit(solution)/shard_map/ppermute | solution.py:756
  8.0 7.3 %collective-permute-start.2 = (f32[56,384]{1,0:T(8,128)}, f32[56,384]{1,0:T(8,128)S(1)}, u32[]{:S(2)}, u32[]{:S(2)}) collective-permute-start(f32[56,384]{1,0:T(8,128)} %shard_map.260), channel_id=1, source_target_pairs={{0,6},{1,7},{2,4},{3,5},{4,2},{5,3},{6,0},{7,1},{8,14},{9,15},{10,... | collective-permute-start | bytes 258056 | tf_op jit(solution)/shard_map/ppermute | solution.py:756
  9.2 6.2 %collective-permute-start.3 = (f32[200,384]{1,0:T(8,128)S(1)}, f32[200,384]{1,0:T(8,128)S(1)}, u32[]{:S(2)}, u32[]{:S(2)}) collective-permute-start(f32[200,384]{1,0:T(8,128)S(1)} %get-tuple-element.290), channel_id=1, source_target_pairs={{0,1},{1,0},{2,3},{3,2},{4,5},{5,4},{6,7},{7,6},{8,9},{9,8},{10,11... | collective-permute-start | bytes 921608 | tf_op jit(solution)/shard_map/ppermute | solution.py:753
  9.2 6.1 %collective-permute-start.4 = (f32[200,384]{1,0:T(8,128)S(1)}, f32[200,384]{1,0:T(8,128)S(1)}, u32[]{:S(2)}, u32[]{:S(2)}) collective-permute-start(f32[200,384]{1,0:T(8,128)S(1)} %get-tuple-element.289), channel_id=1, source_target_pairs={{1,2},{3,4},{5,6},{2,1},{4,3},{6,5},{9,10},{11,12},{13,14},{10,9},... | collective-permute-start | bytes 921608 | tf_op jit(solution)/shard_map/ppermute | solution.py:766
  15.4 7.6 %collective-permute-start.8 = (f32[192,384]{1,0:T(8,128)S(1)}, f32[192,384]{1,0:T(8,128)S(1)}, u32[]{:S(2)}, u32[]{:S(2)}) collective-permute-start(f32[192,384]{1,0:T(8,128)S(1)} %pad_maximum_fusion.6.refs_0_), channel_id=1, source_target_pairs={{0,1},{1,0},{2,3},{3,2},{4,5},{5,4},{6,7},{7,6},{8,9},{9,8},{10,11... | collective-permute-start | bytes 884744 | tf_op jit(solution)/shard_map/ppermute | solution.py:753
  18.1 9.9 %collective-permute-start.5 = (f32[192,384]{1,0:T(8,128)S(1)}, f32[192,384]{1,0:T(8,128)S(1)}, u32[]{:S(2)}, u32[]{:S(2)}) collective-permute-start(f32[192,384]{1,0:T(8,128)S(1)} %pad_maximum_fusion.6.refs_0_), channel_id=1, source_target_pairs={{0,8},{8,0},{16,24},{24,16},{1,9},{9,1},{17,25},{25,17},{2,10},{10... | collective-permute-start | bytes 884744 | tf_op jit(solution)/shard_map/ppermute | solution.py:759
  19.7 15.0 %collective-permute-start.6 = (f32[192,384]{1,0:T(8,128)S(1)}, f32[192,384]{1,0:T(8,128)S(1)}, u32[]{:S(2)}, u32[]{:S(2)}) collective-permute-start(f32[192,384]{1,0:T(8,128)S(1)} %pad_maximum_fusion.6.refs_0_), channel_id=1, source_target_pairs={{0,16},{8,24},{16,0},{24,8},{1,17},{9,25},{17,1},{25,9},{2,18},{10... | collective-permute-start | bytes 884744 | tf_op jit(solution)/shard_map/ppermute | solution.py:759
  21.2 13.4 %collective-permute-start.7 = (f32[192,384]{1,0:T(8,128)S(1)}, f32[192,384]{1,0:T(8,128)S(1)}, u32[]{:S(2)}, u32[]{:S(2)}) collective-permute-start(f32[192,384]{1,0:T(8,128)S(1)} %pad_maximum_fusion.6.refs_0_), channel_id=1, source_target_pairs={{0,24},{8,16},{16,8},{24,0},{1,25},{9,17},{17,9},{25,1},{2,26},{10... | collective-permute-start | bytes 884744 | tf_op jit(solution)/shard_map/ppermute | solution.py:759
  23.0 11.7 %collective-permute-start.10 = (f32[96,384]{1,0:T(8,128)S(1)}, f32[96,384]{1,0:T(8,128)S(1)}, u32[]{:S(2)}, u32[]{:S(2)}) collective-permute-start(f32[96,384]{1,0:T(8,128)S(1)} %pad_maximum_fusion.11), channel_id=1, source_target_pairs={{0,2},{1,3},{2,0},{3,1},{4,6},{5,7},{6,4},{7,5},{8,10},{9,11},{10,... | collective-permute-start | bytes 442376 | tf_op jit(solution)/shard_map/ppermute | solution.py:756
  24.6 13.4 %collective-permute-start.11 = (f32[96,384]{1,0:T(8,128)S(1)}, f32[96,384]{1,0:T(8,128)S(1)}, u32[]{:S(2)}, u32[]{:S(2)}) collective-permute-start(f32[96,384]{1,0:T(8,128)S(1)} %pad_maximum_fusion.11), channel_id=1, source_target_pairs={{0,4},{1,5},{2,6},{3,7},{4,0},{5,1},{6,2},{7,3},{8,12},{9,13},{10,... | collective-permute-start | bytes 442376 | tf_op jit(solution)/shard_map/ppermute | solution.py:756
  28.0 10.0 %collective-permute-start.12 = (f32[96,384]{1,0:T(8,128)S(1)}, f32[96,384]{1,0:T(8,128)S(1)}, u32[]{:S(2)}, u32[]{:S(2)}) collective-permute-start(f32[96,384]{1,0:T(8,128)S(1)} %pad_maximum_fusion.11), channel_id=1, source_target_pairs={{0,6},{1,7},{2,4},{3,5},{4,2},{5,3},{6,0},{7,1},{8,14},{9,15},{10,... | collective-permute-start | bytes 442376 | tf_op jit(solution)/shard_map/ppermute | solution.py:756
  40.4 23.6 %collective-permute-start.16 = (f32[384,384]{1,0:T(8,128)S(1)}, f32[384,384]{1,0:T(8,128)S(1)}, u32[]{:S(2)}, u32[]{:S(2)}) collective-permute-start(f32[384,384]{1,0:T(8,128)S(1)} %pad_maximum_fusion.1.refs_0_), channel_id=1, source_target_pairs={{0,8},{8,0},{16,24},{24,16},{1,9},{9,1},{17,25},{25,17},{2,10},{10... | collective-permute-start | bytes 1769480 | tf_op jit(solution)/shard_map/ppermute | solution.py:759
  41.9 22.1 %collective-permute-start.17 = (f32[384,384]{1,0:T(8,128)S(1)}, f32[384,384]{1,0:T(8,128)S(1)}, u32[]{:S(2)}, u32[]{:S(2)}) collective-permute-start(f32[384,384]{1,0:T(8,128)S(1)} %pad_maximum_fusion.1.refs_0_), channel_id=1, source_target_pairs={{0,16},{8,24},{16,0},{24,8},{1,17},{9,25},{17,1},{25,9},{2,18},{10... | collective-permute-start | bytes 1769480 | tf_op jit(solution)/shard_map/ppermute | solution.py:759
  43.4 20.5 %collective-permute-start.18 = (f32[96,384]{1,0:T(8,128)S(1)}, f32[96,384]{1,0:T(8,128)S(1)}, u32[]{:S(2)}, u32[]{:S(2)}) collective-permute-start(f32[96,384]{1,0:T(8,128)S(1)} %pad_maximum_fusion.10), channel_id=1, source_target_pairs={{0,2},{1,3},{2,0},{3,1},{4,6},{5,7},{6,4},{7,5},{8,10},{9,11},{10,... | collective-permute-start | bytes 442376 | tf_op jit(solution)/shard_map/ppermute | solution.py:756
  46.7 17.4 %collective-permute-start.19 = (f32[96,384]{1,0:T(8,128)S(1)}, f32[96,384]{1,0:T(8,128)S(1)}, u32[]{:S(2)}, u32[]{:S(2)}) collective-permute-start(f32[96,384]{1,0:T(8,128)S(1)} %pad_maximum_fusion.10), channel_id=1, source_target_pairs={{0,4},{1,5},{2,6},{3,7},{4,0},{5,1},{6,2},{7,3},{8,12},{9,13},{10,... | collective-permute-start | bytes 442376 | tf_op jit(solution)/shard_map/ppermute | solution.py:756
  47.8 16.2 %collective-permute-start.20 = (f32[96,384]{1,0:T(8,128)S(1)}, f32[96,384]{1,0:T(8,128)S(1)}, u32[]{:S(2)}, u32[]{:S(2)}) collective-permute-start(f32[96,384]{1,0:T(8,128)S(1)} %pad_maximum_fusion.10), channel_id=1, source_target_pairs={{0,6},{1,7},{2,4},{3,5},{4,2},{5,3},{6,0},{7,1},{8,14},{9,15},{10,... | collective-permute-start | bytes 442376 | tf_op jit(solution)/shard_map/ppermute | solution.py:756
  80.1 8.9 %collective-permute-start.25 = (f32[4,4,48,384]{3,2,1,0:T(8,128)S(1)}, f32[4,4,48,384]{3,2,1,0:T(8,128)S(1)}, u32[]{:S(2)}, u32[]{:S(2)}) collective-permute-start(f32[4,4,48,384]{3,2,1,0:T(8,128)S(1)} %get-tuple-element.174), channel_id=1, source_target_pairs={{0,1},{1,0},{2,3},{3,2},{4,5},{5,4},{6,7},{7,6},{8,9},{9,8},{10,11... | collective-permute-start | bytes 3538952 | tf_op jit(solution)/shard_map/ppermute | solution.py:753
  89.9 10.5 %collective-permute-start.26 = (f32[4,4,48,384]{3,2,1,0:T(8,128)S(1)}, f32[4,4,48,384]{3,2,1,0:T(8,128)S(1)}, u32[]{:S(2)}, u32[]{:S(2)}) collective-permute-start(f32[4,4,48,384]{3,2,1,0:T(8,128)S(1)} %get-tuple-element.180), channel_id=1, source_target_pairs={{0,1},{1,0},{2,3},{3,2},{4,5},{5,4},{6,7},{7,6},{8,9},{9,8},{10,11... | collective-permute-start | bytes 3538952 | tf_op jit(solution)/shard_map/ppermute | solution.py:753
  91.2 12.0 %collective-permute-start.32 = (f32[4,48,384]{2,1,0:T(8,128)S(1)}, f32[4,48,384]{2,1,0:T(8,128)S(1)}, u32[]{:S(2)}, u32[]{:S(2)}) collective-permute-start(f32[4,48,384]{2,1,0:T(8,128)S(1)} %get-tuple-element.211), channel_id=1, source_target_pairs={{0,8},{8,0},{16,24},{24,16},{1,9},{9,1},{17,25},{25,17},{2,10},{10... | collective-permute-start | bytes 884744 | tf_op jit(solution)/shard_map/ppermute | solution.py:759
  91.7 29.1 %collective-permute-start.33 = (f32[4,48,384]{2,1,0:T(8,128)S(1)}, f32[4,48,384]{2,1,0:T(8,128)S(1)}, u32[]{:S(2)}, u32[]{:S(2)}) collective-permute-start(f32[4,48,384]{2,1,0:T(8,128)S(1)} %get-tuple-element.212), channel_id=1, source_target_pairs={{0,16},{8,24},{16,0},{24,8},{1,17},{9,25},{17,1},{25,9},{2,18},{10... | collective-permute-start | bytes 884744 | tf_op jit(solution)/shard_map/ppermute | solution.py:759
  93.2 27.7 %collective-permute-start.34 = (f32[4,48,384]{2,1,0:T(8,128)S(1)}, f32[4,48,384]{2,1,0:T(8,128)S(1)}, u32[]{:S(2)}, u32[]{:S(2)}) collective-permute-start(f32[4,48,384]{2,1,0:T(8,128)S(1)} %get-tuple-element.213), channel_id=1, source_target_pairs={{0,24},{8,16},{16,8},{24,0},{1,25},{9,17},{17,9},{25,1},{2,26},{10... | collective-permute-start | bytes 884744 | tf_op jit(solution)/shard_map/ppermute | solution.py:759
  101.3 19.6 %collective-permute-start.29 = (f32[4,48,384]{2,1,0:T(8,128)S(1)}, f32[4,48,384]{2,1,0:T(8,128)S(1)}, u32[]{:S(2)}, u32[]{:S(2)}) collective-permute-start(f32[4,48,384]{2,1,0:T(8,128)S(1)} %get-tuple-element.207), channel_id=1, source_target_pairs={{0,8},{8,0},{16,24},{24,16},{1,9},{9,1},{17,25},{25,17},{2,10},{10... | collective-permute-start | bytes 884744 | tf_op jit(solution)/shard_map/ppermute | solution.py:759
  101.8 19.1 %collective-permute-start.30 = (f32[4,48,384]{2,1,0:T(8,128)S(1)}, f32[4,48,384]{2,1,0:T(8,128)S(1)}, u32[]{:S(2)}, u32[]{:S(2)}) collective-permute-start(f32[4,48,384]{2,1,0:T(8,128)S(1)} %get-tuple-element.208), channel_id=1, source_target_pairs={{0,16},{8,24},{16,0},{24,8},{1,17},{9,25},{17,1},{25,9},{2,18},{10... | collective-permute-start | bytes 884744 | tf_op jit(solution)/shard_map/ppermute | solution.py:759
  103.9 17.0 %collective-permute-start.31 = (f32[4,48,384]{2,1,0:T(8,128)S(1)}, f32[4,48,384]{2,1,0:T(8,128)S(1)}, u32[]{:S(2)}, u32[]{:S(2)}) collective-permute-start(f32[4,48,384]{2,1,0:T(8,128)S(1)} %get-tuple-element.209), channel_id=1, source_target_pairs={{0,24},{8,16},{16,8},{24,0},{1,25},{9,17},{17,9},{25,1},{2,26},{10... | collective-permute-start | bytes 884744 | tf_op jit(solution)/shard_map/ppermute | solution.py:759
  120.9 6.4 %collective-permute-start.35 = (f32[4,4,48,384]{3,2,1,0:T(8,128)S(1)}, f32[4,4,48,384]{3,2,1,0:T(8,128)}, u32[]{:S(2)}, u32[]{:S(2)}) collective-permute-start(f32[4,4,48,384]{3,2,1,0:T(8,128)S(1)} %get-tuple-element.215), channel_id=1, source_target_pairs={{0,1},{1,0},{2,3},{3,2},{4,5},{5,4},{6,7},{7,6},{8,9},{9,8},{10,11... | collective-permute-start | bytes 3538952 | tf_op jit(solution)/shard_map/ppermute | solution.py:753
  128.9 9.9 %collective-permute-start.37 = (f32[4,48,384]{2,1,0:T(8,128)S(1)}, f32[4,48,384]{2,1,0:T(8,128)S(1)}, u32[]{:S(2)}, u32[]{:S(2)}) collective-permute-start(f32[4,48,384]{2,1,0:T(8,128)S(1)} %get-tuple-element.229), channel_id=1, source_target_pairs={{0,8},{8,0},{16,24},{24,16},{1,9},{9,1},{17,25},{25,17},{2,10},{10... | collective-permute-start | bytes 884744 | tf_op jit(solution)/shard_map/ppermute | solution.py:759
  129.5 15.2 %collective-permute-start.38 = (f32[4,48,384]{2,1,0:T(8,128)S(1)}, f32[4,48,384]{2,1,0:T(8,128)S(1)}, u32[]{:S(2)}, u32[]{:S(2)}) collective-permute-start(f32[4,48,384]{2,1,0:T(8,128)S(1)} %get-tuple-element.230), channel_id=1, source_target_pairs={{0,16},{8,24},{16,0},{24,8},{1,17},{9,25},{17,1},{25,9},{2,18},{10... | collective-permute-start | bytes 884744 | tf_op jit(solution)/shard_map/ppermute | solution.py:759
  130.0 14.7 %collective-permute-start.39 = (f32[4,48,384]{2,1,0:T(8,128)S(1)}, f32[4,48,384]{2,1,0:T(8,128)S(1)}, u32[]{:S(2)}, u32[]{:S(2)}) collective-permute-start(f32[4,48,384]{2,1,0:T(8,128)S(1)} %get-tuple-element.231), channel_id=1, source_target_pairs={{0,24},{8,16},{16,8},{24,0},{1,25},{9,17},{17,9},{25,1},{2,26},{10... | collective-permute-start | bytes 884744 | tf_op jit(solution)/shard_map/ppermute | solution.py:759
  132.7 15.4 %collective-permute-start.43 = (f32[112,384]{1,0:T(8,128)S(1)}, f32[112,384]{1,0:T(8,128)S(1)}, u32[]{:S(2)}, u32[]{:S(2)}) collective-permute-start(f32[112,384]{1,0:T(8,128)S(1)} %get-tuple-element.300), channel_id=1, source_target_pairs={{0,2},{1,3},{2,0},{3,1},{4,6},{5,7},{6,4},{7,5},{8,10},{9,11},{10,... | collective-permute-start | bytes 516104 | tf_op jit(solution)/shard_map/ppermute | solution.py:756
  134.1 15.1 %collective-permute-start.44 = (f32[112,384]{1,0:T(8,128)S(1)}, f32[112,384]{1,0:T(8,128)S(1)}, u32[]{:S(2)}, u32[]{:S(2)}) collective-permute-start(f32[112,384]{1,0:T(8,128)S(1)} %get-tuple-element.301), channel_id=1, source_target_pairs={{0,4},{1,5},{2,6},{3,7},{4,0},{5,1},{6,2},{7,3},{8,12},{9,13},{10,... | collective-permute-start | bytes 516104 | tf_op jit(solution)/shard_map/ppermute | solution.py:756
  138.8 10.4 %collective-permute-start.45 = (f32[112,384]{1,0:T(8,128)S(1)}, f32[112,384]{1,0:T(8,128)S(1)}, u32[]{:S(2)}, u32[]{:S(2)}) collective-permute-start(f32[112,384]{1,0:T(8,128)S(1)} %get-tuple-element.302), channel_id=1, source_target_pairs={{0,6},{1,7},{2,4},{3,5},{4,2},{5,3},{6,0},{7,1},{8,14},{9,15},{10,... | collective-permute-start | bytes 516104 | tf_op jit(solution)/shard_map/ppermute | solution.py:756
  144.7 4.9 %collective-permute-start.40 = (f32[48,384]{1,0:T(8,128)S(1)}, f32[48,384]{1,0:T(8,128)S(1)}, u32[]{:S(2)}, u32[]{:S(2)}) collective-permute-start(f32[48,384]{1,0:T(8,128)S(1)} %get-tuple-element.260), channel_id=1, source_target_pairs={{0,2},{1,3},{2,0},{3,1},{4,6},{5,7},{6,4},{7,5},{8,10},{9,11},{10,... | collective-permute-start | bytes 221192 | tf_op jit(solution)/shard_map/ppermute | solution.py:756
  146.1 10.7 %collective-permute-start.41 = (f32[48,384]{1,0:T(8,128)S(1)}, f32[48,384]{1,0:T(8,128)S(1)}, u32[]{:S(2)}, u32[]{:S(2)}) collective-permute-start(f32[48,384]{1,0:T(8,128)S(1)} %get-tuple-element.262), channel_id=1, source_target_pairs={{0,4},{1,5},{2,6},{3,7},{4,0},{5,1},{6,2},{7,3},{8,12},{9,13},{10,... | collective-permute-start | bytes 221192 | tf_op jit(solution)/shard_map/ppermute | solution.py:756
  148.1 8.8 %collective-permute-start.42 = (f32[48,384]{1,0:T(8,128)S(1)}, f32[48,384]{1,0:T(8,128)S(1)}, u32[]{:S(2)}, u32[]{:S(2)}) collective-permute-start(f32[48,384]{1,0:T(8,128)S(1)} %get-tuple-element.261), channel_id=1, source_target_pairs={{0,6},{1,7},{2,4},{3,5},{4,2},{5,3},{6,0},{7,1},{8,14},{9,15},{10,... | collective-permute-start | bytes 221192 | tf_op jit(solution)/shard_map/ppermute | solution.py:756
  156.9 4.5 %collective-permute-start.49 = (f32[48,384]{1,0:T(8,128)S(1)}, f32[48,384]{1,0:T(8,128)S(1)}, u32[]{:S(2)}, u32[]{:S(2)}) collective-permute-start(f32[48,384]{1,0:T(8,128)S(1)} %get-tuple-element.296), channel_id=1, source_target_pairs={{0,8},{8,0},{16,24},{24,16},{1,9},{9,1},{17,25},{25,17},{2,10},{10... | collective-permute-start | bytes 221192 | tf_op jit(solution)/shard_map/ppermute | solution.py:759
  158.1 5.3 %collective-permute-start.51 = (f32[48,384]{1,0:T(8,128)S(1)}, f32[48,384]{1,0:T(8,128)S(1)}, u32[]{:S(2)}, u32[]{:S(2)}) collective-permute-start(f32[48,384]{1,0:T(8,128)S(1)} %get-tuple-element.258), channel_id=1, source_target_pairs={{0,24},{8,16},{16,8},{24,0},{1,25},{9,17},{17,9},{25,1},{2,26},{10... | collective-permute-start | bytes 221192 | tf_op jit(solution)/shard_map/ppermute | solution.py:759
  167.9 6.4 %collective-permute-start.54 = (f32[96,128]{1,0:T(8,128)S(1)}, f32[96,128]{1,0:T(8,128)S(1)}, u32[]{:S(2)}, u32[]{:S(2)}) collective-permute-start(f32[96,128]{1,0:T(8,128)S(1)} %get-tuple-element.297), channel_id=1, source_target_pairs={{0,4},{1,5},{2,6},{3,7},{4,0},{5,1},{6,2},{7,3},{8,12},{9,13},{10,... | collective-permute-start | bytes 147464 | tf_op jit(solution)/shard_map/ppermute | solution.py:756
  169.6 6.0 %collective-permute-start.55 = (f32[96,128]{1,0:T(8,128)S(1)}, f32[96,128]{1,0:T(8,128)S(1)}, u32[]{:S(2)}, u32[]{:S(2)}) collective-permute-start(f32[96,128]{1,0:T(8,128)S(1)} %get-tuple-element.298), channel_id=1, source_target_pairs={{0,6},{1,7},{2,4},{3,5},{4,2},{5,3},{6,0},{7,1},{8,14},{9,15},{10,... | collective-permute-start | bytes 147464 | tf_op jit(solution)/shard_map/ppermute | solution.py:756
  175.5 7.6 %collective-permute-start.56 = (f32[96,128]{1,0:T(8,128)S(1)}, f32[96,128]{1,0:T(8,128)S(1)}, u32[]{:S(2)}, u32[]{:S(2)}) collective-permute-start(f32[96,128]{1,0:T(8,128)S(1)} %fusion.26), channel_id=1, source_target_pairs={{0,2},{1,3},{2,0},{3,1},{4,6},{5,7},{6,4},{7,5},{8,10},{9,11},{10,... | collective-permute-start | bytes 147464 | tf_op jit(solution)/shard_map/ppermute | solution.py:756
  175.7 7.9 %collective-permute-start.57 = (f32[96,128]{1,0:T(8,128)S(1)}, f32[96,128]{1,0:T(8,128)S(1)}, u32[]{:S(2)}, u32[]{:S(2)}) collective-permute-start(f32[96,128]{1,0:T(8,128)S(1)} %fusion.26), channel_id=1, source_target_pairs={{0,4},{1,5},{2,6},{3,7},{4,0},{5,1},{6,2},{7,3},{8,12},{9,13},{10,... | collective-permute-start | bytes 147464 | tf_op jit(solution)/shard_map/ppermute | solution.py:756
  178.0 5.9 %collective-permute-start.58 = (f32[96,128]{1,0:T(8,128)S(1)}, f32[96,128]{1,0:T(8,128)S(1)}, u32[]{:S(2)}, u32[]{:S(2)}) collective-permute-start(f32[96,128]{1,0:T(8,128)S(1)} %fusion.26), channel_id=1, source_target_pairs={{0,6},{1,7},{2,4},{3,5},{4,2},{5,3},{6,0},{7,1},{8,14},{9,15},{10,... | collective-permute-start | bytes 147464 | tf_op jit(solution)/shard_map/ppermute | solution.py:756
  180.0 20.8 %collective-permute-start.46 = (f32[160,384]{1,0:T(8,128)S(1)}, f32[160,384]{1,0:T(8,128)S(1)}, u32[]{:S(2)}, u32[]{:S(2)}) collective-permute-start(f32[160,384]{1,0:T(8,128)S(1)} %pad_maximum_fusion.7.refs_0_), channel_id=1, source_target_pairs={{0,8},{8,0},{16,24},{24,16},{1,9},{9,1},{17,25},{25,17},{2,10},{10... | collective-permute-start | bytes 737288 | tf_op jit(solution)/shard_map/ppermute | solution.py:759
  181.6 19.2 %collective-permute-start.47 = (f32[160,384]{1,0:T(8,128)S(1)}, f32[160,384]{1,0:T(8,128)S(1)}, u32[]{:S(2)}, u32[]{:S(2)}) collective-permute-start(f32[160,384]{1,0:T(8,128)S(1)} %pad_maximum_fusion.7.refs_0_), channel_id=1, source_target_pairs={{0,16},{8,24},{16,0},{24,8},{1,17},{9,25},{17,1},{25,9},{2,18},{10... | collective-permute-start | bytes 737288 | tf_op jit(solution)/shard_map/ppermute | solution.py:759
  183.1 17.7 %collective-permute-start.48 = (f32[160,384]{1,0:T(8,128)S(1)}, f32[160,384]{1,0:T(8,128)S(1)}, u32[]{:S(2)}, u32[]{:S(2)}) collective-permute-start(f32[160,384]{1,0:T(8,128)S(1)} %pad_maximum_fusion.7.refs_0_), channel_id=1, source_target_pairs={{0,24},{8,16},{16,8},{24,0},{1,25},{9,17},{17,9},{25,1},{2,26},{10... | collective-permute-start | bytes 737288 | tf_op jit(solution)/shard_map/ppermute | solution.py:759
  200.8 9.9 %collective-permute-start.60 = (f32[192,384]{1,0:T(8,128)S(1)}, f32[192,384]{1,0:T(8,128)S(1)}, u32[]{:S(2)}, u32[]{:S(2)}) collective-permute-start(f32[192,384]{1,0:T(8,128)S(1)} %shard_map.271.one), channel_id=1, source_target_pairs={{0,8},{8,0},{16,24},{24,16},{1,9},{9,1},{17,25},{25,17},{2,10},{10... | collective-permute-start | bytes 884744 | tf_op jit(solution)/shard_map/ppermute | solution.py:759
  202.4 15.1 %collective-permute-start.61 = (f32[192,384]{1,0:T(8,128)S(1)}, f32[192,384]{1,0:T(8,128)S(1)}, u32[]{:S(2)}, u32[]{:S(2)}) collective-permute-start(f32[192,384]{1,0:T(8,128)S(1)} %shard_map.271.one), channel_id=1, source_target_pairs={{0,16},{8,24},{16,0},{24,8},{1,17},{9,25},{17,1},{25,9},{2,18},{10... | collective-permute-start | bytes 884744 | tf_op jit(solution)/shard_map/ppermute | solution.py:759
  203.9 13.6 %collective-permute-start.62 = (f32[192,384]{1,0:T(8,128)S(1)}, f32[192,384]{1,0:T(8,128)S(1)}, u32[]{:S(2)}, u32[]{:S(2)}) collective-permute-start(f32[192,384]{1,0:T(8,128)S(1)} %shard_map.271.one), channel_id=1, source_target_pairs={{0,24},{8,16},{16,8},{24,0},{1,25},{9,17},{17,9},{25,1},{2,26},{10... | collective-permute-start | bytes 884744 | tf_op jit(solution)/shard_map/ppermute | solution.py:759
  (46 other events, 271.3 us)
